TPU v7x, 32 devices: a whole 2x2x4 slice. The times are simulated.
32 devices in a mesh: groups: 1, expert: 8 (over z, y), dp: 4 (over x, core).
Axes of the slice: x: 2, y: 2, z: 4, core: 2. Of those that a mesh axis runs over, the one named last changes fastest.
Arguments:
- queries: bfloat16 [2048, 4096], P(('groups', 'dp'), 'expert'), may hold values from -6 to 6
- keys_in: bfloat16 [2048, 4096], P(('groups', 'dp'), 'expert'), may hold values from -6 to 6
- values_in: bfloat16 [2048, 4096], P(('groups', 'dp'), 'expert'), may hold values from -6 to 6
- gate_in: bfloat16 [2048, 4096], P(('groups', 'dp'), 'expert'), may hold values from -6 to 6
- beta: float32 [2048, 32], P(('groups', 'dp'), 'expert'), may hold values from 0.1 to 1
- decay: float32 [2048, 32], P(('groups', 'dp'), 'expert'), may hold values from -1 to 0
- lengths: int32 [4, 4], P(('groups', 'dp')), may hold values from 1 to 256, 512 in all within a row
- cache: float32 [16, 32, 128, 128], P(('groups', 'dp'), 'expert'), may hold values from -6 to 6
- norm_gain: float32 [128], replicated, may hold values from 0.1 to 1.9
- out_proj: bfloat16 [4096, 2048], P('expert'), may hold values from -0.09375 to 0.09375
- residual: bfloat16 [2048, 2048], P(('groups', 'dp', 'expert')), may hold values from -6 to 6
- post_gain: float32 [2048], replicated, may hold values from 0.1 to 1.9
- expert_ids: int32 [2048, 10], P(('groups', 'dp', 'expert')), may hold values from 0 to 31, all different within a row; in each aligned block of 64 rows (0 to 63, 64 to 127, ...) at most 25 rows name the same one
- route_weights: float32 [2048, 10], P(('groups', 'dp', 'expert')), may hold values from 0.05 to 1
- gate_up: bfloat16 [32, 2048, 512], P(('expert', 'dp')), may hold values from -0.125 to 0.125
- down_proj: bfloat16 [32, 256, 2048], P(('expert', 'dp')), may hold values from -0.375 to 0.375
Outputs:
- moe_out: bfloat16 [2048, 2048], P(('groups', 'dp', 'expert'))
- attn_out: bfloat16 [2048, 2048], P(('groups', 'dp', 'expert'))
- new_states: float32 [16, 32, 128, 128], P(('groups', 'dp'), 'expert')
Inputs may be any that keep to these rules, and one draw needn't show every extreme that they name: Each row of lengths fills its shard's 512 rows; the longest span of each row is exactly 256. `expert_ids`: each row names 10 different experts. Within the 64 rows of one device no expert is named more than 25 times, a bound that some block reaches; every expert is named somewhere.
All inputs are finite; a program needn't handle non-finite values.
Results may differ from a plain program's by a relative error of at most 0.025.
Values may be sent and summed in bfloat16 or wider, within the bound.
No kernel may reach another device: no remote copies, remote signals or barrier semaphores. Data moves between devices by JAX's collectives and lax.ppermute only.
A program may use at most 64 MiB of HBM per device.

v0:
```python
import jax
import jax.numpy as jnp
from jax import lax
from jax.sharding import PartitionSpec as P

HIGH = lax.Precision.HIGHEST
epsilon = 1e-06
block_rows = 64


def unit_rows(values):
    return values * lax.rsqrt(jnp.sum(values * values, axis=-1, keepdims=True) + epsilon)


def block_step(states, item):
    query_b, key_b, value_b, beta_b, decay_b, member_b = item
    size = query_b.shape[0]
    places = jnp.arange(size)
    shared = jnp.dot(member_b, member_b.T, precision=HIGH) > 0.5
    inside = shared & (places[:, None] >= places[None, :])
    strict_part = inside & (places[:, None] > places[None, :])
    running = jnp.dot(inside.astype(jnp.float32), decay_b, precision=HIGH).T
    log_gaps = running[:, :, None] - running[:, None, :]
    decays = jnp.where(inside[None], jnp.exp(jnp.minimum(log_gaps, 0.0)), 0.0)
    key_h = jnp.swapaxes(key_b, 0, 1)
    query_h = jnp.swapaxes(query_b, 0, 1)
    value_h = jnp.swapaxes(value_b, 0, 1)
    beta_h = beta_b.T
    key_dots = jnp.einsum("hik,hjk->hij", key_h, key_h, precision=HIGH)
    strict_terms = jnp.where(strict_part[None], decays * key_dots * beta_h[:, :, None], 0.0)
    identity = jnp.eye(size, dtype=jnp.float32)[None]
    inverse = identity - strict_terms
    powered = strict_terms
    covered = 2
    while covered < size:
        powered = jnp.einsum("hij,hjk->hik", powered, powered, precision=HIGH)
        inverse = jnp.einsum("hij,hjk->hik", inverse, identity + powered, precision=HIGH)
        covered = covered * 2
    growth = jnp.exp(running)
    targets = jnp.concatenate(
        [key_h * (beta_h * growth)[:, :, None], value_h * beta_h[:, :, None]], axis=2
    )
    solved = jnp.einsum("hij,hjc->hic", inverse, targets, precision=HIGH)
    width = key_h.shape[2]
    key_mix = solved[:, :, :width]
    value_mix = solved[:, :, width:]
    recalled = jnp.einsum("hck,hrkv->hrcv", key_mix, states, precision=HIGH)
    recalled = jnp.einsum("cr,hrcv->hcv", member_b, recalled, precision=HIGH)
    updates = value_mix - recalled
    from_state = jnp.einsum("hck,hrkv->hrcv", query_h, states, precision=HIGH)
    from_state = jnp.einsum("cr,hrcv->hcv", member_b, from_state, precision=HIGH)
    query_dots = jnp.einsum("hik,hjk->hij", query_h, key_h, precision=HIGH)
    mixed = growth[:, :, None] * from_state + jnp.einsum(
        "hij,hjv->hiv", query_dots * decays, updates, precision=HIGH
    )
    span_total = jnp.einsum("cr,ch->hr", member_b, decay_b, precision=HIGH)
    end_gaps = span_total[:, :, None] - running[:, None, :]
    carried = jnp.where(member_b.T[None] > 0.5, jnp.exp(jnp.minimum(end_gaps, 0.0)), 0.0)
    fresh = jnp.einsum("hrc,hck,hcv->hrkv", carried, key_h, updates, precision=HIGH)
    states = jnp.exp(span_total)[:, :, None, None] * states + fresh
    return (states, jnp.swapaxes(mixed, 0, 1))


def on_device(
    queries,
    keys_in,
    values_in,
    gate_in,
    beta,
    decay,
    lengths,
    cache,
    norm_gain,
    out_proj,
    residual,
    post_gain,
    expert_ids,
    route_weights,
    gate_up,
    down_proj,
):
    tok_count = queries.shape[0]
    heads = beta.shape[1]
    head_dim = norm_gain.shape[0]
    requests = lengths.shape[1]
    block = min(block_rows, tok_count)
    blocks = tok_count // block
    layout = (blocks, block, heads, head_dim)
    query_n = unit_rows(queries.astype(jnp.float32).reshape(layout)) * head_dim ** (-0.5)
    key_n = unit_rows(keys_in.astype(jnp.float32).reshape(layout))
    value_f = values_in.astype(jnp.float32).reshape(layout)
    ends = jnp.cumsum(lengths[0])
    places = jnp.arange(tok_count, dtype=jnp.int32)
    request = jnp.sum((places[:, None] >= ends[None, :]).astype(jnp.int32), axis=1)
    member = (request[:, None] == jnp.arange(requests, dtype=jnp.int32)[None, :]).astype(
        jnp.float32
    )
    inputs = (
        query_n,
        key_n,
        value_f,
        beta.reshape(blocks, block, heads),
        decay.reshape(blocks, block, heads),
        member.reshape(blocks, block, requests),
    )
    states, mixed = lax.scan(block_step, jnp.swapaxes(cache, 0, 1), inputs)
    new_states = jnp.swapaxes(states, 0, 1)
    mixed = mixed.reshape(tok_count, heads, head_dim)
    gate_f = gate_in.astype(jnp.float32).reshape(tok_count, heads, head_dim)
    scale = lax.rsqrt(jnp.mean(mixed * mixed, axis=-1, keepdims=True) + epsilon)
    normed = (
        (mixed * scale * norm_gain * jax.nn.silu(gate_f))
        .astype(jnp.bfloat16)
        .reshape(tok_count, heads * head_dim)
    )
    tok_local = residual.shape[0]
    attn = lax.psum_scatter(
        jnp.dot(normed, out_proj, preferred_element_type=jnp.float32).astype(jnp.bfloat16),
        "expert",
        scatter_dimension=0,
        tiled=True,
    ).astype(jnp.float32)
    attn_out = (residual.astype(jnp.float32) + attn).astype(jnp.bfloat16)
    stream = attn_out.astype(jnp.float32)
    routed = (
        stream * lax.rsqrt(jnp.mean(stream * stream, axis=-1, keepdims=True) + epsilon) * post_gain
    ).astype(jnp.bfloat16)
    expert_axis = lax.axis_size("expert")
    data_axis = lax.axis_size("dp")
    experts_all = expert_axis * data_axis
    top = expert_ids.shape[1]
    capacity = min(tok_local, max(2, 5 * tok_local * top // (4 * experts_all)))
    slots = experts_all * capacity
    width = routed.shape[1]
    flat_ids = expert_ids.reshape(-1)
    chosen = (flat_ids[:, None] == jnp.arange(experts_all, dtype=jnp.int32)[None, :]).astype(
        jnp.int32
    )
    rank = jnp.sum(chosen * (jnp.cumsum(chosen, axis=0) - 1), axis=1)
    slot_of = flat_ids * capacity + rank
    picks = (slot_of[None, :] == jnp.arange(slots, dtype=jnp.int32)[:, None]).reshape(
        slots, tok_local, top
    )
    picks = jnp.any(picks, axis=2).astype(jnp.bfloat16)
    outgoing = jnp.dot(picks, routed, preferred_element_type=jnp.float32).astype(jnp.bfloat16)
    outgoing = outgoing.reshape(expert_axis, data_axis, capacity, width)
    arrived = lax.all_to_all(
        lax.all_to_all(outgoing, "expert", split_axis=0, concat_axis=0, tiled=True),
        "dp",
        split_axis=1,
        concat_axis=1,
        tiled=True,
    )
    shape = arrived.shape
    flat = arrived.reshape(-1, shape[-1])
    both = jnp.dot(flat, gate_up[0], preferred_element_type=jnp.float32)
    hidden_width = down_proj.shape[1]
    hidden = (jax.nn.silu(both[:, :hidden_width]) * both[:, hidden_width:]).astype(jnp.bfloat16)
    result = jnp.dot(hidden, down_proj[0], preferred_element_type=jnp.float32).astype(jnp.bfloat16)
    returned = lax.all_to_all(
        lax.all_to_all(result.reshape(shape), "expert", split_axis=0, concat_axis=0, tiled=True),
        "dp",
        split_axis=1,
        concat_axis=1,
        tiled=True,
    )
    gathered = jnp.take(returned.reshape(slots, width), slot_of, axis=0).reshape(
        tok_local, top, width
    )
    moe_out = jnp.sum(gathered.astype(jnp.float32) * route_weights[:, :, None], axis=1).astype(
        jnp.bfloat16
    )
    return (moe_out, attn_out, new_states)


def solution(mesh):
    return jax.shard_map(
        on_device,
        mesh=mesh,
        in_specs=(
            P(("groups", "dp"), "expert"),
            P(("groups", "dp"), "expert"),
            P(("groups", "dp"), "expert"),
            P(("groups", "dp"), "expert"),
            P(("groups", "dp"), "expert"),
            P(("groups", "dp"), "expert"),
            P(("groups", "dp"), None),
            P(("groups", "dp"), "expert", None, None),
            P(),
            P("expert", None),
            P(("groups", "dp", "expert"), None),
            P(),
            P(("groups", "dp", "expert"), None),
            P(("groups", "dp", "expert"), None),
            P(("expert", "dp"), None, None),
            P(("expert", "dp"), None, None),
        ),
        out_specs=(
            P(("groups", "dp", "expert"), None),
            P(("groups", "dp", "expert"), None),
            P(("groups", "dp"), "expert", None, None),
        ),
        check_vma=False,
    )
```

profile of v0, /device:TPU:0, one launch (start us, length us, event | category | flops | bytes accessed | tf_op | source)
XLA Modules:
  0.0 527.9 jit_solution(2639585679003318834)
XLA Ops:
  9.9 1.4 reshape.246
  12.2 1.5 multiply_multiply_fusion
  13.7 1.4 reshape.242
  16.1 1.6 broadcast_multiply_fusion.1
  17.7 2.4 reshape.244
  21.4 111.9 %while.12 = (s32[]{:T(128)}, f32[4,4,128,128]{3,2,1,0:T(8,128)S(1)}, f32[8,64,4,128]{3,1,2,0:T(8,128)}, f32[8,64,4]{1,0,2:T(8,128)S(1)}, f32[8,64,4]{1,2,0:T(4,1...) while((s32[]{:T(128)}, ...), condition=%wide.region_9.10_spmd, body=%wide.region_8.9_spmd.sunk | while | flops 860401152 | bytes 12359501 | solution.py:106
  30.8 1.3 fusion.226
  33.1 2.3 fusion.225
  42.7 1.3 fusion.224
  44.8 1.3 fusion.226
  47.0 2.3 fusion.225
  56.7 1.3 fusion.224
  61.0 2.3 fusion.225
  75.0 2.3 fusion.225
  84.6 1.3 fusion.224
  86.7 1.3 fusion.226
  88.9 2.3 fusion.225
  102.9 2.3 fusion.225
  116.9 2.3 fusion.225
  126.5 1.3 fusion.224
  128.6 1.3 fusion.226
  130.9 2.3 fusion.225
  133.3 1.6 multiply_reduce_fusion.1
  134.9 2.9 copy.143
  138.6 4.1 convolution_convert_fusion.2
  143.1 1.5 reduce-window.18
  145.6 68.8 %reduce-scatter.2.cloned.1.call-done = bf16[64,2048]{1,0:T(8,128)(2,1)} async-done(((bf16[512,2048]{1,0:T(8,128)(2,1)}), bf16[64,2048]{1,0:T(8,128)(2,1)}) %reduce-scatter.2.cloned.1.call-update) | async-done | bytes 262160 | tf_op jit(solution)/shard_map/reduce_scatter | solution.py:117
  215.6 2.8 convolution_convert_fusion.1
  218.4 4.9 reshape.237
  223.3 4.8 copy.146
  228.2 75.7 %all_to_all.20 = bf16[8,4,25,2048]{3,1,2,0:T(4,128)(2,1)S(1)} all-to-all(bf16[8,4,25,2048]{3,1,2,0:T(4,128)(2,1)S(1)} %copy.146), channel_id=1, replica_groups=mesh['groups'=1,'expert'=8,'dp'=4] {'expert'}, dimensions={0} | all-to-all | bytes 6553600 | tf_op jit(solution)/shard_map/all_to_all | solution.py:148
  303.9 1.8 copy.147
  305.7 41.1 %all_to_all.21 = bf16[8,4,25,2048]{3,0,2,1:T(8,128)(2,1)S(1)} all-to-all(bf16[8,4,25,2048]{3,0,2,1:T(8,128)(2,1)S(1)} %copy.147), channel_id=1, replica_groups=mesh['groups'=1,'expert'=8,'dp'=4] {'dp'}, dimensions={1} | all-to-all | bytes 6553600 | tf_op jit(solution)/shard_map/all_to_all | solution.py:147
  346.7 3.8 copy.148
  350.6 5.1 reshape.238
  355.6 3.9 fusion.46
  359.5 2.8 convolution_convert_fusion
  362.3 4.9 reshape.239
  367.2 4.8 copy.149
  372.0 76.5 %all_to_all.22 = bf16[8,4,25,2048]{3,1,2,0:T(4,128)(2,1)S(1)} all-to-all(bf16[8,4,25,2048]{3,1,2,0:T(4,128)(2,1)S(1)} %copy.149), channel_id=1, replica_groups=mesh['groups'=1,'expert'=8,'dp'=4] {'expert'}, dimensions={0} | all-to-all | bytes 6553600 | tf_op jit(solution)/shard_map/all_to_all | solution.py:161
  448.5 3.5 copy.150
  452.0 5.1 all-to-all-start.3
  458.4 37.0 %all-to-all-done.3 = bf16[8,4,25,2048]{3,0,2,1:T(8,128)(2,1)} async-done(((bf16[8,4,25,2048]{3,0,2,1:T(8,128)(2,1)}), bf16[8,4,25,2048]{3,0,2,1:T(8,128)(2,1)}, u32[]{:S(2)}, u32[]{:S(2)}) %all-to-all-start.3) | async-done | bytes 3276832 | tf_op jit(solution)/shard_map/all_to_all | solution.py:160
  495.4 5.8 %copy.151 = bf16[8,4,25,2048]{3,2,1,0:T(8,128)(2,1)} copy(bf16[8,4,25,2048]{3,0,2,1:T(8,128)(2,1)} %all-to-all-done.3) | data formatting | bytes 6553600 | tf_op jit(solution)/shard_map/all_to_all | solution.py:160
  501.2 3.4 reshape.240
  504.6 4.1 gather_fusion
  508.7 5.5 %gather.7 = bf16[64,10,2048]{2,1,0:T(8,128)(2,1)} reshape(bf16[640,2048]{1,0:T(8,128)(2,1)} %gather_fusion) | data formatting | bytes 5242880 | tf_op jit(solution)/shard_map/jit(_take)/gather | solution.py:167
  514.2 6.4 %multiply_reduce_fusion = bf16[64,2048]{1,0:T(8,128)(2,1)} fusion(f32[64,10]{1,0:T(8,128)S(1)} %copy.152, bf16[64,10,2048]{2,1,0:T(8,128)(2,1)} %gather.7, pred[64,10]{1,0:T(8,128)(4,1)S(1)} %get-tuple-element.125), kind=kLoop, calls=%fused_computation.74 | loop fusion | flops 5111808 | bytes 2886784 | tf_op jit(solution)/shard_map/reduce_sum | solution.py:170
  (315 shorter events, 91.6 us)
Async XLA Ops:
  7.2 131.4 %copy-start = (bf16[512,2048]{1,0:T(8,128)(2,1)S(1)}, bf16[512,2048]{1,0:T(8,128)(2,1)}, u32[]{:S(2)}) copy-start(bf16[512,2048]{1,0:T(8,128)(2,1)} %param.27) | copy-start | bytes 6291460
  7.2 207.2 %reduce-scatter.2.cloned.1.call-start = ((), (), s32[]{:S(2)}) async-start(), calls=%async_computation.5 | async-start | bytes 2359296 | tf_op jit(solution)/shard_map/reduce_scatter | solution.py:117
  21.4 116.4 %copy-start.6 = (f32[128]{0:T(128)S(1)}, f32[128]{0:T(128)}, u32[]{:S(2)}) copy-start(f32[128]{0:T(128)} %param.26) | copy-start | bytes 1540
  138.6 4.2 copy-start.4
  142.7 72.9 %copy-start.3 = (f32[2048]{0:T(1024)S(1)}, f32[2048]{0:T(1024)}, u32[]{:S(2)}) copy-start(f32[2048]{0:T(1024)} %param.29) | copy-start | bytes 24580
  215.6 7.7 %copy-start.2 = (bf16[64,2048]{1,0:T(8,128)(2,1)}, bf16[64,2048]{1,0:T(8,128)(2,1)S(1)}, u32[]{:S(2)}) copy-start(bf16[64,2048]{1,0:T(8,128)(2,1)S(1)} %get-tuple-element.128) | copy-start | bytes 786436
  350.6 5.1 copy-start.7
  355.6 3.9 copy-start.8
  452.0 5.2 copy-start.5
  452.0 43.4 %all-to-all-start.3 = ((bf16[8,4,25,2048]{3,0,2,1:T(8,128)(2,1)}), bf16[8,4,25,2048]{3,0,2,1:T(8,128)(2,1)}, u32[]{:S(2)}, u32[]{:S(2)}) async-start(bf16[8,4,25,2048]{3,0,2,1:T(8,128)(2,1)} %copy.150), calls=%async_computation.4 | async-start | bytes 6553600 | tf_op jit(solution)/shard_map/all_to_all | solution.py:160
  508.7 12.0 %copy-start.1 = (bf16[512,2048]{1,0:T(8,128)(2,1)S(1)}, bf16[512,2048]{1,0:T(8,128)(2,1)}, u32[]{:S(2)}) copy-start(bf16[512,2048]{1,0:T(8,128)(2,1)} %param.27) | copy-start | bytes 6291460
Sparse Core Ops, SparseCore 0:
  142.8 71.4 reduce-scatter.1
where the time goes:
time: 539 us; the launch traced here: 528 us
  blocking collectives  193 us (36%)
  waiting for transfers between devices  106 us (20%)
  matrix products  105 us (19%)
  local copies, waits for them, and re-layouts  83.1 us (15%)
  other arithmetic  19.3 us (4%)
  between operations  14.8 us (3%)
    all_to_all x1, blocking collectives, on_device(): lax.all_to_all(result.reshape(shape), 'expert', split_axis=0, concat_axis...  76.5 us
    all_to_all x1, blocking collectives, on_device(): lax.all_to_all(outgoing, 'expert', split_axis=0, concat_axis=0, tiled=True)  75.7 us
    reduce_scatter x1, waiting for transfers between devices, on_device(): lax.psum_scatter(jnp.dot(normed, out_proj, preferred_element_type=jnp.flo...  68.8 us
    all_to_all x1, blocking collectives, on_device(): lax.all_to_all(lax.all_to_all(outgoing, 'expert', split_axis=0, concat_ax...  41.1 us
    all_to_all x1, waiting for transfers between devices, on_device(): lax.all_to_all(lax.all_to_all(result.reshape(shape), 'expert', split_axis...  37 us
    dot_general x8, matrix products, block_step(): jnp.einsum('hrc,hck,hcv->hrkv', carried, key_h, updates, precision=HIGH)  18.2 us
    dynamic_slice x32, local copies, waits for them, and re-layouts, on_device(): states, mixed = lax.scan(block_step, jnp.swapaxes(cache, 0, 1), inputs)  15.5 us
  transfers between devices with their start and end apart: 2, of which 2 were waited for; matrix products, arithmetic and copies ran while one was open for 1% of the time, Pallas kernels for 0%

commit v1 on v0

--- a/solution.py
+++ b/solution.py
@@ -59,6 +59,68 @@
     fresh = jnp.einsum("hrc,hck,hcv->hrkv", carried, key_h, updates, precision=HIGH)
     states = jnp.exp(span_total)[:, :, None, None] * states + fresh
     return (states, jnp.swapaxes(mixed, 0, 1))
+
+
+def factors(size):
+    low = 2 if size % 2 == 0 else 1
+    return size // low, low
+
+
+def partner(size, step, place):
+    return place ^ step if size & (size - 1) == 0 else (place + step) % size
+
+
+def source(size, step, place):
+    return place ^ step if size & (size - 1) == 0 else (place - step) % size
+
+
+def high_pairs(high, low, step):
+    return [
+        (h * low + m, partner(high, step, h) * low + m) for h in range(high) for m in range(low)
+    ]
+
+
+def low_pairs(high, low):
+    return [(h * low + m, h * low + (m ^ 1)) for h in range(high) for m in range(low)]
+
+
+def reverse(pairs):
+    return [(target, origin) for origin, target in pairs]
+
+
+def gather_parts(block, axis):
+    high, low = factors(lax.axis_size(axis))
+    parts = [[block]]
+    for step in range(1, high):
+        parts.append([lax.ppermute(block, axis, high_pairs(high, low, step))])
+    if low == 2:
+        for row in parts:
+            row.append(lax.ppermute(row[0], axis, low_pairs(high, low)))
+    return parts
+
+
+def scatter_sum(parts, axis):
+    high, low = factors(lax.axis_size(axis))
+    sums = []
+    for row in parts:
+        total = row[0].astype(jnp.float32)
+        if low == 2:
+            total = total + lax.ppermute(row[1], axis, low_pairs(high, low)).astype(jnp.float32)
+        sums.append(total)
+    result = sums[0]
+    for step in range(1, high):
+        sent = sums[step].astype(jnp.bfloat16)
+        result = result + lax.ppermute(
+            sent, axis, reverse(high_pairs(high, low, step))
+        ).astype(jnp.float32)
+    return result
+
+
+def part_sources(axis):
+    high, low = factors(lax.axis_size(axis))
+    place = lax.axis_index(axis)
+    h, m = place // low, place % low
+    return [[source(high, step, h) * low + (m ^ j) for j in range(low)] for step in range(high)]
 
 
 def on_device(
@@ -113,63 +175,59 @@
         .astype(jnp.bfloat16)
         .reshape(tok_count, heads * head_dim)
     )
+    width = residual.shape[1]
     tok_local = residual.shape[0]
-    attn = lax.psum_scatter(
-        jnp.dot(normed, out_proj, preferred_element_type=jnp.float32).astype(jnp.bfloat16),
+    experts_all = lax.axis_size("expert") * lax.axis_size("dp")
+    gate_up_parts = sum(gather_parts(gate_up[0], "dp"), [])
+    down_parts = sum(gather_parts(down_proj[0], "dp"), [])
+    expert_of = sum(part_sources("dp"), [])
+    expert_of = [lax.axis_index("expert") * lax.axis_size("dp") + place for place in expert_of]
+    share = jnp.dot(normed, out_proj, preferred_element_type=jnp.float32).astype(jnp.bfloat16)
+    share = share.reshape(lax.axis_size("expert"), tok_local, width)
+    attn = scatter_sum(
+        [
+            [lax.dynamic_index_in_dim(share, place, 0, keepdims=False) for place in row]
+            for row in part_sources("expert")
+        ],
         "expert",
-        scatter_dimension=0,
-        tiled=True,
-    ).astype(jnp.float32)
+    )
     attn_out = (residual.astype(jnp.float32) + attn).astype(jnp.bfloat16)
     stream = attn_out.astype(jnp.float32)
     routed = (
         stream * lax.rsqrt(jnp.mean(stream * stream, axis=-1, keepdims=True) + epsilon) * post_gain
     ).astype(jnp.bfloat16)
-    expert_axis = lax.axis_size("expert")
-    data_axis = lax.axis_size("dp")
-    experts_all = expert_axis * data_axis
-    top = expert_ids.shape[1]
-    capacity = min(tok_local, max(2, 5 * tok_local * top // (4 * experts_all)))
-    slots = experts_all * capacity
-    width = routed.shape[1]
-    flat_ids = expert_ids.reshape(-1)
-    chosen = (flat_ids[:, None] == jnp.arange(experts_all, dtype=jnp.int32)[None, :]).astype(
-        jnp.int32
-    )
-    rank = jnp.sum(chosen * (jnp.cumsum(chosen, axis=0) - 1), axis=1)
-    slot_of = flat_ids * capacity + rank
-    picks = (slot_of[None, :] == jnp.arange(slots, dtype=jnp.int32)[:, None]).reshape(
-        slots, tok_local, top
-    )
-    picks = jnp.any(picks, axis=2).astype(jnp.bfloat16)
-    outgoing = jnp.dot(picks, routed, preferred_element_type=jnp.float32).astype(jnp.bfloat16)
-    outgoing = outgoing.reshape(expert_axis, data_axis, capacity, width)
-    arrived = lax.all_to_all(
-        lax.all_to_all(outgoing, "expert", split_axis=0, concat_axis=0, tiled=True),
-        "dp",
-        split_axis=1,
-        concat_axis=1,
-        tiled=True,
-    )
-    shape = arrived.shape
-    flat = arrived.reshape(-1, shape[-1])
-    both = jnp.dot(flat, gate_up[0], preferred_element_type=jnp.float32)
+    expert_range = jnp.arange(experts_all, dtype=jnp.int32)
+    mixing = jnp.sum(
+        jnp.where(expert_ids[:, :, None] == expert_range, route_weights[:, :, None], 0.0), axis=1
+    )
+    coarse = mixing.astype(jnp.bfloat16)
+    fine = (mixing - coarse.astype(jnp.float32)).astype(jnp.bfloat16)
+    gathered = gather_parts(jnp.concatenate([routed, coarse, fine], axis=1), "expert")
+    rows = jnp.concatenate(sum(gathered, []), axis=0)
+    weights = rows[:, width : width + experts_all].astype(jnp.float32) + rows[
+        :, width + experts_all :
+    ].astype(jnp.float32)
+    rows = rows[:, :width]
     hidden_width = down_proj.shape[1]
-    hidden = (jax.nn.silu(both[:, :hidden_width]) * both[:, hidden_width:]).astype(jnp.bfloat16)
-    result = jnp.dot(hidden, down_proj[0], preferred_element_type=jnp.float32).astype(jnp.bfloat16)
-    returned = lax.all_to_all(
-        lax.all_to_all(result.reshape(shape), "expert", split_axis=0, concat_axis=0, tiled=True),
-        "dp",
-        split_axis=1,
-        concat_axis=1,
-        tiled=True,
-    )
-    gathered = jnp.take(returned.reshape(slots, width), slot_of, axis=0).reshape(
-        tok_local, top, width
-    )
-    moe_out = jnp.sum(gathered.astype(jnp.float32) * route_weights[:, :, None], axis=1).astype(
-        jnp.bfloat16
-    )
+    hidden = []
+    for place, matrix in zip(expert_of, gate_up_parts):
+        weight = jnp.sum(jnp.where(expert_range == place, weights, 0.0), axis=1, keepdims=True)
+        both = jnp.dot(rows, matrix, preferred_element_type=jnp.float32)
+        hidden.append(
+            (weight * jax.nn.silu(both[:, :hidden_width]) * both[:, hidden_width:]).astype(
+                jnp.bfloat16
+            )
+        )
+    result = jnp.dot(
+        jnp.concatenate(hidden, axis=1),
+        jnp.concatenate(down_parts, axis=0),
+        preferred_element_type=jnp.float32,
+    ).astype(jnp.bfloat16)
+    high, low = factors(lax.axis_size("expert"))
+    result = result.reshape(high, low, tok_local, width)
+    moe_out = scatter_sum(
+        [[result[step, j] for j in range(low)] for step in range(high)], "expert"
+    ).astype(jnp.bfloat16)
     return (moe_out, attn_out, new_states)
 
 

time: 539 us -> 380 us (0.71); the launches traced: 528 us -> 377 us
  blocking collectives: 193 us -> 0 us
  matrix products: 105 us -> 153 us
  starting transfers between devices: 5.09 us -> 36 us
  local copies, waits for them, and re-layouts: 83.1 us -> 64.6 us
  between operations: 14.8 us -> 1.18 us
  waiting for transfers between devices: 106 us -> 93.4 us
  other arithmetic: 19.3 us -> 26.5 us
    all_to_all x3 -> x0, blocking collectives: 193 us -> none  [the longest x1 76.5 us: on_device(): lax.all_to_all(result.reshape(shape), 'expert', split_axis=0, concat_axis...]
    ppermute x0 -> x27, waiting for transfers between devices: none -> 93.4 us  [the longest x5 31 us: gather_parts(): parts.append([lax.ppermute(block, axis, high_pairs(high, low, step))])]
    reduce_scatter x1 -> x0, waiting for transfers between devices: 68.8 us -> none  [on_device(): lax.psum_scatter(jnp.dot(normed, out_proj, preferred_element_type=jnp.flo...]
    all_to_all x1 -> x0, waiting for transfers between devices: 37 us -> none  [on_device(): lax.all_to_all(lax.all_to_all(result.reshape(shape), 'expert', split_axis...]
    ppermute x0 -> x27, starting transfers between devices: none -> 36 us  [the longest x5 10.9 us: gather_parts(): parts.append([lax.ppermute(block, axis, high_pairs(high, low, step))])]
    reshape x7 -> x0, local copies, waits for them, and re-layouts: 28 us -> none  [the longest x2 9.71 us: on_device(): outgoing = outgoing.reshape(expert_axis, data_axis, capacity, width)]
    squeeze x16, local copies, waits for them, and re-layouts: 0.85 us -> 21.1 us  [on_device(): states, mixed = lax.scan(block_step, jnp.swapaxes(cache, 0, 1), inputs)]
    all_to_all x4 -> x0, local copies, waits for them, and re-layouts: 14.9 us -> none  [the longest x1 5.77 us: on_device(): lax.all_to_all(lax.all_to_all(result.reshape(shape), 'expert', split_axis...]
  transfers between devices with their start and end apart: 2 -> 27, of which waited for: 2 -> 15; matrix products, arithmetic and copies ran while one was open for 1% -> 5% of each run, Pallas kernels for 0% -> 0%
where the time goes in v1:
time: 380 us; the launch traced here: 377 us
  matrix products  153 us (40%)
  waiting for transfers between devices  93.4 us (25%)
  local copies, waits for them, and re-layouts  64.6 us (17%)
  starting transfers between devices  36 us (9%)
  other arithmetic  26.5 us (7%)
    ppermute x5, waiting for transfers between devices, gather_parts(): parts.append([lax.ppermute(block, axis, high_pairs(high, low, step))])  31 us
    ppermute x8, waiting for transfers between devices, scatter_sum(): lax.ppermute(row[1], axis, low_pairs(high, low)).astype(jnp.float32)  30.5 us
    dynamic_slice x32, local copies, waits for them, and re-layouts, on_device(): states, mixed = lax.scan(block_step, jnp.swapaxes(cache, 0, 1), inputs)  26.9 us
    ppermute x6, waiting for transfers between devices, scatter_sum(): lax.ppermute(sent, axis, reverse(high_pairs(high, low, step)))  25.9 us
    squeeze x16, local copies, waits for them, and re-layouts, on_device(): states, mixed = lax.scan(block_step, jnp.swapaxes(cache, 0, 1), inputs)  21.1 us
    dot_general x8, matrix products, block_step(): recalled = jnp.einsum('cr,hrcv->hcv', member_b, recalled, precision=HIGH)  19.1 us
    dot_general x8, matrix products, block_step(): jnp.einsum('hrc,hck,hcv->hrkv', carried, key_h, updates, precision=HIGH)  18.2 us
    dot_general x8, matrix products, block_step(): jnp.einsum('hij,hjv->hiv', query_dots * decays, updates, precision=HIGH)  12.8 us
  transfers between devices with their start and end apart: 27, of which 15 were waited for; matrix products, arithmetic and copies ran while one was open for 5% of the time, Pallas kernels for 0%

profile of v1, /device:TPU:0, one launch (start us, length us, event | category | flops | bytes accessed | tf_op | source)
XLA Modules:
  0.0 376.9 jit_solution(13367366230055345428)
XLA Ops:
  7.1 1.7 multiply_multiply_fusion
  8.8 2.3 reshape.174
  13.5 199.0 %while.12 = (s32[]{:T(128)}, f32[4,4,128,128]{3,2,1,0:T(8,128)S(1)}, f32[8,64,4,128]{3,1,2,0:T(8,128)}, f32[8,64,4]{1,0,2:T(8,128)}, f32[8,64,4]{1,2,0:T(4,128)}...) while((s32[]{:T(128)}, ...), condition=%wide.region_5.6_spmd, body=%wide.region_4.5_spmd.sunk | while | flops 860401152 | bytes 12364117 | solution.py:168
  26.2 2.4 fusion.256
  36.0 2.3 fusion.257
  51.1 2.4 fusion.256
  60.9 2.3 fusion.257
  75.9 2.4 fusion.256
  85.7 2.3 fusion.257
  100.8 2.4 fusion.256
  110.6 2.3 fusion.257
  125.7 2.4 fusion.256
  135.5 2.3 fusion.257
  150.5 2.4 fusion.256
  160.3 2.3 fusion.257
  175.4 2.4 fusion.256
  185.2 2.3 fusion.257
  200.2 2.4 fusion.256
  210.0 2.3 fusion.257
  214.1 2.9 copy.97
  217.9 2.8 convolution_convert_fusion
  223.0 3.0 collective-permute-start.1
  226.0 2.0 collective-permute-start.5
  228.1 5.4 %collective-permute-done.1 = bf16[64,2048]{1,0:T(8,128)(2,1)} collective-permute-done((bf16[64,2048]{1,0:T(8,128)(2,1)}, bf16[64,2048]{1,0:T(8,128)(2,1)}, u32[]{:S(2)}, u32[]{:S(2)}) %collective-permute-start.1) | collective-permute-done | bytes 262176 | tf_op jit(solution)/shard_map/ppermute | solution.py:108
  233.4 5.6 %collective-permute-done.3 = bf16[64,2048]{1,0:T(8,128)(2,1)} collective-permute-done((bf16[64,2048]{1,0:T(8,128)(2,1)}, bf16[64,2048]{1,0:T(8,128)(2,1)}, u32[]{:S(2)}, u32[]{:S(2)}) %collective-permute-start.3) | collective-permute-done | bytes 262176 | tf_op jit(solution)/shard_map/ppermute | solution.py:108
  239.0 5.6 %collective-permute-done.5 = bf16[64,2048]{1,0:T(8,128)(2,1)} collective-permute-done((bf16[64,2048]{1,0:T(8,128)(2,1)}, bf16[64,2048]{1,0:T(8,128)(2,1)}, u32[]{:S(2)}, u32[]{:S(2)}) %collective-permute-start.5) | collective-permute-done | bytes 262176 | tf_op jit(solution)/shard_map/ppermute | solution.py:108
  244.7 2.3 fusion.94
  247.0 2.1 collective-permute-start.2
  249.0 2.6 collective-permute-start.4
  251.9 1.7 collective-permute-start.15
  253.7 4.0 %collective-permute-done.2 = bf16[64,2048]{1,0:T(8,128)(2,1)} collective-permute-done((bf16[64,2048]{1,0:T(8,128)(2,1)}, bf16[64,2048]{1,0:T(8,128)(2,1)}, u32[]{:S(2)}, u32[]{:S(2)}) %collective-permute-start.2) | collective-permute-done | bytes 262176 | tf_op jit(solution)/shard_map/ppermute | solution.py:113
  259.1 11.1 %collective-permute-done.4 = bf16[64,2048]{1,0:T(8,128)(2,1)} collective-permute-done((bf16[64,2048]{1,0:T(8,128)(2,1)}, bf16[64,2048]{1,0:T(8,128)(2,1)}, u32[]{:S(2)}, u32[]{:S(2)}) %collective-permute-start.4) | collective-permute-done | bytes 262176 | tf_op jit(solution)/shard_map/ppermute | solution.py:113
  275.9 3.4 collective-permute-start.8
  281.0 4.4 %collective-permute-start.10 = (bf16[64,2112]{1,0:T(8,128)(2,1)S(1)}, bf16[64,2112]{1,0:T(8,128)(2,1)S(1)}, u32[]{:S(2)}, u32[]{:S(2)}) collective-permute-start(bf16[64,2112]{1,0:T(8,128)(2,1)S(1)} %concatenate.15), channel_id=1, source_target_pairs={{0,16},{4,20},{8,24},{12,28},{16,0},{20,4},{24,8},{28,12},{1,17},{... | collective-permute-start | bytes 811016 | tf_op jit(solution)/shard_map/ppermute | solution.py:95
  287.0 9.8 %collective-permute-done.10 = bf16[64,2112]{1,0:T(8,128)(2,1)S(1)} collective-permute-done((bf16[64,2112]{1,0:T(8,128)(2,1)S(1)}, bf16[64,2112]{1,0:T(8,128)(2,1)S(1)}, u32[]{:S(2)}, u32[]{:S(2)}) %collective-permute-start.10) | collective-permute-done | bytes 270368 | tf_op jit(solution)/shard_map/ppermute | solution.py:95
  298.4 6.8 %collective-permute-done.12 = bf16[64,2112]{1,0:T(8,128)(2,1)S(1)} collective-permute-done((bf16[64,2112]{1,0:T(8,128)(2,1)S(1)}, bf16[64,2112]{1,0:T(8,128)(2,1)S(1)}, u32[]{:S(2)}, u32[]{:S(2)}) %collective-permute-start.12) | collective-permute-done | bytes 270368 | tf_op jit(solution)/shard_map/ppermute | solution.py:95
  305.2 14.4 %collective-permute-done.18 = bf16[256,2048]{1,0:T(8,128)(2,1)} collective-permute-done((bf16[256,2048]{1,0:T(8,128)(2,1)}, bf16[256,2048]{1,0:T(8,128)(2,1)}, u32[]{:S(2)}, u32[]{:S(2)}) %collective-permute-start.18) | collective-permute-done | bytes 1048608 | tf_op jit(solution)/shard_map/ppermute | solution.py:95
  321.8 4.4 %collective-permute-done.13 = bf16[64,2112]{1,0:T(8,128)(2,1)S(1)} collective-permute-done((bf16[64,2112]{1,0:T(8,128)(2,1)S(1)}, bf16[64,2112]{1,0:T(8,128)(2,1)S(1)}, u32[]{:S(2)}, u32[]{:S(2)}) %collective-permute-start.13) | collective-permute-done | bytes 270368 | tf_op jit(solution)/shard_map/ppermute | solution.py:98
  326.6 2.9 fusion.62
  329.7 2.9 fusion.58
  332.6 2.9 fusion.60
  337.4 3.9 %fusion.53 = bf16[512,2048]{1,0:T(8,128)(2,1)S(1)} fusion(bf16[256,2048]{1,0:T(8,128)(2,1)S(1)} %collective-permute-done.19, bf16[256,2048]{1,0:T(8,128)(2,1)} %collective-permute-done.18, bf16[256,2048]{1,0:T(8,128)(2,1)S(1)} %collective-permute-done.17, bf16[256,2048]{1,0:T(8,128)(2,1)S(1)} %bitcast.336, bf16[512,256]{0,1:T(8,128)(2,1)S(1)} %fusion.81, ...), kind=kOutput, calls=%fused_computation.81 | convolution fusion | flops 2169503744 | bytes 7340032 | tf_op jit(solution)/shard_map/dot_general | solution.py:221
  345.5 5.1 %collective-permute-done.21 = bf16[64,2048]{1,0:T(8,128)(2,1)S(1)} collective-permute-done((bf16[64,2048]{1,0:T(8,128)(2,1)S(1)}, bf16[64,2048]{1,0:T(8,128)(2,1)S(1)}, u32[]{:S(2)}, u32[]{:S(2)}) %collective-permute-start.21) | collective-permute-done | bytes 262176 | tf_op jit(solution)/shard_map/ppermute | solution.py:108
  350.6 5.6 %collective-permute-done.23 = bf16[64,2048]{1,0:T(8,128)(2,1)S(1)} collective-permute-done((bf16[64,2048]{1,0:T(8,128)(2,1)S(1)}, bf16[64,2048]{1,0:T(8,128)(2,1)S(1)}, u32[]{:S(2)}, u32[]{:S(2)}) %collective-permute-start.23) | collective-permute-done | bytes 262176 | tf_op jit(solution)/shard_map/ppermute | solution.py:108
  356.2 3.1 collective-permute-done.25
  360.6 3.2 collective-permute-start.24
  365.1 3.6 collective-permute-done.22
  368.7 7.3 %collective-permute-done.24 = bf16[64,2048]{1,0:T(8,128)(2,1)S(1)} collective-permute-done((bf16[64,2048]{1,0:T(8,128)(2,1)S(1)}, bf16[64,2048]{1,0:T(8,128)(2,1)S(1)}, u32[]{:S(2)}, u32[]{:S(2)}) %collective-permute-start.24) | collective-permute-done | bytes 262176 | tf_op jit(solution)/shard_map/ppermute | solution.py:113
  (383 shorter events, 198.1 us)
Async XLA Ops:
  0.6 217.2 %copy-start = (bf16[512,2048]{1,0:T(8,128)(2,1)S(1)}, bf16[512,2048]{1,0:T(8,128)(2,1)}, u32[]{:S(2)}) copy-start(bf16[512,2048]{1,0:T(8,128)(2,1)} %param.27) | copy-start | bytes 6291460
  7.1 1.7 copy-start.4
  8.7 2.4 copy-start.13
  8.7 3.4 copy-start.7
  8.7 4.1 %copy-start.8 = (f32[512,4]{0,1:T(4,128)S(1)}, f32[512,4]{0,1:T(4,128)}, u32[]{:S(2)}) copy-start(f32[512,4]{0,1:T(4,128)} %param.22) | copy-start | bytes 24580
  26.2 5.2 %copy-start.1 = (f32[64,4,1,1]{1,2,3,0:T(1,128)S(1)}, f32[64,4,1,1]{1,2,3,0:T(1,128)}, u32[]{:S(2)}) copy-start(f32[64,4,1,1]{1,2,3,0:T(1,128)} %copy.188) | copy-start | bytes 3076 | tf_op jit(solution)/shard_map/while
  51.1 5.2 %copy-start.1 = (f32[64,4,1,1]{1,2,3,0:T(1,128)S(1)}, f32[64,4,1,1]{1,2,3,0:T(1,128)}, u32[]{:S(2)}) copy-start(f32[64,4,1,1]{1,2,3,0:T(1,128)} %copy.188) | copy-start | bytes 3076 | tf_op jit(solution)/shard_map/while
  75.9 5.2 %copy-start.1 = (f32[64,4,1,1]{1,2,3,0:T(1,128)S(1)}, f32[64,4,1,1]{1,2,3,0:T(1,128)}, u32[]{:S(2)}) copy-start(f32[64,4,1,1]{1,2,3,0:T(1,128)} %copy.188) | copy-start | bytes 3076 | tf_op jit(solution)/shard_map/while
  100.8 5.3 %copy-start.1 = (f32[64,4,1,1]{1,2,3,0:T(1,128)S(1)}, f32[64,4,1,1]{1,2,3,0:T(1,128)}, u32[]{:S(2)}) copy-start(f32[64,4,1,1]{1,2,3,0:T(1,128)} %copy.188) | copy-start | bytes 3076 | tf_op jit(solution)/shard_map/while
  125.7 5.2 %copy-start.1 = (f32[64,4,1,1]{1,2,3,0:T(1,128)S(1)}, f32[64,4,1,1]{1,2,3,0:T(1,128)}, u32[]{:S(2)}) copy-start(f32[64,4,1,1]{1,2,3,0:T(1,128)} %copy.188) | copy-start | bytes 3076 | tf_op jit(solution)/shard_map/while
  150.5 5.2 %copy-start.1 = (f32[64,4,1,1]{1,2,3,0:T(1,128)S(1)}, f32[64,4,1,1]{1,2,3,0:T(1,128)}, u32[]{:S(2)}) copy-start(f32[64,4,1,1]{1,2,3,0:T(1,128)} %copy.188) | copy-start | bytes 3076 | tf_op jit(solution)/shard_map/while
  175.4 5.2 %copy-start.1 = (f32[64,4,1,1]{1,2,3,0:T(1,128)S(1)}, f32[64,4,1,1]{1,2,3,0:T(1,128)}, u32[]{:S(2)}) copy-start(f32[64,4,1,1]{1,2,3,0:T(1,128)} %copy.188) | copy-start | bytes 3076 | tf_op jit(solution)/shard_map/while
  200.2 5.2 %copy-start.1 = (f32[64,4,1,1]{1,2,3,0:T(1,128)S(1)}, f32[64,4,1,1]{1,2,3,0:T(1,128)}, u32[]{:S(2)}) copy-start(f32[64,4,1,1]{1,2,3,0:T(1,128)} %copy.188) | copy-start | bytes 3076 | tf_op jit(solution)/shard_map/while
  212.5 4.7 %copy-start.11 = (f32[128]{0:T(128)S(1)}, f32[128]{0:T(128)}, u32[]{:S(2)}) copy-start(f32[128]{0:T(128)} %param.26) | copy-start | bytes 1540
  217.8 10.2 %copy-start.9 = (f32[64,10]{0,1:T(8,128)S(1)}, f32[64,10]{0,1:T(8,128)}, u32[]{:S(2)}) copy-start(f32[64,10]{0,1:T(8,128)} %param.31) | copy-start | bytes 7684
  217.9 10.2 %copy-start.10 = (s32[64,10]{0,1:T(8,128)S(1)}, s32[64,10]{0,1:T(8,128)}, u32[]{:S(2)}) copy-start(s32[64,10]{0,1:T(8,128)} %param.30) | copy-start | bytes 7684
  220.6 1.3 copy-start.2
  222.0 48.2 %copy-start.5 = (bf16[64,2048]{1,0:T(8,128)(2,1)S(1)}, bf16[64,2048]{1,0:T(8,128)(2,1)}, u32[]{:S(2)}) copy-start(bf16[64,2048]{1,0:T(8,128)(2,1)} %param.28) | copy-start | bytes 786436
  222.9 49.5 %copy-start.6 = (f32[2048]{0:T(1024)S(1)}, f32[2048]{0:T(1024)}, u32[]{:S(2)}) copy-start(f32[2048]{0:T(1024)} %param.29) | copy-start | bytes 24580
  223.0 10.5 %collective-permute-start.1 = (bf16[64,2048]{1,0:T(8,128)(2,1)}, bf16[64,2048]{1,0:T(8,128)(2,1)}, u32[]{:S(2)}, u32[]{:S(2)}) collective-permute-start(bf16[64,2048]{1,0:T(8,128)(2,1)} %get-tuple-element.153), channel_id=1, source_target_pairs={{0,4},{4,0},{8,12},{12,8},{16,20},{20,16},{24,28},{28,24},{1,5},{5... | collective-permute-start | bytes 786440 | tf_op jit(solution)/shard_map/ppermute | solution.py:108
  226.0 13.1 %collective-permute-start.3 = (bf16[64,2048]{1,0:T(8,128)(2,1)}, bf16[64,2048]{1,0:T(8,128)(2,1)}, u32[]{:S(2)}, u32[]{:S(2)}) collective-permute-start(bf16[64,2048]{1,0:T(8,128)(2,1)} %get-tuple-element.152), channel_id=1, source_target_pairs={{0,4},{4,0},{8,12},{12,8},{16,20},{20,16},{24,28},{28,24},{1,5},{5... | collective-permute-start | bytes 786440 | tf_op jit(solution)/shard_map/ppermute | solution.py:108
  226.0 18.7 %collective-permute-start.5 = (bf16[64,2048]{1,0:T(8,128)(2,1)}, bf16[64,2048]{1,0:T(8,128)(2,1)}, u32[]{:S(2)}, u32[]{:S(2)}) collective-permute-start(bf16[64,2048]{1,0:T(8,128)(2,1)} %get-tuple-element.151), channel_id=1, source_target_pairs={{0,4},{4,0},{8,12},{12,8},{16,20},{20,16},{24,28},{28,24},{1,5},{5... | collective-permute-start | bytes 786440 | tf_op jit(solution)/shard_map/ppermute | solution.py:108
  228.0 23.9 %collective-permute-start = (bf16[64,2048]{1,0:T(8,128)(2,1)}, bf16[64,2048]{1,0:T(8,128)(2,1)}, u32[]{:S(2)}, u32[]{:S(2)}) collective-permute-start(bf16[64,2048]{1,0:T(8,128)(2,1)} %get-tuple-element.150), channel_id=1, source_target_pairs={{0,4},{4,0},{8,12},{12,8},{16,20},{20,16},{24,28},{28,24},{1,5},{5... | collective-permute-start | bytes 786440 | tf_op jit(solution)/shard_map/ppermute | solution.py:108
  228.0 104.6 %collective-permute-start.14 = (bf16[2048,512]{1,0:T(8,128)(2,1)}, bf16[2048,512]{1,0:T(8,128)(2,1)}, u32[]{:S(2)}, u32[]{:S(2)}) collective-permute-start(bf16[2048,512]{1,0:T(8,128)(2,1)} %bitcast.45), channel_id=1, source_target_pairs={{0,1},{1,0},{2,3},{3,2},{4,5},{5,4},{6,7},{7,6},{8,9},{9,8},{10,11... | collective-permute-start | bytes 6291464 | tf_op jit(solution)/shard_map/ppermute | solution.py:98
  247.0 10.7 %collective-permute-start.2 = (bf16[64,2048]{1,0:T(8,128)(2,1)}, bf16[64,2048]{1,0:T(8,128)(2,1)}, u32[]{:S(2)}, u32[]{:S(2)}) collective-permute-start(bf16[64,2048]{1,0:T(8,128)(2,1)} %get-tuple-element.154), channel_id=1, source_target_pairs={{8,0},{12,4},{0,8},{4,12},{24,16},{28,20},{16,24},{20,28},{9,1},{1... | collective-permute-start | bytes 786440 | tf_op jit(solution)/shard_map/ppermute | solution.py:113
  249.0 21.1 %collective-permute-start.4 = (bf16[64,2048]{1,0:T(8,128)(2,1)}, bf16[64,2048]{1,0:T(8,128)(2,1)}, u32[]{:S(2)}, u32[]{:S(2)}) collective-permute-start(bf16[64,2048]{1,0:T(8,128)(2,1)} %get-tuple-element.156), channel_id=1, source_target_pairs={{16,0},{20,4},{24,8},{28,12},{0,16},{4,20},{8,24},{12,28},{17,1},{... | collective-permute-start | bytes 786440 | tf_op jit(solution)/shard_map/ppermute | solution.py:113
  251.6 18.5 %collective-permute-start.6 = (bf16[64,2048]{1,0:T(8,128)(2,1)}, bf16[64,2048]{1,0:T(8,128)(2,1)}, u32[]{:S(2)}, u32[]{:S(2)}) collective-permute-start(bf16[64,2048]{1,0:T(8,128)(2,1)} %get-tuple-element.155), channel_id=1, source_target_pairs={{24,0},{28,4},{16,8},{20,12},{8,16},{12,20},{0,24},{4,28},{25,1},{... | collective-permute-start | bytes 786440 | tf_op jit(solution)/shard_map/ppermute | solution.py:113
  251.9 69.3 %collective-permute-start.15 = (bf16[2048,512]{1,0:T(8,128)(2,1)}, bf16[2048,512]{1,0:T(8,128)(2,1)}, u32[]{:S(2)}, u32[]{:S(2)}) collective-permute-start(bf16[2048,512]{1,0:T(8,128)(2,1)} %bitcast.45), channel_id=1, source_target_pairs={{0,2},{1,3},{2,0},{3,1},{4,6},{5,7},{6,4},{7,5},{8,10},{9,11},{10,... | collective-permute-start | bytes 6291464 | tf_op jit(solution)/shard_map/ppermute | solution.py:95
  257.7 62.0 %collective-permute-start.18 = (bf16[256,2048]{1,0:T(8,128)(2,1)}, bf16[256,2048]{1,0:T(8,128)(2,1)}, u32[]{:S(2)}, u32[]{:S(2)}) collective-permute-start(bf16[256,2048]{1,0:T(8,128)(2,1)} %bitcast.334), channel_id=1, source_target_pairs={{0,2},{1,3},{2,0},{3,1},{4,6},{5,7},{6,4},{7,5},{8,10},{9,11},{10,... | collective-permute-start | bytes 3145736 | tf_op jit(solution)/shard_map/ppermute | solution.py:95
  271.7 0.7 copy-start.3
  274.3 30.9 %copy-start.12 = (bf16[1,256,2048]{2,1,0:T(8,128)(2,1)S(1)}, bf16[1,256,2048]{2,1,0:T(8,128)(2,1)}, u32[]{:S(2)}) copy-start(bf16[1,256,2048]{2,1,0:T(8,128)(2,1)} %param.33) | copy-start | bytes 3145732
  274.3 6.6 %collective-permute-start.7 = (bf16[64,2112]{1,0:T(8,128)(2,1)S(1)}, bf16[64,2112]{1,0:T(8,128)(2,1)S(1)}, u32[]{:S(2)}, u32[]{:S(2)}) collective-permute-start(bf16[64,2112]{1,0:T(8,128)(2,1)S(1)} %concatenate.15), channel_id=1, source_target_pairs={{0,4},{4,0},{8,12},{12,8},{16,20},{20,16},{24,28},{28,24},{1,5},{5... | collective-permute-start | bytes 811016 | tf_op jit(solution)/shard_map/ppermute | solution.py:98
  275.9 9.4 %collective-permute-start.8 = (bf16[64,2112]{1,0:T(8,128)(2,1)S(1)}, bf16[64,2112]{1,0:T(8,128)(2,1)S(1)}, u32[]{:S(2)}, u32[]{:S(2)}) collective-permute-start(bf16[64,2112]{1,0:T(8,128)(2,1)S(1)} %concatenate.15), channel_id=1, source_target_pairs={{0,8},{4,12},{8,0},{12,4},{16,24},{20,28},{24,16},{28,20},{1,9},{5... | collective-permute-start | bytes 811016 | tf_op jit(solution)/shard_map/ppermute | solution.py:95
  281.0 15.8 %collective-permute-start.10 = (bf16[64,2112]{1,0:T(8,128)(2,1)S(1)}, bf16[64,2112]{1,0:T(8,128)(2,1)S(1)}, u32[]{:S(2)}, u32[]{:S(2)}) collective-permute-start(bf16[64,2112]{1,0:T(8,128)(2,1)S(1)} %concatenate.15), channel_id=1, source_target_pairs={{0,16},{4,20},{8,24},{12,28},{16,0},{20,4},{24,8},{28,12},{1,17},{... | collective-permute-start | bytes 811016 | tf_op jit(solution)/shard_map/ppermute | solution.py:95
  285.3 11.4 %collective-permute-start.9 = (bf16[64,2112]{1,0:T(8,128)(2,1)S(1)}, bf16[64,2112]{1,0:T(8,128)(2,1)S(1)}, u32[]{:S(2)}, u32[]{:S(2)}) collective-permute-start(bf16[64,2112]{1,0:T(8,128)(2,1)S(1)} %collective-permute-done.8), channel_id=1, source_target_pairs={{0,4},{4,0},{8,12},{12,8},{16,20},{20,16},{24,28},{28,24},{1,5},{5... | collective-permute-start | bytes 811016 | tf_op jit(solution)/shard_map/ppermute | solution.py:98
  296.8 8.4 %collective-permute-start.12 = (bf16[64,2112]{1,0:T(8,128)(2,1)S(1)}, bf16[64,2112]{1,0:T(8,128)(2,1)S(1)}, u32[]{:S(2)}, u32[]{:S(2)}) collective-permute-start(bf16[64,2112]{1,0:T(8,128)(2,1)S(1)} %concatenate.15), channel_id=1, source_target_pairs={{0,24},{4,28},{8,16},{12,20},{16,8},{20,12},{24,0},{28,4},{1,25},{... | collective-permute-start | bytes 811016 | tf_op jit(solution)/shard_map/ppermute | solution.py:95
  296.8 24.4 %collective-permute-start.11 = (bf16[64,2112]{1,0:T(8,128)(2,1)S(1)}, bf16[64,2112]{1,0:T(8,128)(2,1)S(1)}, u32[]{:S(2)}, u32[]{:S(2)}) collective-permute-start(bf16[64,2112]{1,0:T(8,128)(2,1)S(1)} %collective-permute-done.10), channel_id=1, source_target_pairs={{0,4},{4,0},{8,12},{12,8},{16,20},{20,16},{24,28},{28,24},{1,5},{5... | collective-permute-start | bytes 811016 | tf_op jit(solution)/shard_map/ppermute | solution.py:98
  305.2 32.1 %collective-permute-start.17 = (bf16[256,2048]{1,0:T(8,128)(2,1)S(1)}, bf16[256,2048]{1,0:T(8,128)(2,1)S(1)}, u32[]{:S(2)}, u32[]{:S(2)}) collective-permute-start(bf16[256,2048]{1,0:T(8,128)(2,1)S(1)} %bitcast.335), channel_id=1, source_target_pairs={{0,1},{1,0},{2,3},{3,2},{4,5},{5,4},{6,7},{7,6},{8,9},{9,8},{10,11... | collective-permute-start | bytes 3145736 | tf_op jit(solution)/shard_map/ppermute | solution.py:98
  319.6 6.5 %collective-permute-start.13 = (bf16[64,2112]{1,0:T(8,128)(2,1)S(1)}, bf16[64,2112]{1,0:T(8,128)(2,1)S(1)}, u32[]{:S(2)}, u32[]{:S(2)}) collective-permute-start(bf16[64,2112]{1,0:T(8,128)(2,1)S(1)} %collective-permute-done.12), channel_id=1, source_target_pairs={{0,4},{4,0},{8,12},{12,8},{16,20},{20,16},{24,28},{28,24},{1,5},{5... | collective-permute-start | bytes 811016 | tf_op jit(solution)/shard_map/ppermute | solution.py:98
  321.1 16.2 %collective-permute-start.19 = (bf16[256,2048]{1,0:T(8,128)(2,1)}, bf16[256,2048]{1,0:T(8,128)(2,1)S(1)}, u32[]{:S(2)}, u32[]{:S(2)}) collective-permute-start(bf16[256,2048]{1,0:T(8,128)(2,1)} %collective-permute-done.18), channel_id=1, source_target_pairs={{0,1},{1,0},{2,3},{3,2},{4,5},{5,4},{6,7},{7,6},{8,9},{9,8},{10,11... | collective-permute-start | bytes 3145736 | tf_op jit(solution)/shard_map/ppermute | solution.py:98
  321.2 14.6 %collective-permute-start.16 = (bf16[2048,512]{1,0:T(8,128)(2,1)}, bf16[2048,512]{1,0:T(8,128)(2,1)S(1)}, u32[]{:S(2)}, u32[]{:S(2)}) collective-permute-start(bf16[2048,512]{1,0:T(8,128)(2,1)} %collective-permute-done.15), channel_id=1, source_target_pairs={{0,1},{1,0},{2,3},{3,2},{4,5},{5,4},{6,7},{7,6},{8,9},{9,8},{10,11... | collective-permute-start | bytes 6291464 | tf_op jit(solution)/shard_map/ppermute | solution.py:98
  341.4 9.2 %collective-permute-start.21 = (bf16[64,2048]{1,0:T(8,128)(2,1)S(1)}, bf16[64,2048]{1,0:T(8,128)(2,1)S(1)}, u32[]{:S(2)}, u32[]{:S(2)}) collective-permute-start(bf16[64,2048]{1,0:T(8,128)(2,1)S(1)} %get-tuple-element.146), channel_id=1, source_target_pairs={{0,4},{4,0},{8,12},{12,8},{16,20},{20,16},{24,28},{28,24},{1,5},{5... | collective-permute-start | bytes 786440 | tf_op jit(solution)/shard_map/ppermute | solution.py:108
  342.9 13.3 %collective-permute-start.23 = (bf16[64,2048]{1,0:T(8,128)(2,1)S(1)}, bf16[64,2048]{1,0:T(8,128)(2,1)S(1)}, u32[]{:S(2)}, u32[]{:S(2)}) collective-permute-start(bf16[64,2048]{1,0:T(8,128)(2,1)S(1)} %get-tuple-element.145), channel_id=1, source_target_pairs={{0,4},{4,0},{8,12},{12,8},{16,20},{20,16},{24,28},{28,24},{1,5},{5... | collective-permute-start | bytes 786440 | tf_op jit(solution)/shard_map/ppermute | solution.py:108
  343.5 15.9 %collective-permute-start.25 = (bf16[64,2048]{1,0:T(8,128)(2,1)S(1)}, bf16[64,2048]{1,0:T(8,128)(2,1)S(1)}, u32[]{:S(2)}, u32[]{:S(2)}) collective-permute-start(bf16[64,2048]{1,0:T(8,128)(2,1)S(1)} %get-tuple-element.144), channel_id=1, source_target_pairs={{0,4},{4,0},{8,12},{12,8},{16,20},{20,16},{24,28},{28,24},{1,5},{5... | collective-permute-start | bytes 786440 | tf_op jit(solution)/shard_map/ppermute | solution.py:108
  345.0 20.1 %collective-permute-start.20 = (bf16[64,2048]{1,0:T(8,128)(2,1)S(1)}, bf16[64,2048]{1,0:T(8,128)(2,1)S(1)}, u32[]{:S(2)}, u32[]{:S(2)}) collective-permute-start(bf16[64,2048]{1,0:T(8,128)(2,1)S(1)} %get-tuple-element.143), channel_id=1, source_target_pairs={{0,4},{4,0},{8,12},{12,8},{16,20},{20,16},{24,28},{28,24},{1,5},{5... | collective-permute-start | bytes 786440 | tf_op jit(solution)/shard_map/ppermute | solution.py:108
  359.6 9.1 %collective-permute-start.22 = (bf16[64,2048]{1,0:T(8,128)(2,1)S(1)}, bf16[64,2048]{1,0:T(8,128)(2,1)S(1)}, u32[]{:S(2)}, u32[]{:S(2)}) collective-permute-start(bf16[64,2048]{1,0:T(8,128)(2,1)S(1)} %get-tuple-element.147), channel_id=1, source_target_pairs={{8,0},{12,4},{0,8},{4,12},{24,16},{28,20},{16,24},{20,28},{9,1},{1... | collective-permute-start | bytes 786440 | tf_op jit(solution)/shard_map/ppermute | solution.py:113
  360.6 15.4 %collective-permute-start.24 = (bf16[64,2048]{1,0:T(8,128)(2,1)S(1)}, bf16[64,2048]{1,0:T(8,128)(2,1)S(1)}, u32[]{:S(2)}, u32[]{:S(2)}) collective-permute-start(bf16[64,2048]{1,0:T(8,128)(2,1)S(1)} %get-tuple-element.149), channel_id=1, source_target_pairs={{16,0},{20,4},{24,8},{28,12},{0,16},{4,20},{8,24},{12,28},{17,1},{... | collective-permute-start | bytes 786440 | tf_op jit(solution)/shard_map/ppermute | solution.py:113
  363.7 12.3 %collective-permute-start.26 = (bf16[64,2048]{1,0:T(8,128)(2,1)S(1)}, bf16[64,2048]{1,0:T(8,128)(2,1)S(1)}, u32[]{:S(2)}, u32[]{:S(2)}) collective-permute-start(bf16[64,2048]{1,0:T(8,128)(2,1)S(1)} %get-tuple-element.148), channel_id=1, source_target_pairs={{24,0},{28,4},{16,8},{20,12},{8,16},{12,20},{0,24},{4,28},{25,1},{... | collective-permute-start | bytes 786440 | tf_op jit(solution)/shard_map/ppermute | solution.py:113

commit v2 on v1

--- a/solution.py
+++ b/solution.py
@@ -1,64 +1,183 @@
+import functools
+
 import jax
 import jax.numpy as jnp
 from jax import lax
+from jax.experimental import pallas as pl
+from jax.experimental.pallas import tpu as pltpu
 from jax.sharding import PartitionSpec as P
+
 
 HIGH = lax.Precision.HIGHEST
 epsilon = 1e-06
-block_rows = 64
-
-
-def unit_rows(values):
-    return values * lax.rsqrt(jnp.sum(values * values, axis=-1, keepdims=True) + epsilon)
-
-
-def block_step(states, item):
-    query_b, key_b, value_b, beta_b, decay_b, member_b = item
-    size = query_b.shape[0]
-    places = jnp.arange(size)
-    shared = jnp.dot(member_b, member_b.T, precision=HIGH) > 0.5
-    inside = shared & (places[:, None] >= places[None, :])
-    strict_part = inside & (places[:, None] > places[None, :])
-    running = jnp.dot(inside.astype(jnp.float32), decay_b, precision=HIGH).T
-    log_gaps = running[:, :, None] - running[:, None, :]
-    decays = jnp.where(inside[None], jnp.exp(jnp.minimum(log_gaps, 0.0)), 0.0)
-    key_h = jnp.swapaxes(key_b, 0, 1)
-    query_h = jnp.swapaxes(query_b, 0, 1)
-    value_h = jnp.swapaxes(value_b, 0, 1)
-    beta_h = beta_b.T
-    key_dots = jnp.einsum("hik,hjk->hij", key_h, key_h, precision=HIGH)
-    strict_terms = jnp.where(strict_part[None], decays * key_dots * beta_h[:, :, None], 0.0)
-    identity = jnp.eye(size, dtype=jnp.float32)[None]
-    inverse = identity - strict_terms
-    powered = strict_terms
-    covered = 2
-    while covered < size:
-        powered = jnp.einsum("hij,hjk->hik", powered, powered, precision=HIGH)
-        inverse = jnp.einsum("hij,hjk->hik", inverse, identity + powered, precision=HIGH)
-        covered = covered * 2
-    growth = jnp.exp(running)
-    targets = jnp.concatenate(
-        [key_h * (beta_h * growth)[:, :, None], value_h * beta_h[:, :, None]], axis=2
-    )
-    solved = jnp.einsum("hij,hjc->hic", inverse, targets, precision=HIGH)
-    width = key_h.shape[2]
-    key_mix = solved[:, :, :width]
-    value_mix = solved[:, :, width:]
-    recalled = jnp.einsum("hck,hrkv->hrcv", key_mix, states, precision=HIGH)
-    recalled = jnp.einsum("cr,hrcv->hcv", member_b, recalled, precision=HIGH)
-    updates = value_mix - recalled
-    from_state = jnp.einsum("hck,hrkv->hrcv", query_h, states, precision=HIGH)
-    from_state = jnp.einsum("cr,hrcv->hcv", member_b, from_state, precision=HIGH)
-    query_dots = jnp.einsum("hik,hjk->hij", query_h, key_h, precision=HIGH)
-    mixed = growth[:, :, None] * from_state + jnp.einsum(
-        "hij,hjv->hiv", query_dots * decays, updates, precision=HIGH
-    )
-    span_total = jnp.einsum("cr,ch->hr", member_b, decay_b, precision=HIGH)
-    end_gaps = span_total[:, :, None] - running[:, None, :]
-    carried = jnp.where(member_b.T[None] > 0.5, jnp.exp(jnp.minimum(end_gaps, 0.0)), 0.0)
-    fresh = jnp.einsum("hrc,hck,hcv->hrkv", carried, key_h, updates, precision=HIGH)
-    states = jnp.exp(span_total)[:, :, None, None] * states + fresh
-    return (states, jnp.swapaxes(mixed, 0, 1))
+chunk_rows = 128
+
+
+def product(left, right, contract=((1,), (0,))):
+    left, right = left.astype(jnp.bfloat16), right.astype(jnp.bfloat16)
+    return lax.dot_general(left, right, (contract, ((), ())), preferred_element_type=jnp.float32)
+
+
+def mix_kernel(
+    heads,
+    requests,
+    query_ref,
+    key_ref,
+    value_ref,
+    gate_ref,
+    beta_ref,
+    decay_ref,
+    lengths_ref,
+    cache_ref,
+    gain_ref,
+    proj_ref,
+    share_ref,
+    states_ref,
+):
+    step = pl.program_id(0)
+    rows = query_ref.shape[0]
+    dim = gain_ref.shape[1]
+    f32, bf16 = jnp.float32, jnp.bfloat16
+
+    @pl.when(step == 0)
+    def _():
+        states_ref[...] = cache_ref[...]
+
+    row_of = lax.broadcasted_iota(jnp.int32, (rows, rows), 0)
+    col_of = lax.broadcasted_iota(jnp.int32, (rows, rows), 1)
+    request_col = jnp.zeros((rows, 1), jnp.int32)
+    request_row = jnp.zeros((1, rows), jnp.int32)
+    place_col = lax.broadcasted_iota(jnp.int32, (rows, 1), 0) + step * rows
+    place_row = lax.broadcasted_iota(jnp.int32, (1, rows), 1) + step * rows
+    end = jnp.int32(0)
+    for r in range(requests):
+        end = end + lengths_ref[0, r]
+        request_col = request_col + (place_col >= end).astype(jnp.int32)
+        request_row = request_row + (place_row >= end).astype(jnp.int32)
+    shared = request_col == request_row
+    inside = shared & (row_of >= col_of)
+    after = shared & (row_of < col_of)
+    strict = shared & (row_of > col_of)
+    eye = (row_of == col_of).astype(f32)
+    decay = decay_ref[...]
+    inside_f = inside.astype(f32)
+    running = lax.dot_general(
+        inside_f, decay, (((1,), (0,)), ((), ())), precision=HIGH, preferred_element_type=f32
+    )
+    running_t = lax.dot_general(
+        decay, inside_f, (((0,), (1,)), ((), ())), precision=HIGH, preferred_element_type=f32
+    )
+    left = lax.dot_general(
+        after.astype(f32), decay, (((1,), (0,)), ((), ())), precision=HIGH, preferred_element_type=f32
+    )
+    totals = [
+        jnp.exp(jnp.sum(jnp.where(request_col == r, decay, 0.0), axis=0, keepdims=True))
+        for r in range(requests)
+    ]
+    in_col = [request_col == r for r in range(requests)]
+    in_row = [request_row == r for r in range(requests)]
+    levels = []
+    span = 2
+    while span < rows:
+        levels.append(
+            (row_of // (2 * span) == col_of // (2 * span))
+            & ((row_of // span) % 2 == 1)
+            & ((col_of // span) % 2 == 0)
+        )
+        span *= 2
+    first = (row_of // 2 == col_of // 2) & (row_of != col_of)
+
+    keys, queries, betas, growths, dots_q, terms, inverses = [], [], [], [], [], [], []
+    for h in range(heads):
+        lanes = slice(h * dim, (h + 1) * dim)
+        key = key_ref[:, lanes].astype(f32)
+        key = key * lax.rsqrt(jnp.sum(key * key, axis=-1, keepdims=True) + epsilon)
+        query = query_ref[:, lanes].astype(f32)
+        query = query * (
+            lax.rsqrt(jnp.sum(query * query, axis=-1, keepdims=True) + epsilon) * dim ** (-0.5)
+        )
+        beta = beta_ref[:, h : h + 1]
+        gaps = running[:, h : h + 1] - running_t[h : h + 1, :]
+        decays = jnp.where(inside, jnp.exp(jnp.minimum(gaps, 0.0)), 0.0)
+        key_b = key.astype(bf16)
+        both = product(
+            jnp.concatenate([key_b, query.astype(bf16)], axis=0), key_b, ((1,), (1,))
+        )
+        terms.append(jnp.where(strict, decays * both[:rows] * beta, 0.0))
+        dots_q.append((both[rows:] * decays).astype(bf16))
+        keys.append(key)
+        queries.append(query)
+        betas.append(beta)
+        growths.append(jnp.exp(running[:, h : h + 1]))
+    inverses = [eye - jnp.where(first, term, 0.0) for term in terms]
+    for mask in levels:
+        inner = [
+            product(jnp.where(mask, terms[h], 0.0), inverses[h]) for h in range(heads)
+        ]
+        inverses = [
+            inverses[h] - product(inverses[h], inner[h]) for h in range(heads)
+        ]
+    normed = []
+    for h in range(heads):
+        lanes = slice(h * dim, (h + 1) * dim)
+        targets = jnp.concatenate(
+            [keys[h] * (betas[h] * growths[h]), value_ref[:, lanes].astype(f32) * betas[h]], axis=1
+        )
+        solved = product(inverses[h], targets)
+        probe = jnp.concatenate(
+            [solved[:, :dim].astype(bf16), (queries[h] * growths[h]).astype(bf16)], axis=0
+        )
+        wide = jnp.concatenate(
+            [jnp.where(jnp.concatenate([in_col[r], in_col[r]], axis=0), probe, 0) for r in range(requests)],
+            axis=1,
+        )
+        state = states_ref[:, h].reshape(requests * dim, dim)
+        seen = product(wide, state)
+        update = (solved[:, dim:] - seen[:rows]).astype(bf16)
+        mixed = seen[rows:] + product(dots_q[h], update)
+        key_t = (keys[h] * jnp.exp(left[:, h : h + 1])).T.astype(bf16)
+        for r in range(requests):
+            fresh = product(jnp.where(in_row[r], key_t, 0), update)
+            states_ref[r, h] = totals[r][:, h : h + 1] * states_ref[r, h] + fresh
+        scale = lax.rsqrt(jnp.mean(mixed * mixed, axis=-1, keepdims=True) + epsilon)
+        gate = gate_ref[:, lanes].astype(f32)
+        normed.append(
+            (mixed * scale * gain_ref[...] * (gate * jax.nn.sigmoid(gate))).astype(bf16)
+        )
+    share_ref[...] = product(jnp.concatenate(normed, axis=1), proj_ref[...]).astype(bf16)
+
+
+def mix(queries, keys_in, values_in, gate_in, beta, decay, lengths, cache, norm_gain, out_proj):
+    tok_count, heads = beta.shape
+    requests = lengths.shape[1]
+    dim = norm_gain.shape[0]
+    rows = min(chunk_rows, tok_count)
+    width = out_proj.shape[1]
+    block = lambda cols: pl.BlockSpec((rows, cols), lambda c: (c, 0))
+    whole = lambda shape: pl.BlockSpec(shape, lambda c: (0,) * len(shape))
+    return pl.pallas_call(
+        functools.partial(mix_kernel, heads, requests),
+        grid=(tok_count // rows,),
+        in_specs=[
+            block(heads * dim),
+            block(heads * dim),
+            block(heads * dim),
+            block(heads * dim),
+            block(heads),
+            block(heads),
+            pl.BlockSpec(memory_space=pltpu.SMEM),
+            whole(cache.shape),
+            whole((1, dim)),
+            whole(out_proj.shape),
+        ],
+        out_specs=[block(width), whole(cache.shape)],
+        out_shape=[
+            jax.ShapeDtypeStruct((tok_count, width), jnp.bfloat16),
+            jax.ShapeDtypeStruct(cache.shape, jnp.float32),
+        ],
+        compiler_params=pltpu.CompilerParams(dimension_semantics=("arbitrary",)),
+        name="mix",
+    )(queries, keys_in, values_in, gate_in, beta, decay, lengths, cache, norm_gain[None], out_proj)
 
 
 def factors(size):
@@ -141,40 +260,6 @@
     gate_up,
     down_proj,
 ):
-    tok_count = queries.shape[0]
-    heads = beta.shape[1]
-    head_dim = norm_gain.shape[0]
-    requests = lengths.shape[1]
-    block = min(block_rows, tok_count)
-    blocks = tok_count // block
-    layout = (blocks, block, heads, head_dim)
-    query_n = unit_rows(queries.astype(jnp.float32).reshape(layout)) * head_dim ** (-0.5)
-    key_n = unit_rows(keys_in.astype(jnp.float32).reshape(layout))
-    value_f = values_in.astype(jnp.float32).reshape(layout)
-    ends = jnp.cumsum(lengths[0])
-    places = jnp.arange(tok_count, dtype=jnp.int32)
-    request = jnp.sum((places[:, None] >= ends[None, :]).astype(jnp.int32), axis=1)
-    member = (request[:, None] == jnp.arange(requests, dtype=jnp.int32)[None, :]).astype(
-        jnp.float32
-    )
-    inputs = (
-        query_n,
-        key_n,
-        value_f,
-        beta.reshape(blocks, block, heads),
-        decay.reshape(blocks, block, heads),
-        member.reshape(blocks, block, requests),
-    )
-    states, mixed = lax.scan(block_step, jnp.swapaxes(cache, 0, 1), inputs)
-    new_states = jnp.swapaxes(states, 0, 1)
-    mixed = mixed.reshape(tok_count, heads, head_dim)
-    gate_f = gate_in.astype(jnp.float32).reshape(tok_count, heads, head_dim)
-    scale = lax.rsqrt(jnp.mean(mixed * mixed, axis=-1, keepdims=True) + epsilon)
-    normed = (
-        (mixed * scale * norm_gain * jax.nn.silu(gate_f))
-        .astype(jnp.bfloat16)
-        .reshape(tok_count, heads * head_dim)
-    )
     width = residual.shape[1]
     tok_local = residual.shape[0]
     experts_all = lax.axis_size("expert") * lax.axis_size("dp")
@@ -182,7 +267,18 @@
     down_parts = sum(gather_parts(down_proj[0], "dp"), [])
     expert_of = sum(part_sources("dp"), [])
     expert_of = [lax.axis_index("expert") * lax.axis_size("dp") + place for place in expert_of]
-    share = jnp.dot(normed, out_proj, preferred_element_type=jnp.float32).astype(jnp.bfloat16)
+    share, new_states = mix(
+        queries,
+        keys_in,
+        values_in,
+        gate_in,
+        beta,
+        decay,
+        lengths,
+        cache,
+        norm_gain,
+        out_proj,
+    )
     share = share.reshape(lax.axis_size("expert"), tok_local, width)
     attn = scatter_sum(
         [

time: 380 us -> 179 us (0.47)
  matrix products: 153 us -> 12 us
  local copies, waits for them, and re-layouts: 64.6 us -> 5.92 us
  other arithmetic: 26.5 us -> 5.84 us
  Pallas kernels: 0 us -> 20.5 us
    dot_general x177 -> x0, matrix products: 139 us -> none  [the longest x8 19.1 us: block_step(): recalled = jnp.einsum('cr,hrcv->hcv', member_b, recalled, precision=HIGH)]
    dynamic_slice x32 -> x0, local copies, waits for them, and re-layouts: 26.9 us -> none  [on_device(): states, mixed = lax.scan(block_step, jnp.swapaxes(cache, 0, 1), inputs)]
    squeeze x16 -> x0, local copies, waits for them, and re-layouts: 21.1 us -> none  [on_device(): states, mixed = lax.scan(block_step, jnp.swapaxes(cache, 0, 1), inputs)]
    pallas_call x0 -> x1, Pallas kernels: none -> 20.5 us  [mix(): pl.pallas_call(functools.partial(mix_kernel, heads, requests), grid=(tok_...]
    reshape x5 -> x0, local copies, waits for them, and re-layouts: 6.56 us -> none  [the longest x1 2.34 us: on_device(): value_f = values_in.astype(jnp.float32).reshape(layout)]
    gt x8 -> x0, other arithmetic: 5.54 us -> none  [block_step(): member_b.T[None] > 0.5]
    exp x8 -> x0, other arithmetic: 4.8 us -> none  [block_step(): growth = jnp.exp(running)]
    mul x18 -> x0, other arithmetic: 4.78 us -> none  [the longest x1 1.67 us: on_device(): unit_rows(queries.astype(jnp.float32).reshape(layout)) * head_dim ** (-0.5)]
  transfers between devices with their start and end apart: 27 -> 27, of which waited for: 15 -> 15; matrix products, arithmetic and copies ran while one was open for 5% -> 8% of each run, Pallas kernels for 0% -> 0%
where the time goes in v2:
time: 179 us; the launch traced here: 178 us
  waiting for transfers between devices  97 us (54%)
  starting transfers between devices  36 us (20%)
  Pallas kernels  20.5 us (11%)
  matrix products  12 us (7%)
  local copies, waits for them, and re-layouts  5.92 us (3%)
  other arithmetic  5.84 us (3%)
    ppermute x5, waiting for transfers between devices, gather_parts(): parts.append([lax.ppermute(block, axis, high_pairs(high, low, step))])  33.5 us
    ppermute x8, waiting for transfers between devices, scatter_sum(): lax.ppermute(row[1], axis, low_pairs(high, low)).astype(jnp.float32)  30.5 us
    ppermute x6, waiting for transfers between devices, scatter_sum(): lax.ppermute(sent, axis, reverse(high_pairs(high, low, step)))  27 us
    pallas_call x1, Pallas kernels, mix(): pl.pallas_call(functools.partial(mix_kernel, heads, requests), grid=(tok_...  20.5 us
    ppermute x5, starting transfers between devices, gather_parts(): parts.append([lax.ppermute(block, axis, high_pairs(high, low, step))])  10.9 us
    ppermute x8, starting transfers between devices, scatter_sum(): lax.ppermute(row[1], axis, low_pairs(high, low)).astype(jnp.float32)  9.18 us
    ppermute x6, starting transfers between devices, scatter_sum(): lax.ppermute(sent, axis, reverse(high_pairs(high, low, step)))  9.13 us
    dot_general x4, matrix products, on_device(): both = jnp.dot(rows, matrix, preferred_element_type=jnp.float32)  8.37 us
  transfers between devices with their start and end apart: 27, of which 15 were waited for; matrix products, arithmetic and copies ran while one was open for 8% of the time, Pallas kernels for 0%

profile of v2, /device:TPU:0, one launch (start us, length us, event | category | flops | bytes accessed | tf_op | source)
XLA Modules:
  0.0 178.4 jit_solution(2145803639209032135)
XLA Ops:
  0.7 1.6 copy.23.beta_ref
  2.2 1.5 copy.24.decay_ref
  3.8 20.5 %mix.1 = (bf16[512,2048]{1,0:T(8,128)(2,1)}, f32[4,4,128,128]{3,2,1,0:T(8,128)}) custom-call(bf16[512,512]{1,0:T(8,128)(2,1)} %query_ref.1, bf16[512,512]{1,0:T(8,128)(2,1)} %key_ref.1, bf16[512,512]{1,0:T(8,128)(2,1)} %value_ref.1, bf16[512,512]{1,0:T(8,128)(2,1)} %gate_ref.1, f32[512,4]{1,0:T(8,128)} %copy.23.beta_ref, f32[512,4]{1,0:T(8,128)} %copy.24.decay_ref, ...), custom_call_target="tpu_custom_call" | custom-call | tf_op jit(solution)/shard_map/mix/pallas_call | solution.py:158
  24.3 2.2 %dynamic-slice_bitcast_fusion.3 = (bf16[64,2048]{1,0:T(8,128)(2,1)S(1)}, bf16[64,2048]{1,0:T(8,128)(2,1)S(1)}, bf16[64,2048]{1,0:T(8,128)(2,1)}, bf16[64,2048]{1,0:T(8,128)(2,1)}) fusion(bf16[8,64,2048]{2,1,0:T(8,128)(2,1)} %bitcast.59, s32[]{:T(128)S(6)} %select_n.65, s32[]{:T(128)S(6)} %select_n.71, s32[]{:T(128)S(6)} %select_n.69, s32[]{:T(128)S(6)} %select_n.67), kind=kLoop, calls=%fused_computation.76 | loop fusion | bytes 2097168 | tf_op jit(solution)/shard_map/jit(dynamic_index_in_dim)/squeeze | solution.py:285
  26.5 3.0 %collective-permute-start.1 = (bf16[64,2048]{1,0:T(8,128)(2,1)}, bf16[64,2048]{1,0:T(8,128)(2,1)S(1)}, u32[]{:S(2)}, u32[]{:S(2)}) collective-permute-start(bf16[64,2048]{1,0:T(8,128)(2,1)} %get-tuple-element.25), channel_id=1, source_target_pairs={{0,4},{4,0},{8,12},{12,8},{16,20},{20,16},{24,28},{28,24},{1,5},{5... | collective-permute-start | bytes 786440 | tf_op jit(solution)/shard_map/ppermute | solution.py:227
  29.6 2.0 %collective-permute-start.5 = (bf16[64,2048]{1,0:T(8,128)(2,1)S(1)}, bf16[64,2048]{1,0:T(8,128)(2,1)}, u32[]{:S(2)}, u32[]{:S(2)}) collective-permute-start(bf16[64,2048]{1,0:T(8,128)(2,1)S(1)} %get-tuple-element.23), channel_id=1, source_target_pairs={{0,4},{4,0},{8,12},{12,8},{16,20},{20,16},{24,28},{28,24},{1,5},{5... | collective-permute-start | bytes 786440 | tf_op jit(solution)/shard_map/ppermute | solution.py:227
  31.6 5.2 %collective-permute-done.1 = bf16[64,2048]{1,0:T(8,128)(2,1)S(1)} collective-permute-done((bf16[64,2048]{1,0:T(8,128)(2,1)}, bf16[64,2048]{1,0:T(8,128)(2,1)S(1)}, u32[]{:S(2)}, u32[]{:S(2)}) %collective-permute-start.1) | collective-permute-done | bytes 262176 | tf_op jit(solution)/shard_map/ppermute | solution.py:227
  36.9 5.7 %collective-permute-done.3 = bf16[64,2048]{1,0:T(8,128)(2,1)} collective-permute-done((bf16[64,2048]{1,0:T(8,128)(2,1)}, bf16[64,2048]{1,0:T(8,128)(2,1)}, u32[]{:S(2)}, u32[]{:S(2)}) %collective-permute-start.3) | collective-permute-done | bytes 262176 | tf_op jit(solution)/shard_map/ppermute | solution.py:227
  42.6 5.6 %collective-permute-done.5 = bf16[64,2048]{1,0:T(8,128)(2,1)} collective-permute-done((bf16[64,2048]{1,0:T(8,128)(2,1)S(1)}, bf16[64,2048]{1,0:T(8,128)(2,1)}, u32[]{:S(2)}, u32[]{:S(2)}) %collective-permute-start.5) | collective-permute-done | bytes 262176 | tf_op jit(solution)/shard_map/ppermute | solution.py:227
  48.2 2.1 %fusion.42 = (bf16[64,2048]{1,0:T(8,128)(2,1)}, bf16[64,2048]{1,0:T(8,128)(2,1)S(1)}, bf16[64,2048]{1,0:T(8,128)(2,1)}) fusion(bf16[64,2048]{1,0:T(8,128)(2,1)S(1)} %collective-permute-done.1, bf16[8,64,2048]{2,1,0:T(8,128)(2,1)S(1)} %bitcast.60, s32[]{:T(128)S(6)} %select_n.66, bf16[64,2048]{1,0:T(8,128)(2,1)} %collective-permute-done.5, s32[]{:T(128)S(6)} %select_n.70, ...), kind=kLoop, calls=%fused_computation.53 | loop fusion | flops 1572864 | bytes 2359308 | tf_op jit(solution)/shard_map/convert_element_type | solution.py:231
  50.3 2.1 %collective-permute-start.2 = (bf16[64,2048]{1,0:T(8,128)(2,1)}, bf16[64,2048]{1,0:T(8,128)(2,1)S(1)}, u32[]{:S(2)}, u32[]{:S(2)}) collective-permute-start(bf16[64,2048]{1,0:T(8,128)(2,1)} %get-tuple-element.26), channel_id=1, source_target_pairs={{8,0},{12,4},{0,8},{4,12},{24,16},{28,20},{16,24},{20,28},{9,1},{1... | collective-permute-start | bytes 786440 | tf_op jit(solution)/shard_map/ppermute | solution.py:232
  52.4 2.6 %collective-permute-start.4 = (bf16[64,2048]{1,0:T(8,128)(2,1)}, bf16[64,2048]{1,0:T(8,128)(2,1)}, u32[]{:S(2)}, u32[]{:S(2)}) collective-permute-start(bf16[64,2048]{1,0:T(8,128)(2,1)} %get-tuple-element.28), channel_id=1, source_target_pairs={{16,0},{20,4},{24,8},{28,12},{0,16},{4,20},{8,24},{12,28},{17,1},{... | collective-permute-start | bytes 786440 | tf_op jit(solution)/shard_map/ppermute | solution.py:232
  55.3 1.7 collective-permute-start.15
  57.0 3.9 %collective-permute-done.2 = bf16[64,2048]{1,0:T(8,128)(2,1)S(1)} collective-permute-done((bf16[64,2048]{1,0:T(8,128)(2,1)}, bf16[64,2048]{1,0:T(8,128)(2,1)S(1)}, u32[]{:S(2)}, u32[]{:S(2)}) %collective-permute-start.2) | collective-permute-done | bytes 262176 | tf_op jit(solution)/shard_map/ppermute | solution.py:232
  60.9 1.4 collective-permute-start.18
  62.3 11.2 %collective-permute-done.4 = bf16[64,2048]{1,0:T(8,128)(2,1)} collective-permute-done((bf16[64,2048]{1,0:T(8,128)(2,1)}, bf16[64,2048]{1,0:T(8,128)(2,1)}, u32[]{:S(2)}, u32[]{:S(2)}) %collective-permute-start.4) | collective-permute-done | bytes 262176 | tf_op jit(solution)/shard_map/ppermute | solution.py:232
  73.5 1.4 fusion.26
  75.1 1.6 collective-permute-start.7
  76.7 3.4 %collective-permute-start.8 = (bf16[64,2112]{1,0:T(8,128)(2,1)S(1)}, bf16[64,2112]{1,0:T(8,128)(2,1)S(1)}, u32[]{:S(2)}, u32[]{:S(2)}) collective-permute-start(bf16[64,2112]{1,0:T(8,128)(2,1)S(1)} %concatenate.12), channel_id=1, source_target_pairs={{0,8},{4,12},{8,0},{12,4},{16,24},{20,28},{24,16},{28,20},{1,9},{5... | collective-permute-start | bytes 811016 | tf_op jit(solution)/shard_map/ppermute | solution.py:214
  80.1 1.6 collective-permute-done.7
  81.7 4.4 %collective-permute-start.10 = (bf16[64,2112]{1,0:T(8,128)(2,1)S(1)}, bf16[64,2112]{1,0:T(8,128)(2,1)S(1)}, u32[]{:S(2)}, u32[]{:S(2)}) collective-permute-start(bf16[64,2112]{1,0:T(8,128)(2,1)S(1)} %concatenate.12), channel_id=1, source_target_pairs={{0,16},{4,20},{8,24},{12,28},{16,0},{20,4},{24,8},{28,12},{1,17},{... | collective-permute-start | bytes 811016 | tf_op jit(solution)/shard_map/ppermute | solution.py:214
  86.1 1.6 collective-permute-start.9
  87.7 9.8 %collective-permute-done.10 = bf16[64,2112]{1,0:T(8,128)(2,1)S(1)} collective-permute-done((bf16[64,2112]{1,0:T(8,128)(2,1)S(1)}, bf16[64,2112]{1,0:T(8,128)(2,1)S(1)}, u32[]{:S(2)}, u32[]{:S(2)}) %collective-permute-start.10) | collective-permute-done | bytes 270368 | tf_op jit(solution)/shard_map/ppermute | solution.py:214
  97.5 1.6 collective-permute-start.11
  99.2 6.8 %collective-permute-done.12 = bf16[64,2112]{1,0:T(8,128)(2,1)S(1)} collective-permute-done((bf16[64,2112]{1,0:T(8,128)(2,1)S(1)}, bf16[64,2112]{1,0:T(8,128)(2,1)S(1)}, u32[]{:S(2)}, u32[]{:S(2)}) %collective-permute-start.12) | collective-permute-done | bytes 270368 | tf_op jit(solution)/shard_map/ppermute | solution.py:214
  106.0 16.9 %collective-permute-done.18 = bf16[256,2048]{1,0:T(8,128)(2,1)} collective-permute-done((bf16[256,2048]{1,0:T(8,128)(2,1)}, bf16[256,2048]{1,0:T(8,128)(2,1)}, u32[]{:S(2)}, u32[]{:S(2)}) %collective-permute-start.18) | collective-permute-done | bytes 1048608 | tf_op jit(solution)/shard_map/ppermute | solution.py:214
  122.9 1.5 collective-permute-start.13
  124.5 0.6 collective-permute-start.16
  125.1 4.3 %collective-permute-done.13 = bf16[64,2112]{1,0:T(8,128)(2,1)S(1)} collective-permute-done((bf16[64,2112]{1,0:T(8,128)(2,1)S(1)}, bf16[64,2112]{1,0:T(8,128)(2,1)S(1)}, u32[]{:S(2)}, u32[]{:S(2)}) %collective-permute-start.13) | collective-permute-done | bytes 270368 | tf_op jit(solution)/shard_map/ppermute | solution.py:217
  129.5 0.4 select_reduce_fusion.3
  129.9 1.3 fusion.17
  131.4 2.9 %fusion.13 = f32[512,512]{0,1:T(8,128)S(1)} fusion(bf16[2048,512]{1,0:T(8,128)(2,1)} %collective-permute-done.15, bf16[512,2112]{1,0:T(8,128)(2,1)S(1)} %constant_dynamic-update-slice_fusion), kind=kOutput, calls=%fused_computation.11 | convolution fusion | flops 1073741824 | bytes 5242880 | tf_op jit(solution)/shard_map/dot_general | solution.py:311
  134.3 2.9 %fusion.15 = f32[512,512]{0,1:T(8,128)S(1)} fusion(bf16[2048,512]{1,0:T(8,128)(2,1)} %collective-permute-done.14, bf16[512,2112]{1,0:T(8,128)(2,1)S(1)} %constant_dynamic-update-slice_fusion), kind=kOutput, calls=%fused_computation.13 | convolution fusion | flops 1073741824 | bytes 5242880 | tf_op jit(solution)/shard_map/dot_general | solution.py:311
  137.6 1.3 fusion.11
  139.1 3.6 %fusion.8 = bf16[512,2048]{1,0:T(8,128)(2,1)S(1)} fusion(bf16[256,2048]{1,0:T(8,128)(2,1)S(1)} %collective-permute-done.19, bf16[256,2048]{1,0:T(8,128)(2,1)} %collective-permute-done.18, bf16[256,2048]{1,0:T(8,128)(2,1)S(1)} %collective-permute-done.17, bf16[256,2048]{1,0:T(8,128)(2,1)S(1)} %bitcast.70, bf16[512,256]{0,1:T(8,128)(2,1)S(1)} %fusion.29, ...), kind=kOutput, calls=%fused_computation.8 | convolution fusion | flops 2169503744 | bytes 7340032 | tf_op jit(solution)/shard_map/dot_general | solution.py:317
  142.8 1.6 collective-permute-start.21
  144.4 0.5 collective-permute-start.23
  144.9 1.5 collective-permute-start.25
  146.4 0.5 collective-permute-start.20
  146.9 5.1 %collective-permute-done.21 = bf16[64,2048]{1,0:T(8,128)(2,1)S(1)} collective-permute-done((bf16[64,2048]{1,0:T(8,128)(2,1)S(1)}, bf16[64,2048]{1,0:T(8,128)(2,1)S(1)}, u32[]{:S(2)}, u32[]{:S(2)}) %collective-permute-start.21) | collective-permute-done | bytes 262176 | tf_op jit(solution)/shard_map/ppermute | solution.py:227
  152.0 5.6 %collective-permute-done.23 = bf16[64,2048]{1,0:T(8,128)(2,1)S(1)} collective-permute-done((bf16[64,2048]{1,0:T(8,128)(2,1)S(1)}, bf16[64,2048]{1,0:T(8,128)(2,1)S(1)}, u32[]{:S(2)}, u32[]{:S(2)}) %collective-permute-start.23) | collective-permute-done | bytes 262176 | tf_op jit(solution)/shard_map/ppermute | solution.py:227
  157.6 3.1 %collective-permute-done.25 = bf16[64,2048]{1,0:T(8,128)(2,1)S(1)} collective-permute-done((bf16[64,2048]{1,0:T(8,128)(2,1)S(1)}, bf16[64,2048]{1,0:T(8,128)(2,1)S(1)}, u32[]{:S(2)}, u32[]{:S(2)}) %collective-permute-start.25) | collective-permute-done | bytes 262176 | tf_op jit(solution)/shard_map/ppermute | solution.py:227
  161.0 1.1 collective-permute-start.22
  162.2 3.0 %collective-permute-start.24 = (bf16[64,2048]{1,0:T(8,128)(2,1)S(1)}, bf16[64,2048]{1,0:T(8,128)(2,1)S(1)}, u32[]{:S(2)}, u32[]{:S(2)}) collective-permute-start(bf16[64,2048]{1,0:T(8,128)(2,1)S(1)} %get-tuple-element.21), channel_id=1, source_target_pairs={{16,0},{20,4},{24,8},{28,12},{0,16},{4,20},{8,24},{12,28},{17,1},{... | collective-permute-start | bytes 786440 | tf_op jit(solution)/shard_map/ppermute | solution.py:232
  165.2 0.3 collective-permute-start.26
  165.5 4.7 %collective-permute-done.22 = bf16[64,2048]{1,0:T(8,128)(2,1)S(1)} collective-permute-done((bf16[64,2048]{1,0:T(8,128)(2,1)S(1)}, bf16[64,2048]{1,0:T(8,128)(2,1)S(1)}, u32[]{:S(2)}, u32[]{:S(2)}) %collective-permute-start.22) | collective-permute-done | bytes 262176 | tf_op jit(solution)/shard_map/ppermute | solution.py:232
  170.2 7.3 %collective-permute-done.24 = bf16[64,2048]{1,0:T(8,128)(2,1)S(1)} collective-permute-done((bf16[64,2048]{1,0:T(8,128)(2,1)S(1)}, bf16[64,2048]{1,0:T(8,128)(2,1)S(1)}, u32[]{:S(2)}, u32[]{:S(2)}) %collective-permute-start.24) | collective-permute-done | bytes 262176 | tf_op jit(solution)/shard_map/ppermute | solution.py:232
  177.5 0.9 fusion.39
  (58 shorter events, 1.8 us)
Async XLA Ops:
  3.8 27.8 %copy-start.4 = (f32[64,10]{0,1:T(8,128)S(1)}, f32[64,10]{0,1:T(8,128)}, u32[]{:S(2)}) copy-start(f32[64,10]{0,1:T(8,128)} %param.29) | copy-start | bytes 7684
  3.8 27.8 %copy-start.5 = (s32[64,10]{0,1:T(8,128)S(1)}, s32[64,10]{0,1:T(8,128)}, u32[]{:S(2)}) copy-start(s32[64,10]{0,1:T(8,128)} %param.28) | copy-start | bytes 7684
  24.3 23.9 %copy-start = (bf16[512,2048]{1,0:T(8,128)(2,1)S(1)}, bf16[512,2048]{1,0:T(8,128)(2,1)}, u32[]{:S(2)}) copy-start(bf16[512,2048]{1,0:T(8,128)(2,1)} %get-tuple-element.5) | copy-start | bytes 6291460
  24.3 49.2 %copy-start.2 = (bf16[64,2048]{1,0:T(8,128)(2,1)S(1)}, bf16[64,2048]{1,0:T(8,128)(2,1)}, u32[]{:S(2)}) copy-start(bf16[64,2048]{1,0:T(8,128)(2,1)} %param.26) | copy-start | bytes 786436
  26.5 48.4 %copy-start.3 = (f32[2048]{0:T(1024)S(1)}, f32[2048]{0:T(1024)}, u32[]{:S(2)}) copy-start(f32[2048]{0:T(1024)} %param.27) | copy-start | bytes 24580
  26.5 10.4 %collective-permute-start.1 = (bf16[64,2048]{1,0:T(8,128)(2,1)}, bf16[64,2048]{1,0:T(8,128)(2,1)S(1)}, u32[]{:S(2)}, u32[]{:S(2)}) collective-permute-start(bf16[64,2048]{1,0:T(8,128)(2,1)} %get-tuple-element.25), channel_id=1, source_target_pairs={{0,4},{4,0},{8,12},{12,8},{16,20},{20,16},{24,28},{28,24},{1,5},{5... | collective-permute-start | bytes 786440 | tf_op jit(solution)/shard_map/ppermute | solution.py:227
  29.5 13.1 %collective-permute-start.3 = (bf16[64,2048]{1,0:T(8,128)(2,1)}, bf16[64,2048]{1,0:T(8,128)(2,1)}, u32[]{:S(2)}, u32[]{:S(2)}) collective-permute-start(bf16[64,2048]{1,0:T(8,128)(2,1)} %get-tuple-element.24), channel_id=1, source_target_pairs={{0,4},{4,0},{8,12},{12,8},{16,20},{20,16},{24,28},{28,24},{1,5},{5... | collective-permute-start | bytes 786440 | tf_op jit(solution)/shard_map/ppermute | solution.py:227
  29.6 18.7 %collective-permute-start.5 = (bf16[64,2048]{1,0:T(8,128)(2,1)S(1)}, bf16[64,2048]{1,0:T(8,128)(2,1)}, u32[]{:S(2)}, u32[]{:S(2)}) collective-permute-start(bf16[64,2048]{1,0:T(8,128)(2,1)S(1)} %get-tuple-element.23), channel_id=1, source_target_pairs={{0,4},{4,0},{8,12},{12,8},{16,20},{20,16},{24,28},{28,24},{1,5},{5... | collective-permute-start | bytes 786440 | tf_op jit(solution)/shard_map/ppermute | solution.py:227
  31.5 23.7 %collective-permute-start = (bf16[64,2048]{1,0:T(8,128)(2,1)S(1)}, bf16[64,2048]{1,0:T(8,128)(2,1)S(1)}, u32[]{:S(2)}, u32[]{:S(2)}) collective-permute-start(bf16[64,2048]{1,0:T(8,128)(2,1)S(1)} %get-tuple-element.22), channel_id=1, source_target_pairs={{0,4},{4,0},{8,12},{12,8},{16,20},{20,16},{24,28},{28,24},{1,5},{5... | collective-permute-start | bytes 786440 | tf_op jit(solution)/shard_map/ppermute | solution.py:227
  31.6 102.7 %collective-permute-start.14 = (bf16[2048,512]{1,0:T(8,128)(2,1)}, bf16[2048,512]{1,0:T(8,128)(2,1)}, u32[]{:S(2)}, u32[]{:S(2)}) collective-permute-start(bf16[2048,512]{1,0:T(8,128)(2,1)} %bitcast.66), channel_id=1, source_target_pairs={{0,1},{1,0},{2,3},{3,2},{4,5},{5,4},{6,7},{7,6},{8,9},{9,8},{10,11... | collective-permute-start | bytes 6291464 | tf_op jit(solution)/shard_map/ppermute | solution.py:217
  50.3 10.6 %collective-permute-start.2 = (bf16[64,2048]{1,0:T(8,128)(2,1)}, bf16[64,2048]{1,0:T(8,128)(2,1)S(1)}, u32[]{:S(2)}, u32[]{:S(2)}) collective-permute-start(bf16[64,2048]{1,0:T(8,128)(2,1)} %get-tuple-element.26), channel_id=1, source_target_pairs={{8,0},{12,4},{0,8},{4,12},{24,16},{28,20},{16,24},{20,28},{9,1},{1... | collective-permute-start | bytes 786440 | tf_op jit(solution)/shard_map/ppermute | solution.py:232
  52.4 21.1 %collective-permute-start.4 = (bf16[64,2048]{1,0:T(8,128)(2,1)}, bf16[64,2048]{1,0:T(8,128)(2,1)}, u32[]{:S(2)}, u32[]{:S(2)}) collective-permute-start(bf16[64,2048]{1,0:T(8,128)(2,1)} %get-tuple-element.28), channel_id=1, source_target_pairs={{16,0},{20,4},{24,8},{28,12},{0,16},{4,20},{8,24},{12,28},{17,1},{... | collective-permute-start | bytes 786440 | tf_op jit(solution)/shard_map/ppermute | solution.py:232
  55.0 18.5 %collective-permute-start.6 = (bf16[64,2048]{1,0:T(8,128)(2,1)S(1)}, bf16[64,2048]{1,0:T(8,128)(2,1)}, u32[]{:S(2)}, u32[]{:S(2)}) collective-permute-start(bf16[64,2048]{1,0:T(8,128)(2,1)S(1)} %get-tuple-element.27), channel_id=1, source_target_pairs={{24,0},{28,4},{16,8},{20,12},{8,16},{12,20},{0,24},{4,28},{25,1},{... | collective-permute-start | bytes 786440 | tf_op jit(solution)/shard_map/ppermute | solution.py:232
  55.3 69.3 %collective-permute-start.15 = (bf16[2048,512]{1,0:T(8,128)(2,1)}, bf16[2048,512]{1,0:T(8,128)(2,1)}, u32[]{:S(2)}, u32[]{:S(2)}) collective-permute-start(bf16[2048,512]{1,0:T(8,128)(2,1)} %bitcast.67), channel_id=1, source_target_pairs={{0,2},{1,3},{2,0},{3,1},{4,6},{5,7},{6,4},{7,5},{8,10},{9,11},{10,... | collective-permute-start | bytes 6291464 | tf_op jit(solution)/shard_map/ppermute | solution.py:214
  60.9 62.0 %collective-permute-start.18 = (bf16[256,2048]{1,0:T(8,128)(2,1)}, bf16[256,2048]{1,0:T(8,128)(2,1)}, u32[]{:S(2)}, u32[]{:S(2)}) collective-permute-start(bf16[256,2048]{1,0:T(8,128)(2,1)} %bitcast.68), channel_id=1, source_target_pairs={{0,2},{1,3},{2,0},{3,1},{4,6},{5,7},{6,4},{7,5},{8,10},{9,11},{10,... | collective-permute-start | bytes 3145736 | tf_op jit(solution)/shard_map/ppermute | solution.py:214
  74.8 49.7 %copy-start.1 = (bf16[64,2048]{1,0:T(8,128)(2,1)}, bf16[64,2048]{1,0:T(8,128)(2,1)S(1)}, u32[]{:S(2)}) copy-start(bf16[64,2048]{1,0:T(8,128)(2,1)S(1)} %get-tuple-element.14) | copy-start | bytes 786436
  74.8 31.1 %copy-start.7 = (bf16[1,256,2048]{2,1,0:T(8,128)(2,1)S(1)}, bf16[1,256,2048]{2,1,0:T(8,128)(2,1)}, u32[]{:S(2)}) copy-start(bf16[1,256,2048]{2,1,0:T(8,128)(2,1)} %param.31) | copy-start | bytes 3145732
  75.1 6.6 %collective-permute-start.7 = (bf16[64,2112]{1,0:T(8,128)(2,1)S(1)}, bf16[64,2112]{1,0:T(8,128)(2,1)S(1)}, u32[]{:S(2)}, u32[]{:S(2)}) collective-permute-start(bf16[64,2112]{1,0:T(8,128)(2,1)S(1)} %concatenate.12), channel_id=1, source_target_pairs={{0,4},{4,0},{8,12},{12,8},{16,20},{20,16},{24,28},{28,24},{1,5},{5... | collective-permute-start | bytes 811016 | tf_op jit(solution)/shard_map/ppermute | solution.py:217
  76.7 9.4 %collective-permute-start.8 = (bf16[64,2112]{1,0:T(8,128)(2,1)S(1)}, bf16[64,2112]{1,0:T(8,128)(2,1)S(1)}, u32[]{:S(2)}, u32[]{:S(2)}) collective-permute-start(bf16[64,2112]{1,0:T(8,128)(2,1)S(1)} %concatenate.12), channel_id=1, source_target_pairs={{0,8},{4,12},{8,0},{12,4},{16,24},{20,28},{24,16},{28,20},{1,9},{5... | collective-permute-start | bytes 811016 | tf_op jit(solution)/shard_map/ppermute | solution.py:214
  80.1 49.8 %copy-start.6 = (bf16[1,2048,512]{2,1,0:T(8,128)(2,1)S(1)}, bf16[1,2048,512]{2,1,0:T(8,128)(2,1)}, u32[]{:S(2)}) copy-start(bf16[1,2048,512]{2,1,0:T(8,128)(2,1)} %param.30) | copy-start | bytes 6291460
  81.7 15.8 %collective-permute-start.10 = (bf16[64,2112]{1,0:T(8,128)(2,1)S(1)}, bf16[64,2112]{1,0:T(8,128)(2,1)S(1)}, u32[]{:S(2)}, u32[]{:S(2)}) collective-permute-start(bf16[64,2112]{1,0:T(8,128)(2,1)S(1)} %concatenate.12), channel_id=1, source_target_pairs={{0,16},{4,20},{8,24},{12,28},{16,0},{20,4},{24,8},{28,12},{1,17},{... | collective-permute-start | bytes 811016 | tf_op jit(solution)/shard_map/ppermute | solution.py:214
  86.1 11.4 %collective-permute-start.9 = (bf16[64,2112]{1,0:T(8,128)(2,1)S(1)}, bf16[64,2112]{1,0:T(8,128)(2,1)S(1)}, u32[]{:S(2)}, u32[]{:S(2)}) collective-permute-start(bf16[64,2112]{1,0:T(8,128)(2,1)S(1)} %collective-permute-done.8), channel_id=1, source_target_pairs={{0,4},{4,0},{8,12},{12,8},{16,20},{20,16},{24,28},{28,24},{1,5},{5... | collective-permute-start | bytes 811016 | tf_op jit(solution)/shard_map/ppermute | solution.py:217
  97.5 8.4 %collective-permute-start.12 = (bf16[64,2112]{1,0:T(8,128)(2,1)S(1)}, bf16[64,2112]{1,0:T(8,128)(2,1)S(1)}, u32[]{:S(2)}, u32[]{:S(2)}) collective-permute-start(bf16[64,2112]{1,0:T(8,128)(2,1)S(1)} %concatenate.12), channel_id=1, source_target_pairs={{0,24},{4,28},{8,16},{12,20},{16,8},{20,12},{24,0},{28,4},{1,25},{... | collective-permute-start | bytes 811016 | tf_op jit(solution)/shard_map/ppermute | solution.py:214
  97.5 26.9 %collective-permute-start.11 = (bf16[64,2112]{1,0:T(8,128)(2,1)S(1)}, bf16[64,2112]{1,0:T(8,128)(2,1)S(1)}, u32[]{:S(2)}, u32[]{:S(2)}) collective-permute-start(bf16[64,2112]{1,0:T(8,128)(2,1)S(1)} %collective-permute-done.10), channel_id=1, source_target_pairs={{0,4},{4,0},{8,12},{12,8},{16,20},{20,16},{24,28},{28,24},{1,5},{5... | collective-permute-start | bytes 811016 | tf_op jit(solution)/shard_map/ppermute | solution.py:217
  106.0 33.1 %collective-permute-start.17 = (bf16[256,2048]{1,0:T(8,128)(2,1)S(1)}, bf16[256,2048]{1,0:T(8,128)(2,1)S(1)}, u32[]{:S(2)}, u32[]{:S(2)}) collective-permute-start(bf16[256,2048]{1,0:T(8,128)(2,1)S(1)} %bitcast.69), channel_id=1, source_target_pairs={{0,1},{1,0},{2,3},{3,2},{4,5},{5,4},{6,7},{7,6},{8,9},{9,8},{10,11... | collective-permute-start | bytes 3145736 | tf_op jit(solution)/shard_map/ppermute | solution.py:217
  122.9 6.5 %collective-permute-start.13 = (bf16[64,2112]{1,0:T(8,128)(2,1)S(1)}, bf16[64,2112]{1,0:T(8,128)(2,1)S(1)}, u32[]{:S(2)}, u32[]{:S(2)}) collective-permute-start(bf16[64,2112]{1,0:T(8,128)(2,1)S(1)} %collective-permute-done.12), channel_id=1, source_target_pairs={{0,4},{4,0},{8,12},{12,8},{16,20},{20,16},{24,28},{28,24},{1,5},{5... | collective-permute-start | bytes 811016 | tf_op jit(solution)/shard_map/ppermute | solution.py:217
  124.5 14.6 %collective-permute-start.19 = (bf16[256,2048]{1,0:T(8,128)(2,1)}, bf16[256,2048]{1,0:T(8,128)(2,1)S(1)}, u32[]{:S(2)}, u32[]{:S(2)}) collective-permute-start(bf16[256,2048]{1,0:T(8,128)(2,1)} %collective-permute-done.18), channel_id=1, source_target_pairs={{0,1},{1,0},{2,3},{3,2},{4,5},{5,4},{6,7},{7,6},{8,9},{9,8},{10,11... | collective-permute-start | bytes 3145736 | tf_op jit(solution)/shard_map/ppermute | solution.py:217
  124.5 13.0 %collective-permute-start.16 = (bf16[2048,512]{1,0:T(8,128)(2,1)}, bf16[2048,512]{1,0:T(8,128)(2,1)S(1)}, u32[]{:S(2)}, u32[]{:S(2)}) collective-permute-start(bf16[2048,512]{1,0:T(8,128)(2,1)} %collective-permute-done.15), channel_id=1, source_target_pairs={{0,1},{1,0},{2,3},{3,2},{4,5},{5,4},{6,7},{7,6},{8,9},{9,8},{10,11... | collective-permute-start | bytes 6291464 | tf_op jit(solution)/shard_map/ppermute | solution.py:217
  142.8 9.2 %collective-permute-start.21 = (bf16[64,2048]{1,0:T(8,128)(2,1)S(1)}, bf16[64,2048]{1,0:T(8,128)(2,1)S(1)}, u32[]{:S(2)}, u32[]{:S(2)}) collective-permute-start(bf16[64,2048]{1,0:T(8,128)(2,1)S(1)} %get-tuple-element.18), channel_id=1, source_target_pairs={{0,4},{4,0},{8,12},{12,8},{16,20},{20,16},{24,28},{28,24},{1,5},{5... | collective-permute-start | bytes 786440 | tf_op jit(solution)/shard_map/ppermute | solution.py:227
  144.4 13.3 %collective-permute-start.23 = (bf16[64,2048]{1,0:T(8,128)(2,1)S(1)}, bf16[64,2048]{1,0:T(8,128)(2,1)S(1)}, u32[]{:S(2)}, u32[]{:S(2)}) collective-permute-start(bf16[64,2048]{1,0:T(8,128)(2,1)S(1)} %get-tuple-element.17), channel_id=1, source_target_pairs={{0,4},{4,0},{8,12},{12,8},{16,20},{20,16},{24,28},{28,24},{1,5},{5... | collective-permute-start | bytes 786440 | tf_op jit(solution)/shard_map/ppermute | solution.py:227
  144.9 15.9 %collective-permute-start.25 = (bf16[64,2048]{1,0:T(8,128)(2,1)S(1)}, bf16[64,2048]{1,0:T(8,128)(2,1)S(1)}, u32[]{:S(2)}, u32[]{:S(2)}) collective-permute-start(bf16[64,2048]{1,0:T(8,128)(2,1)S(1)} %get-tuple-element.16), channel_id=1, source_target_pairs={{0,4},{4,0},{8,12},{12,8},{16,20},{20,16},{24,28},{28,24},{1,5},{5... | collective-permute-start | bytes 786440 | tf_op jit(solution)/shard_map/ppermute | solution.py:227
  146.4 19.1 %collective-permute-start.20 = (bf16[64,2048]{1,0:T(8,128)(2,1)S(1)}, bf16[64,2048]{1,0:T(8,128)(2,1)S(1)}, u32[]{:S(2)}, u32[]{:S(2)}) collective-permute-start(bf16[64,2048]{1,0:T(8,128)(2,1)S(1)} %get-tuple-element.15), channel_id=1, source_target_pairs={{0,4},{4,0},{8,12},{12,8},{16,20},{20,16},{24,28},{28,24},{1,5},{5... | collective-permute-start | bytes 786440 | tf_op jit(solution)/shard_map/ppermute | solution.py:227
  161.0 9.2 %collective-permute-start.22 = (bf16[64,2048]{1,0:T(8,128)(2,1)S(1)}, bf16[64,2048]{1,0:T(8,128)(2,1)S(1)}, u32[]{:S(2)}, u32[]{:S(2)}) collective-permute-start(bf16[64,2048]{1,0:T(8,128)(2,1)S(1)} %get-tuple-element.19), channel_id=1, source_target_pairs={{8,0},{12,4},{0,8},{4,12},{24,16},{28,20},{16,24},{20,28},{9,1},{1... | collective-permute-start | bytes 786440 | tf_op jit(solution)/shard_map/ppermute | solution.py:232
  162.2 15.3 %collective-permute-start.24 = (bf16[64,2048]{1,0:T(8,128)(2,1)S(1)}, bf16[64,2048]{1,0:T(8,128)(2,1)S(1)}, u32[]{:S(2)}, u32[]{:S(2)}) collective-permute-start(bf16[64,2048]{1,0:T(8,128)(2,1)S(1)} %get-tuple-element.21), channel_id=1, source_target_pairs={{16,0},{20,4},{24,8},{28,12},{0,16},{4,20},{8,24},{12,28},{17,1},{... | collective-permute-start | bytes 786440 | tf_op jit(solution)/shard_map/ppermute | solution.py:232
  165.2 12.3 %collective-permute-start.26 = (bf16[64,2048]{1,0:T(8,128)(2,1)S(1)}, bf16[64,2048]{1,0:T(8,128)(2,1)S(1)}, u32[]{:S(2)}, u32[]{:S(2)}) collective-permute-start(bf16[64,2048]{1,0:T(8,128)(2,1)S(1)} %get-tuple-element.20), channel_id=1, source_target_pairs={{24,0},{28,4},{16,8},{20,12},{8,16},{12,20},{0,24},{4,28},{25,1},{... | collective-permute-start | bytes 786440 | tf_op jit(solution)/shard_map/ppermute | solution.py:232

commit v3 on v2

--- a/solution.py
+++ b/solution.py
@@ -18,9 +18,16 @@
     return lax.dot_general(left, right, (contract, ((), ())), preferred_element_type=jnp.float32)
 
 
+def exact_product(left, right):
+    return lax.dot_general(
+        left, right, (((1,), (1,)), ((), ())), precision=HIGH, preferred_element_type=jnp.float32
+    )
+
+
 def mix_kernel(
     heads,
     requests,
+    owned,
     query_ref,
     key_ref,
     value_ref,
@@ -61,17 +68,12 @@
     eye = (row_of == col_of).astype(f32)
     decay = decay_ref[...]
     inside_f = inside.astype(f32)
-    running = lax.dot_general(
-        inside_f, decay, (((1,), (0,)), ((), ())), precision=HIGH, preferred_element_type=f32
-    )
-    running_t = lax.dot_general(
-        decay, inside_f, (((0,), (1,)), ((), ())), precision=HIGH, preferred_element_type=f32
-    )
-    left = lax.dot_general(
-        after.astype(f32), decay, (((1,), (0,)), ((), ())), precision=HIGH, preferred_element_type=f32
-    )
+    running = exact_product(inside_f, decay)
+    running_t = exact_product(decay, inside_f)
+    left = exact_product(after.astype(f32), decay)
+    strength = exact_product(eye, beta_ref[...])
     totals = [
-        jnp.exp(jnp.sum(jnp.where(request_col == r, decay, 0.0), axis=0, keepdims=True))
+        jnp.exp(jnp.sum(jnp.where(request_row == r, decay, 0.0), axis=1, keepdims=True))
         for r in range(requests)
     ]
     in_col = [request_col == r for r in range(requests)]
@@ -96,7 +98,7 @@
         query = query * (
             lax.rsqrt(jnp.sum(query * query, axis=-1, keepdims=True) + epsilon) * dim ** (-0.5)
         )
-        beta = beta_ref[:, h : h + 1]
+        beta = strength[:, h : h + 1]
         gaps = running[:, h : h + 1] - running_t[h : h + 1, :]
         decays = jnp.where(inside, jnp.exp(jnp.minimum(gaps, 0.0)), 0.0)
         key_b = key.astype(bf16)
@@ -138,16 +140,21 @@
         key_t = (keys[h] * jnp.exp(left[:, h : h + 1])).T.astype(bf16)
         for r in range(requests):
             fresh = product(jnp.where(in_row[r], key_t, 0), update)
-            states_ref[r, h] = totals[r][:, h : h + 1] * states_ref[r, h] + fresh
+            states_ref[r, h] = totals[r][h : h + 1, :] * states_ref[r, h] + fresh
         scale = lax.rsqrt(jnp.mean(mixed * mixed, axis=-1, keepdims=True) + epsilon)
         gate = gate_ref[:, lanes].astype(f32)
         normed.append(
             (mixed * scale * gain_ref[...] * (gate * jax.nn.sigmoid(gate))).astype(bf16)
         )
-    share_ref[...] = product(jnp.concatenate(normed, axis=1), proj_ref[...]).astype(bf16)
-
-
-def mix(queries, keys_in, values_in, gate_in, beta, decay, lengths, cache, norm_gain, out_proj):
+    share = product(jnp.concatenate(normed, axis=1), proj_ref[...]).astype(bf16)
+    for block in range(rows // owned):
+        slot = part_slot("expert", step * (rows // owned) + block)
+        share_ref[pl.ds(pl.multiple_of(slot * owned, owned), owned), :] = share[
+            block * owned : (block + 1) * owned
+        ]
+
+
+def mix(queries, keys_in, values_in, gate_in, beta, decay, lengths, cache, norm_gain, out_proj, owned):
     tok_count, heads = beta.shape
     requests = lengths.shape[1]
     dim = norm_gain.shape[0]
@@ -156,28 +163,39 @@
     block = lambda cols: pl.BlockSpec((rows, cols), lambda c: (c, 0))
     whole = lambda shape: pl.BlockSpec(shape, lambda c: (0,) * len(shape))
     return pl.pallas_call(
-        functools.partial(mix_kernel, heads, requests),
+        functools.partial(mix_kernel, heads, requests, owned),
         grid=(tok_count // rows,),
         in_specs=[
             block(heads * dim),
             block(heads * dim),
             block(heads * dim),
             block(heads * dim),
-            block(heads),
-            block(heads),
+            pl.BlockSpec((heads, rows), lambda c: (0, c)),
+            pl.BlockSpec((heads, rows), lambda c: (0, c)),
             pl.BlockSpec(memory_space=pltpu.SMEM),
             whole(cache.shape),
             whole((1, dim)),
             whole(out_proj.shape),
         ],
-        out_specs=[block(width), whole(cache.shape)],
+        out_specs=[whole((tok_count, width)), whole(cache.shape)],
         out_shape=[
             jax.ShapeDtypeStruct((tok_count, width), jnp.bfloat16),
             jax.ShapeDtypeStruct(cache.shape, jnp.float32),
         ],
         compiler_params=pltpu.CompilerParams(dimension_semantics=("arbitrary",)),
         name="mix",
-    )(queries, keys_in, values_in, gate_in, beta, decay, lengths, cache, norm_gain[None], out_proj)
+    )(
+        queries,
+        keys_in,
+        values_in,
+        gate_in,
+        beta.T,
+        decay.T,
+        lengths,
+        cache,
+        norm_gain[None],
+        out_proj,
+    )
 
 
 def factors(size):
@@ -220,19 +238,34 @@
 
 def scatter_sum(parts, axis):
     high, low = factors(lax.axis_size(axis))
-    sums = []
-    for row in parts:
-        total = row[0].astype(jnp.float32)
+    order = list(range(high - 1, 0, -1)) + [0]
+    near = {}
+    if low == 2:
+        for step in order:
+            near[step] = lax.ppermute(parts[step][1], axis, low_pairs(high, low))
+    sums, before = {}, None
+    for step in order:
+        total = parts[step][0].astype(jnp.float32)
         if low == 2:
-            total = total + lax.ppermute(row[1], axis, low_pairs(high, low)).astype(jnp.float32)
-        sums.append(total)
-    result = sums[0]
-    for step in range(1, high):
-        sent = sums[step].astype(jnp.bfloat16)
-        result = result + lax.ppermute(
-            sent, axis, reverse(high_pairs(high, low, step))
-        ).astype(jnp.float32)
-    return result
+            other = near[step]
+            if before is not None:
+                other, before = lax.optimization_barrier((other, before))
+            total = total + other.astype(jnp.float32)
+        if step:
+            before = total.astype(jnp.bfloat16)
+            sums[step] = lax.ppermute(before, axis, reverse(high_pairs(high, low, step)))
+    for step in order[:-1]:
+        total = total + sums[step].astype(jnp.float32)
+    return total
+
+
+def part_slot(axis, owner):
+    high, low = factors(lax.axis_size(axis))
+    place = lax.axis_index(axis)
+    h, m = place // low, place % low
+    other, n = owner // low, owner % low
+    step = other ^ h if high & (high - 1) == 0 else (h - other + high) % high
+    return step * low + (m ^ n)
 
 
 def part_sources(axis):
@@ -278,15 +311,11 @@
         cache,
         norm_gain,
         out_proj,
+        tok_local,
     )
-    share = share.reshape(lax.axis_size("expert"), tok_local, width)
-    attn = scatter_sum(
-        [
-            [lax.dynamic_index_in_dim(share, place, 0, keepdims=False) for place in row]
-            for row in part_sources("expert")
-        ],
-        "expert",
-    )
+    high, low = factors(lax.axis_size("expert"))
+    share = share.reshape(high, low, tok_local, width)
+    attn = scatter_sum([[share[step, j] for j in range(low)] for step in range(high)], "expert")
     attn_out = (residual.astype(jnp.float32) + attn).astype(jnp.bfloat16)
     stream = attn_out.astype(jnp.float32)
     routed = (
@@ -298,33 +327,91 @@
     )
     coarse = mixing.astype(jnp.bfloat16)
     fine = (mixing - coarse.astype(jnp.float32)).astype(jnp.bfloat16)
-    gathered = gather_parts(jnp.concatenate([routed, coarse, fine], axis=1), "expert")
-    rows = jnp.concatenate(sum(gathered, []), axis=0)
-    weights = rows[:, width : width + experts_all].astype(jnp.float32) + rows[
-        :, width + experts_all :
-    ].astype(jnp.float32)
-    rows = rows[:, :width]
-    hidden_width = down_proj.shape[1]
-    hidden = []
-    for place, matrix in zip(expert_of, gate_up_parts):
-        weight = jnp.sum(jnp.where(expert_range == place, weights, 0.0), axis=1, keepdims=True)
-        both = jnp.dot(rows, matrix, preferred_element_type=jnp.float32)
-        hidden.append(
-            (weight * jax.nn.silu(both[:, :hidden_width]) * both[:, hidden_width:]).astype(
-                jnp.bfloat16
-            )
-        )
-    result = jnp.dot(
-        jnp.concatenate(hidden, axis=1),
-        jnp.concatenate(down_parts, axis=0),
-        preferred_element_type=jnp.float32,
-    ).astype(jnp.bfloat16)
-    high, low = factors(lax.axis_size("expert"))
-    result = result.reshape(high, low, tok_local, width)
+    pad = jnp.zeros((tok_local, -2 * experts_all % 128), jnp.bfloat16)
+    gathered = gather_parts(jnp.concatenate([routed, coarse, fine, pad], axis=1), "expert")
+    places = jnp.stack(expert_of).astype(jnp.int32)
+    split = max(1, high // 2)
+    results = []
+    for first in range(0, high, split):
+        results += experts(
+            places,
+            sum(gathered[first : first + split], []),
+            gate_up_parts,
+            down_parts,
+            experts_all,
+        )
     moe_out = scatter_sum(
-        [[result[step, j] for j in range(low)] for step in range(high)], "expert"
+        [results[step * low : (step + 1) * low] for step in range(high)], "expert"
     ).astype(jnp.bfloat16)
     return (moe_out, attn_out, new_states)
+
+
+def experts_kernel(blocks, slots, experts_all, places_ref, *refs):
+    row_refs = refs[:blocks]
+    gate_up_refs = refs[blocks : blocks + slots]
+    down_refs = refs[blocks + slots : blocks + 2 * slots]
+    out_refs = refs[blocks + 2 * slots : 2 * blocks + 2 * slots]
+    gate_up_buf, down_buf, hidden_buf, gate_up_sem, down_sem = refs[2 * blocks + 2 * slots :]
+    width, hidden_width = gate_up_buf.shape[1], down_buf.shape[1]
+    loads = [
+        pltpu.make_async_copy(gate_up_refs[i], gate_up_buf.at[i], gate_up_sem.at[i])
+        for i in range(slots)
+    ]
+    loads_down = [
+        pltpu.make_async_copy(down_refs[i], down_buf.at[i], down_sem.at[i]) for i in range(slots)
+    ]
+    for load in loads + loads_down:
+        load.start()
+    rows = jnp.concatenate([ref[:, :width] for ref in row_refs], axis=0)
+    mixing = jnp.concatenate([ref[:, width:] for ref in row_refs], axis=0).astype(jnp.float32)
+    lane = lax.broadcasted_iota(jnp.int32, mixing.shape, 1)
+    for i in range(slots):
+        place = places_ref[i]
+        named = (lane == place) | (lane == place + experts_all)
+        weight = jnp.sum(jnp.where(named, mixing, 0.0), axis=1, keepdims=True)
+        loads[i].wait()
+        both = product(rows, gate_up_buf[i])
+        gate = both[:, :hidden_width]
+        hidden = gate * jax.nn.sigmoid(gate) * both[:, hidden_width:] * weight
+        hidden_buf[:, i * hidden_width : (i + 1) * hidden_width] = hidden.astype(jnp.bfloat16)
+    for load in loads_down:
+        load.wait()
+    size = row_refs[0].shape[0]
+    tile = min(512, width)
+    for start in range(0, width, tile):
+        down = jnp.concatenate([down_buf[i, :, start : start + tile] for i in range(slots)], axis=0)
+        result = product(hidden_buf[...], down).astype(jnp.bfloat16)
+        for n in range(blocks):
+            out_refs[n][:, start : start + tile] = result[n * size : (n + 1) * size]
+
+
+def experts(places, row_blocks, gate_up_parts, down_parts, experts_all):
+    blocks, slots = len(row_blocks), len(gate_up_parts)
+    size = row_blocks[0].shape[0]
+    width, hidden_twice = gate_up_parts[0].shape
+    hidden_width = down_parts[0].shape[0]
+    vmem = pl.BlockSpec(memory_space=pltpu.VMEM)
+    return pl.pallas_call(
+        functools.partial(experts_kernel, blocks, slots, experts_all),
+        in_specs=[pl.BlockSpec(memory_space=pltpu.SMEM)]
+        + [vmem] * blocks
+        + [pl.BlockSpec(memory_space=pl.ANY)] * (2 * slots),
+        out_specs=[vmem] * blocks,
+        out_shape=[jax.ShapeDtypeStruct((size, width), jnp.bfloat16)] * blocks,
+        scratch_shapes=[
+            pltpu.VMEM((slots, width, hidden_twice), jnp.bfloat16),
+            pltpu.VMEM((slots, hidden_width, width), jnp.bfloat16),
+            pltpu.VMEM((blocks * size, slots * hidden_width), jnp.bfloat16),
+            pltpu.SemaphoreType.DMA((slots,)),
+            pltpu.SemaphoreType.DMA((slots,)),
+        ],
+        cost_estimate=pl.CostEstimate(
+            flops=2 * blocks * size * slots * width * (hidden_twice + hidden_width),
+            bytes_accessed=2 * slots * width * (hidden_twice + hidden_width),
+            transcendentals=0,
+        ),
+        name="experts",
+    )(places, *row_blocks, *gate_up_parts, *down_parts)
 
 
 def solution(mesh):

time: 179 us -> 176 us (0.983)
  Pallas kernels: 20.5 us -> 38.2 us
  waiting for transfers between devices: 97 us -> 84.6 us
  matrix products: 12 us -> 0 us
  other arithmetic: 5.84 us -> 9.64 us
    pallas_call x1 -> x3, Pallas kernels: 20.5 us -> 38.2 us  [the longest x1 21 us: mix(): pl.pallas_call(functools.partial(mix_kernel, heads, requests, owned), gri...]
    dot_general x5 -> x0, matrix products: 12 us -> none  [the longest x4 8.37 us: on_device(): both = jnp.dot(rows, matrix, preferred_element_type=jnp.float32)]
    ppermute x14, waiting for transfers between devices: 57.5 us -> 48.4 us  [the longest x6 30.4 us: scatter_sum(): lax.ppermute(before, axis, reverse(high_pairs(high, low, step)))]
    ppermute x5, waiting for transfers between devices: 33.5 us -> 24.8 us  [gather_parts(): parts.append([lax.ppermute(block, axis, high_pairs(high, low, step))])]
    ppermute x8, waiting for transfers between devices: 5.99 us -> 11.4 us  [gather_parts(): row.append(lax.ppermute(row[0], axis, low_pairs(high, low)))]
    convert_element_type x7 -> x8, other arithmetic: 3.85 us -> 6.48 us  [the longest x6 5.6 us: scatter_sum(): before = total.astype(jnp.bfloat16)]
    ppermute x5, starting transfers between devices: 10.9 us -> 13.2 us  [gather_parts(): parts.append([lax.ppermute(block, axis, high_pairs(high, low, step))])]
    unnamed x25 -> x28, local copies, waits for them, and re-layouts: 3.32 us -> 1.48 us
  transfers between devices with their start and end apart: 27 -> 27, of which waited for: 15 -> 14; matrix products, arithmetic and copies ran while one was open for 8% -> 7% of each run, Pallas kernels for 0% -> 22%
where the time goes in v3:
time: 176 us; the launch traced here: 174 us
  waiting for transfers between devices  84.6 us (48%)
  Pallas kernels  38.2 us (22%)
  starting transfers between devices  36 us (20%)
  other arithmetic  9.64 us (5%)
  local copies, waits for them, and re-layouts  4.86 us (3%)
    ppermute x6, waiting for transfers between devices, scatter_sum(): lax.ppermute(before, axis, reverse(high_pairs(high, low, step)))  30.4 us
    ppermute x5, waiting for transfers between devices, gather_parts(): parts.append([lax.ppermute(block, axis, high_pairs(high, low, step))])  24.8 us
    pallas_call x1, Pallas kernels, mix(): pl.pallas_call(functools.partial(mix_kernel, heads, requests, owned), gri...  21 us
    ppermute x8, waiting for transfers between devices, scatter_sum(): near[step] = lax.ppermute(parts[step][1], axis, low_pairs(high, low))  18 us
    pallas_call x2, Pallas kernels, experts(): pl.pallas_call(functools.partial(experts_kernel, blocks, slots, experts_a...  17.1 us
    ppermute x5, starting transfers between devices, gather_parts(): parts.append([lax.ppermute(block, axis, high_pairs(high, low, step))])  13.2 us
    ppermute x8, waiting for transfers between devices, gather_parts(): row.append(lax.ppermute(row[0], axis, low_pairs(high, low)))  11.4 us
    ppermute x6, starting transfers between devices, scatter_sum(): lax.ppermute(before, axis, reverse(high_pairs(high, low, step)))  9.17 us
  transfers between devices with their start and end apart: 27, of which 14 were waited for; matrix products, arithmetic and copies ran while one was open for 7% of the time, Pallas kernels for 22%

profile of v3, /device:TPU:0, one launch (start us, length us, event | category | flops | bytes accessed | tf_op | source)
XLA Modules:
  0.0 174.1 jit_solution(7761852171928166654)
XLA Ops:
  0.6 3.0 %collective-permute-start.11 = (bf16[2048,512]{1,0:T(8,128)(2,1)}, bf16[2048,512]{1,0:T(8,128)(2,1)}, u32[]{:S(2)}, u32[]{:S(2)}) collective-permute-start(bf16[2048,512]{1,0:T(8,128)(2,1)} %bitcast.39), channel_id=1, source_target_pairs={{0,2},{1,3},{2,0},{3,1},{4,6},{5,7},{6,4},{7,5},{8,10},{9,11},{10,... | collective-permute-start | bytes 6291464 | tf_op jit(solution)/shard_map/ppermute | solution.py:232
  3.7 21.0 %mix.1 = (bf16[512,2048]{1,0:T(8,128)(2,1)}, f32[4,4,128,128]{3,2,1,0:T(8,128)}) custom-call(bf16[512,512]{1,0:T(8,128)(2,1)} %query_ref.1, bf16[512,512]{1,0:T(8,128)(2,1)} %key_ref.1, bf16[512,512]{1,0:T(8,128)(2,1)} %value_ref.1, bf16[512,512]{1,0:T(8,128)(2,1)} %gate_ref.1, f32[4,512]{1,0:T(4,128)} %bitcast.52, f32[4,512]{1,0:T(4,128)} %bitcast.53, ...), custom_call_target="tpu_custom_call" | custom-call | tf_op jit(solution)/shard_map/mix/pallas_call | solution.py:165
  24.8 2.2 %slice_bitcast_fusion.6 = (bf16[64,2048]{1,0:T(8,128)(2,1)}, bf16[64,2048]{1,0:T(8,128)(2,1)S(1)}, bf16[64,2048]{1,0:T(8,128)(2,1)S(1)}, bf16[64,2048]{1,0:T(8,128)(2,1)S(1)}) fusion(bf16[4,2,64,2048]{3,2,1,0:T(8,128)(2,1)} %bitcast.47), kind=kLoop, calls=%fused_computation.27 | loop fusion | bytes 2097152 | tf_op jit(solution)/shard_map/squeeze | solution.py:318
  26.9 1.5 collective-permute-start.3
  28.9 1.5 collective-permute-start.1
  31.0 5.1 %collective-permute-done.3 = bf16[64,2048]{1,0:T(8,128)(2,1)S(1)} collective-permute-done((bf16[64,2048]{1,0:T(8,128)(2,1)S(1)}, bf16[64,2048]{1,0:T(8,128)(2,1)S(1)}, u32[]{:S(2)}, u32[]{:S(2)}) %collective-permute-start.3) | collective-permute-done | bytes 262176 | tf_op jit(solution)/shard_map/ppermute | solution.py:245
  36.1 1.0 fusion.3
  37.1 4.6 %collective-permute-done.2 = bf16[64,2048]{1,0:T(8,128)(2,1)S(1)} collective-permute-done((bf16[64,2048]{1,0:T(8,128)(2,1)S(1)}, bf16[64,2048]{1,0:T(8,128)(2,1)S(1)}, u32[]{:S(2)}, u32[]{:S(2)}) %collective-permute-start.2) | collective-permute-done | bytes 262176 | tf_op jit(solution)/shard_map/ppermute | solution.py:245
  41.7 1.7 fusion.4
  43.4 3.9 %collective-permute-done.1 = bf16[64,2048]{1,0:T(8,128)(2,1)S(1)} collective-permute-done((bf16[64,2048]{1,0:T(8,128)(2,1)S(1)}, bf16[64,2048]{1,0:T(8,128)(2,1)S(1)}, u32[]{:S(2)}, u32[]{:S(2)}) %collective-permute-start.1) | collective-permute-done | bytes 262176 | tf_op jit(solution)/shard_map/ppermute | solution.py:245
  47.3 1.7 fusion.5
  49.0 1.6 collective-permute-start.6
  50.6 2.6 %collective-permute-start.5 = (bf16[64,2048]{1,0:T(8,128)(2,1)}, bf16[64,2048]{1,0:T(8,128)(2,1)}, u32[]{:S(2)}, u32[]{:S(2)}) collective-permute-start(bf16[64,2048]{1,0:T(8,128)(2,1)} %fusion.4), channel_id=1, source_target_pairs={{16,0},{20,4},{24,8},{28,12},{0,16},{4,20},{8,24},{12,28},{17,1},{... | collective-permute-start | bytes 786440 | tf_op jit(solution)/shard_map/ppermute | solution.py:256
  53.8 4.8 %collective-permute-done.6 = bf16[64,2048]{1,0:T(8,128)(2,1)} collective-permute-done((bf16[64,2048]{1,0:T(8,128)(2,1)}, bf16[64,2048]{1,0:T(8,128)(2,1)}, u32[]{:S(2)}, u32[]{:S(2)}) %collective-permute-start.6) | collective-permute-done | bytes 262176 | tf_op jit(solution)/shard_map/ppermute | solution.py:256
  58.6 0.6 collective-permute-start.14
  59.2 12.0 %collective-permute-done.5 = bf16[64,2048]{1,0:T(8,128)(2,1)} collective-permute-done((bf16[64,2048]{1,0:T(8,128)(2,1)}, bf16[64,2048]{1,0:T(8,128)(2,1)}, u32[]{:S(2)}, u32[]{:S(2)}) %collective-permute-start.5) | collective-permute-done | bytes 262176 | tf_op jit(solution)/shard_map/ppermute | solution.py:256
  71.2 1.7 fusion
  73.0 0.8 fusion.2
  73.8 1.0 concatenate.3.refs_0_
  74.9 4.4 %collective-permute-start.18 = (bf16[64,2176]{1,0:T(8,128)(2,1)S(1)}, bf16[64,2176]{1,0:T(8,128)(2,1)}, u32[]{:S(2)}, u32[]{:S(2)}) collective-permute-start(bf16[64,2176]{1,0:T(8,128)(2,1)S(1)} %concatenate.3.refs_0_), channel_id=1, source_target_pairs={{0,16},{4,20},{8,24},{12,28},{16,0},{20,4},{24,8},{28,12},{1,17},{... | collective-permute-start | bytes 835592 | tf_op jit(solution)/shard_map/ppermute | solution.py:232
  79.3 1.5 collective-permute-done.14.refs_10_
  80.8 9.8 %collective-permute-done.18.refs_0_ = bf16[64,2176]{1,0:T(8,128)(2,1)} collective-permute-done((bf16[64,2176]{1,0:T(8,128)(2,1)S(1)}, bf16[64,2176]{1,0:T(8,128)(2,1)}, u32[]{:S(2)}, u32[]{:S(2)}) %collective-permute-start.18) | collective-permute-done | bytes 278560 | tf_op jit(solution)/shard_map/ppermute | solution.py:232
  90.6 2.3 %collective-permute-start.20 = (bf16[64,2176]{1,0:T(8,128)(2,1)S(1)}, bf16[64,2176]{1,0:T(8,128)(2,1)}, u32[]{:S(2)}, u32[]{:S(2)}) collective-permute-start(bf16[64,2176]{1,0:T(8,128)(2,1)S(1)} %concatenate.3.refs_0_), channel_id=1, source_target_pairs={{0,24},{4,28},{8,16},{12,20},{16,8},{20,12},{24,0},{28,4},{1,25},{... | collective-permute-start | bytes 835592 | tf_op jit(solution)/shard_map/ppermute | solution.py:232
  92.9 8.3 %collective-permute-done.20.refs_2_ = bf16[64,2176]{1,0:T(8,128)(2,1)} collective-permute-done((bf16[64,2176]{1,0:T(8,128)(2,1)S(1)}, bf16[64,2176]{1,0:T(8,128)(2,1)}, u32[]{:S(2)}, u32[]{:S(2)}) %collective-permute-start.20) | collective-permute-done | bytes 278560 | tf_op jit(solution)/shard_map/ppermute | solution.py:232
  101.2 2.8 %collective-permute-start.8 = (bf16[64,2176]{1,0:T(8,128)(2,1)S(1)}, bf16[64,2176]{1,0:T(8,128)(2,1)S(1)}, u32[]{:S(2)}, u32[]{:S(2)}) collective-permute-start(bf16[64,2176]{1,0:T(8,128)(2,1)S(1)} %concatenate.3.refs_0_), channel_id=1, source_target_pairs={{0,8},{4,12},{8,0},{12,4},{16,24},{20,28},{24,16},{28,20},{1,9},{5... | collective-permute-start | bytes 835592 | tf_op jit(solution)/shard_map/ppermute | solution.py:232
  103.9 5.3 %collective-permute-done.8.refs_2_ = bf16[64,2176]{1,0:T(8,128)(2,1)S(1)} collective-permute-done((bf16[64,2176]{1,0:T(8,128)(2,1)S(1)}, bf16[64,2176]{1,0:T(8,128)(2,1)S(1)}, u32[]{:S(2)}, u32[]{:S(2)}) %collective-permute-start.8) | collective-permute-done | bytes 278560 | tf_op jit(solution)/shard_map/ppermute | solution.py:232
  109.2 1.5 collective-permute-start.19
  110.7 0.7 collective-permute-start.21
  112.1 7.0 %collective-permute-done.19.refs_1_ = bf16[64,2176]{1,0:T(8,128)(2,1)} collective-permute-done((bf16[64,2176]{1,0:T(8,128)(2,1)}, bf16[64,2176]{1,0:T(8,128)(2,1)}, u32[]{:S(2)}, u32[]{:S(2)}) %collective-permute-start.19) | collective-permute-done | bytes 278560 | tf_op jit(solution)/shard_map/ppermute | solution.py:235
  119.1 1.5 collective-permute-start.7
  120.6 4.3 %collective-permute-done.21.refs_3_ = bf16[64,2176]{1,0:T(8,128)(2,1)S(1)} collective-permute-done((bf16[64,2176]{1,0:T(8,128)(2,1)}, bf16[64,2176]{1,0:T(8,128)(2,1)S(1)}, u32[]{:S(2)}, u32[]{:S(2)}) %collective-permute-start.21) | collective-permute-done | bytes 278560 | tf_op jit(solution)/shard_map/ppermute | solution.py:235
  124.9 1.5 collective-permute-start.9
  126.5 8.6 %experts.3 = (bf16[64,2048]{1,0:T(8,128)(2,1)}, bf16[64,2048]{1,0:T(8,128)(2,1)}, bf16[64,2048]{1,0:T(8,128)(2,1)}, bf16[64,2048]{1,0:T(8,128)(2,1)}) custom-call(s32[4]{0:T(128)} %pad_add_fusion.places_ref, bf16[64,2176]{1,0:T(8,128)(2,1)} %collective-permute-done.18.refs_0_, bf16[64,2176]{1,0:T(8,128)(2,1)} %collective-permute-done.19.refs_1_, ...), custom_call_target="tpu_custom_call" | custom-call | flops 3221225472 | bytes 12582912 | tf_op jit(solution)/shard_map/experts/pallas_call | solution.py:394
  135.1 0.7 collective-permute-start.23
  135.8 1.3 collective-permute-start.22
  137.2 0.7 copy-done.6
  137.9 0.7 copy-done.7
  138.6 8.5 %experts.2 = (bf16[64,2048]{1,0:T(8,128)(2,1)}, bf16[64,2048]{1,0:T(8,128)(2,1)}, bf16[64,2048]{1,0:T(8,128)(2,1)}, bf16[64,2048]{1,0:T(8,128)(2,1)}) custom-call(s32[4]{0:T(128)} %pad_add_fusion.places_ref, bf16[64,2176]{1,0:T(8,128)(2,1)} %copy-done.2, bf16[64,2176]{1,0:T(8,128)(2,1)} %copy-done.6, bf16[64,2176]{1,0:T(8,128)(2,1)} %copy-done.4, ...), custom_call_target="tpu_custom_call" | custom-call | flops 3221225472 | bytes 12582912 | tf_op jit(solution)/shard_map/experts/pallas_call | solution.py:394
  147.1 0.7 collective-permute-start.17
  147.9 1.3 collective-permute-start.16
  149.4 4.4 %collective-permute-done.17 = bf16[64,2048]{1,0:T(8,128)(2,1)S(1)} collective-permute-done((bf16[64,2048]{1,0:T(8,128)(2,1)}, bf16[64,2048]{1,0:T(8,128)(2,1)S(1)}, u32[]{:S(2)}, u32[]{:S(2)}) %collective-permute-start.17) | collective-permute-done | bytes 262176 | tf_op jit(solution)/shard_map/ppermute | solution.py:245
  153.8 1.0 add_convert_fusion.1
  154.8 1.8 %collective-permute-start.26 = (bf16[64,2048]{1,0:T(8,128)(2,1)S(1)}, bf16[64,2048]{1,0:T(8,128)(2,1)S(1)}, u32[]{:S(2)}, u32[]{:S(2)}) collective-permute-start(bf16[64,2048]{1,0:T(8,128)(2,1)S(1)} %add_convert_fusion.1), channel_id=1, source_target_pairs={{8,0},{12,4},{0,8},{4,12},{24,16},{28,20},{16,24},{20,28},{9,1},{1... | collective-permute-start | bytes 786440 | tf_op jit(solution)/shard_map/ppermute | solution.py:256
  156.6 2.1 %collective-permute-start.25 = (bf16[64,2048]{1,0:T(8,128)(2,1)S(1)}, bf16[64,2048]{1,0:T(8,128)(2,1)S(1)}, u32[]{:S(2)}, u32[]{:S(2)}) collective-permute-start(bf16[64,2048]{1,0:T(8,128)(2,1)S(1)} %add_convert_fusion.2), channel_id=1, source_target_pairs={{16,0},{20,4},{24,8},{28,12},{0,16},{4,20},{8,24},{12,28},{17,1},{... | collective-permute-start | bytes 786440 | tf_op jit(solution)/shard_map/ppermute | solution.py:256
  158.7 0.9 collective-permute-start.24
  159.6 5.6 %collective-permute-done.26 = bf16[64,2048]{1,0:T(8,128)(2,1)S(1)} collective-permute-done((bf16[64,2048]{1,0:T(8,128)(2,1)S(1)}, bf16[64,2048]{1,0:T(8,128)(2,1)S(1)}, u32[]{:S(2)}, u32[]{:S(2)}) %collective-permute-start.26) | collective-permute-done | bytes 262176 | tf_op jit(solution)/shard_map/ppermute | solution.py:256
  165.2 8.0 %collective-permute-done.25 = bf16[64,2048]{1,0:T(8,128)(2,1)S(1)} collective-permute-done((bf16[64,2048]{1,0:T(8,128)(2,1)S(1)}, bf16[64,2048]{1,0:T(8,128)(2,1)S(1)}, u32[]{:S(2)}, u32[]{:S(2)}) %collective-permute-start.25) | collective-permute-done | bytes 262176 | tf_op jit(solution)/shard_map/ppermute | solution.py:256
  173.2 0.9 add_convert_fusion
  (56 shorter events, 2.4 us)
Async XLA Ops:
  0.6 58.6 %collective-permute-start.11 = (bf16[2048,512]{1,0:T(8,128)(2,1)}, bf16[2048,512]{1,0:T(8,128)(2,1)}, u32[]{:S(2)}, u32[]{:S(2)}) collective-permute-start(bf16[2048,512]{1,0:T(8,128)(2,1)} %bitcast.39), channel_id=1, source_target_pairs={{0,2},{1,3},{2,0},{3,1},{4,6},{5,7},{6,4},{7,5},{8,10},{9,11},{10,... | collective-permute-start | bytes 6291464 | tf_op jit(solution)/shard_map/ppermute | solution.py:232
  24.7 28.7 %copy-start.12 = (f32[64,10]{0,1:T(8,128)S(1)}, f32[64,10]{0,1:T(8,128)}, u32[]{:S(2)}) copy-start(f32[64,10]{0,1:T(8,128)} %param.29) | copy-start | bytes 7684
  24.7 28.7 %copy-start.13 = (s32[64,10]{0,1:T(8,128)S(1)}, s32[64,10]{0,1:T(8,128)}, u32[]{:S(2)}) copy-start(s32[64,10]{0,1:T(8,128)} %param.28) | copy-start | bytes 7684
  24.7 28.9 %copy-start = (bf16[1,2048,512]{2,1,0:T(8,128)(2,1)S(1)}, bf16[1,2048,512]{2,1,0:T(8,128)(2,1)}, u32[]{:S(2)}) copy-start(bf16[1,2048,512]{2,1,0:T(8,128)(2,1)} %param.30) | copy-start | bytes 6291460
  24.7 33.8 %copy-start.1 = (bf16[1,256,2048]{2,1,0:T(8,128)(2,1)S(1)}, bf16[1,256,2048]{2,1,0:T(8,128)(2,1)}, u32[]{:S(2)}) copy-start(bf16[1,256,2048]{2,1,0:T(8,128)(2,1)} %param.31) | copy-start | bytes 3145732
  26.9 9.2 %collective-permute-start.3 = (bf16[64,2048]{1,0:T(8,128)(2,1)S(1)}, bf16[64,2048]{1,0:T(8,128)(2,1)S(1)}, u32[]{:S(2)}, u32[]{:S(2)}) collective-permute-start(bf16[64,2048]{1,0:T(8,128)(2,1)S(1)} %get-tuple-element.38), channel_id=1, source_target_pairs={{0,4},{4,0},{8,12},{12,8},{16,20},{20,16},{24,28},{28,24},{1,5},{5... | collective-permute-start | bytes 786440 | tf_op jit(solution)/shard_map/ppermute | solution.py:245
  28.4 13.3 %collective-permute-start.2 = (bf16[64,2048]{1,0:T(8,128)(2,1)S(1)}, bf16[64,2048]{1,0:T(8,128)(2,1)S(1)}, u32[]{:S(2)}, u32[]{:S(2)}) collective-permute-start(bf16[64,2048]{1,0:T(8,128)(2,1)S(1)} %get-tuple-element.39), channel_id=1, source_target_pairs={{0,4},{4,0},{8,12},{12,8},{16,20},{20,16},{24,28},{28,24},{1,5},{5... | collective-permute-start | bytes 786440 | tf_op jit(solution)/shard_map/ppermute | solution.py:245
  28.9 18.4 %collective-permute-start.1 = (bf16[64,2048]{1,0:T(8,128)(2,1)S(1)}, bf16[64,2048]{1,0:T(8,128)(2,1)S(1)}, u32[]{:S(2)}, u32[]{:S(2)}) collective-permute-start(bf16[64,2048]{1,0:T(8,128)(2,1)S(1)} %get-tuple-element.40), channel_id=1, source_target_pairs={{0,4},{4,0},{8,12},{12,8},{16,20},{20,16},{24,28},{28,24},{1,5},{5... | collective-permute-start | bytes 786440 | tf_op jit(solution)/shard_map/ppermute | solution.py:245
  30.5 42.5 %copy-start.11 = (f32[2048]{0:T(1024)S(1)}, f32[2048]{0:T(1024)}, u32[]{:S(2)}) copy-start(f32[2048]{0:T(1024)} %param.27) | copy-start | bytes 24580
  30.5 23.2 %collective-permute-start = (bf16[64,2048]{1,0:T(8,128)(2,1)}, bf16[64,2048]{1,0:T(8,128)(2,1)}, u32[]{:S(2)}, u32[]{:S(2)}) collective-permute-start(bf16[64,2048]{1,0:T(8,128)(2,1)} %get-tuple-element.37), channel_id=1, source_target_pairs={{0,4},{4,0},{8,12},{12,8},{16,20},{20,16},{24,28},{28,24},{1,5},{5... | collective-permute-start | bytes 786440 | tf_op jit(solution)/shard_map/ppermute | solution.py:245
  49.0 9.5 %collective-permute-start.6 = (bf16[64,2048]{1,0:T(8,128)(2,1)}, bf16[64,2048]{1,0:T(8,128)(2,1)}, u32[]{:S(2)}, u32[]{:S(2)}) collective-permute-start(bf16[64,2048]{1,0:T(8,128)(2,1)} %fusion.5), channel_id=1, source_target_pairs={{8,0},{12,4},{0,8},{4,12},{24,16},{28,20},{16,24},{20,28},{9,1},{1... | collective-permute-start | bytes 786440 | tf_op jit(solution)/shard_map/ppermute | solution.py:256
  50.6 20.6 %collective-permute-start.5 = (bf16[64,2048]{1,0:T(8,128)(2,1)}, bf16[64,2048]{1,0:T(8,128)(2,1)}, u32[]{:S(2)}, u32[]{:S(2)}) collective-permute-start(bf16[64,2048]{1,0:T(8,128)(2,1)} %fusion.4), channel_id=1, source_target_pairs={{16,0},{20,4},{24,8},{28,12},{0,16},{4,20},{8,24},{12,28},{17,1},{... | collective-permute-start | bytes 786440 | tf_op jit(solution)/shard_map/ppermute | solution.py:256
  53.2 18.0 %collective-permute-start.4 = (bf16[64,2048]{1,0:T(8,128)(2,1)S(1)}, bf16[64,2048]{1,0:T(8,128)(2,1)}, u32[]{:S(2)}, u32[]{:S(2)}) collective-permute-start(bf16[64,2048]{1,0:T(8,128)(2,1)S(1)} %fusion.3), channel_id=1, source_target_pairs={{24,0},{28,4},{16,8},{20,12},{8,16},{12,20},{0,24},{4,28},{25,1},{... | collective-permute-start | bytes 786440 | tf_op jit(solution)/shard_map/ppermute | solution.py:256
  53.7 72.8 %collective-permute-start.10 = (bf16[2048,512]{1,0:T(8,128)(2,1)S(1)}, bf16[2048,512]{1,0:T(8,128)(2,1)}, u32[]{:S(2)}, u32[]{:S(2)}) collective-permute-start(bf16[2048,512]{1,0:T(8,128)(2,1)S(1)} %bitcast.42), channel_id=1, source_target_pairs={{0,1},{1,0},{2,3},{3,2},{4,5},{5,4},{6,7},{7,6},{8,9},{9,8},{10,11... | collective-permute-start | bytes 6291464 | tf_op jit(solution)/shard_map/ppermute | solution.py:235
  58.6 22.2 %collective-permute-start.14 = (bf16[256,2048]{1,0:T(8,128)(2,1)S(1)}, bf16[256,2048]{1,0:T(8,128)(2,1)}, u32[]{:S(2)}, u32[]{:S(2)}) collective-permute-start(bf16[256,2048]{1,0:T(8,128)(2,1)S(1)} %bitcast.45), channel_id=1, source_target_pairs={{0,2},{1,3},{2,0},{3,1},{4,6},{5,7},{6,4},{7,5},{8,10},{9,11},{10,... | collective-permute-start | bytes 3145736 | tf_op jit(solution)/shard_map/ppermute | solution.py:232
  59.2 67.3 %collective-permute-start.12 = (bf16[2048,512]{1,0:T(8,128)(2,1)}, bf16[2048,512]{1,0:T(8,128)(2,1)}, u32[]{:S(2)}, u32[]{:S(2)}) collective-permute-start(bf16[2048,512]{1,0:T(8,128)(2,1)} %collective-permute-done.11.refs_6_), channel_id=1, source_target_pairs={{0,1},{1,0},{2,3},{3,2},{4,5},{5,4},{6,7},{7,6},{8,9},{9,8},{10,11... | collective-permute-start | bytes 6291464 | tf_op jit(solution)/shard_map/ppermute | solution.py:235
  71.2 39.5 %collective-permute-start.13 = (bf16[256,2048]{1,0:T(8,128)(2,1)S(1)}, bf16[256,2048]{1,0:T(8,128)(2,1)}, u32[]{:S(2)}, u32[]{:S(2)}) collective-permute-start(bf16[256,2048]{1,0:T(8,128)(2,1)S(1)} %bitcast.46), channel_id=1, source_target_pairs={{0,1},{1,0},{2,3},{3,2},{4,5},{5,4},{6,7},{7,6},{8,9},{9,8},{10,11... | collective-permute-start | bytes 3145736 | tf_op jit(solution)/shard_map/ppermute | solution.py:235
  72.9 0.9 copy-start.3
  74.9 60.2 %copy-start.2 = (bf16[64,2176]{1,0:T(8,128)(2,1)}, bf16[64,2176]{1,0:T(8,128)(2,1)S(1)}, u32[]{:S(2)}) copy-start(bf16[64,2176]{1,0:T(8,128)(2,1)S(1)} %concatenate.3.refs_0_) | copy-start | bytes 835588
  74.9 15.7 %collective-permute-start.18 = (bf16[64,2176]{1,0:T(8,128)(2,1)S(1)}, bf16[64,2176]{1,0:T(8,128)(2,1)}, u32[]{:S(2)}, u32[]{:S(2)}) collective-permute-start(bf16[64,2176]{1,0:T(8,128)(2,1)S(1)} %concatenate.3.refs_0_), channel_id=1, source_target_pairs={{0,16},{4,20},{8,24},{12,28},{16,0},{20,4},{24,8},{28,12},{1,17},{... | collective-permute-start | bytes 835592 | tf_op jit(solution)/shard_map/ppermute | solution.py:232
  80.8 45.7 %collective-permute-start.15 = (bf16[256,2048]{1,0:T(8,128)(2,1)}, bf16[256,2048]{1,0:T(8,128)(2,1)}, u32[]{:S(2)}, u32[]{:S(2)}) collective-permute-start(bf16[256,2048]{1,0:T(8,128)(2,1)} %collective-permute-done.14.refs_10_), channel_id=1, source_target_pairs={{0,1},{1,0},{2,3},{3,2},{4,5},{5,4},{6,7},{7,6},{8,9},{9,8},{10,11... | collective-permute-start | bytes 3145736 | tf_op jit(solution)/shard_map/ppermute | solution.py:235
  90.6 10.6 %collective-permute-start.20 = (bf16[64,2176]{1,0:T(8,128)(2,1)S(1)}, bf16[64,2176]{1,0:T(8,128)(2,1)}, u32[]{:S(2)}, u32[]{:S(2)}) collective-permute-start(bf16[64,2176]{1,0:T(8,128)(2,1)S(1)} %concatenate.3.refs_0_), channel_id=1, source_target_pairs={{0,24},{4,28},{8,16},{12,20},{16,8},{20,12},{24,0},{28,4},{1,25},{... | collective-permute-start | bytes 835592 | tf_op jit(solution)/shard_map/ppermute | solution.py:232
  101.2 8.0 %collective-permute-start.8 = (bf16[64,2176]{1,0:T(8,128)(2,1)S(1)}, bf16[64,2176]{1,0:T(8,128)(2,1)S(1)}, u32[]{:S(2)}, u32[]{:S(2)}) collective-permute-start(bf16[64,2176]{1,0:T(8,128)(2,1)S(1)} %concatenate.3.refs_0_), channel_id=1, source_target_pairs={{0,8},{4,12},{8,0},{12,4},{16,24},{20,28},{24,16},{28,20},{1,9},{5... | collective-permute-start | bytes 835592 | tf_op jit(solution)/shard_map/ppermute | solution.py:232
  109.2 1.5 copy-start.4
  109.2 9.8 %collective-permute-start.19 = (bf16[64,2176]{1,0:T(8,128)(2,1)}, bf16[64,2176]{1,0:T(8,128)(2,1)}, u32[]{:S(2)}, u32[]{:S(2)}) collective-permute-start(bf16[64,2176]{1,0:T(8,128)(2,1)} %collective-permute-done.18.refs_0_), channel_id=1, source_target_pairs={{0,4},{4,0},{8,12},{12,8},{16,20},{20,16},{24,28},{28,24},{1,5},{5... | collective-permute-start | bytes 835592 | tf_op jit(solution)/shard_map/ppermute | solution.py:235
  110.7 14.2 %collective-permute-start.21 = (bf16[64,2176]{1,0:T(8,128)(2,1)}, bf16[64,2176]{1,0:T(8,128)(2,1)S(1)}, u32[]{:S(2)}, u32[]{:S(2)}) collective-permute-start(bf16[64,2176]{1,0:T(8,128)(2,1)} %collective-permute-done.20.refs_2_), channel_id=1, source_target_pairs={{0,4},{4,0},{8,12},{12,8},{16,20},{20,16},{24,28},{28,24},{1,5},{5... | collective-permute-start | bytes 835592 | tf_op jit(solution)/shard_map/ppermute | solution.py:235
  119.1 18.1 %collective-permute-start.7 = (bf16[64,2176]{1,0:T(8,128)(2,1)S(1)}, bf16[64,2176]{1,0:T(8,128)(2,1)S(1)}, u32[]{:S(2)}, u32[]{:S(2)}) collective-permute-start(bf16[64,2176]{1,0:T(8,128)(2,1)S(1)} %concatenate.3.refs_0_), channel_id=1, source_target_pairs={{0,4},{4,0},{8,12},{12,8},{16,20},{20,16},{24,28},{28,24},{1,5},{5... | collective-permute-start | bytes 835592 | tf_op jit(solution)/shard_map/ppermute | solution.py:235
  124.9 1.5 copy-start.5
  124.9 12.2 %collective-permute-start.9 = (bf16[64,2176]{1,0:T(8,128)(2,1)}, bf16[64,2176]{1,0:T(8,128)(2,1)S(1)}, u32[]{:S(2)}, u32[]{:S(2)}) collective-permute-start(bf16[64,2176]{1,0:T(8,128)(2,1)} %copy-done.4), channel_id=1, source_target_pairs={{0,4},{4,0},{8,12},{12,8},{16,20},{20,16},{24,28},{28,24},{1,5},{5... | collective-permute-start | bytes 835592 | tf_op jit(solution)/shard_map/ppermute | solution.py:235
  135.1 14.2 %collective-permute-start.23 = (bf16[64,2048]{1,0:T(8,128)(2,1)}, bf16[64,2048]{1,0:T(8,128)(2,1)S(1)}, u32[]{:S(2)}, u32[]{:S(2)}) collective-permute-start(bf16[64,2048]{1,0:T(8,128)(2,1)} %get-tuple-element.30), channel_id=1, source_target_pairs={{0,4},{4,0},{8,12},{12,8},{16,20},{20,16},{24,28},{28,24},{1,5},{5... | collective-permute-start | bytes 786440 | tf_op jit(solution)/shard_map/ppermute | solution.py:245
  135.8 13.4 %copy-start.9 = (bf16[64,2048]{1,0:T(8,128)(2,1)S(1)}, bf16[64,2048]{1,0:T(8,128)(2,1)}, u32[]{:S(2)}) copy-start(bf16[64,2048]{1,0:T(8,128)(2,1)} %get-tuple-element.29) | copy-start | bytes 786436
  135.8 13.5 %copy-start.8 = (bf16[64,2048]{1,0:T(8,128)(2,1)S(1)}, bf16[64,2048]{1,0:T(8,128)(2,1)}, u32[]{:S(2)}) copy-start(bf16[64,2048]{1,0:T(8,128)(2,1)} %get-tuple-element.27) | copy-start | bytes 786436
  135.8 13.5 %collective-permute-start.22 = (bf16[64,2048]{1,0:T(8,128)(2,1)}, bf16[64,2048]{1,0:T(8,128)(2,1)S(1)}, u32[]{:S(2)}, u32[]{:S(2)}) collective-permute-start(bf16[64,2048]{1,0:T(8,128)(2,1)} %get-tuple-element.28), channel_id=1, source_target_pairs={{0,4},{4,0},{8,12},{12,8},{16,20},{20,16},{24,28},{28,24},{1,5},{5... | collective-permute-start | bytes 786440 | tf_op jit(solution)/shard_map/ppermute | solution.py:245
  137.1 0.7 copy-start.6
  137.9 0.7 copy-start.7
  147.1 26.1 %copy-start.10 = (bf16[64,2048]{1,0:T(8,128)(2,1)S(1)}, bf16[64,2048]{1,0:T(8,128)(2,1)}, u32[]{:S(2)}) copy-start(bf16[64,2048]{1,0:T(8,128)(2,1)} %get-tuple-element.23) | copy-start | bytes 786436
  147.1 6.6 %collective-permute-start.17 = (bf16[64,2048]{1,0:T(8,128)(2,1)}, bf16[64,2048]{1,0:T(8,128)(2,1)S(1)}, u32[]{:S(2)}, u32[]{:S(2)}) collective-permute-start(bf16[64,2048]{1,0:T(8,128)(2,1)} %get-tuple-element.26), channel_id=1, source_target_pairs={{0,4},{4,0},{8,12},{12,8},{16,20},{20,16},{24,28},{28,24},{1,5},{5... | collective-permute-start | bytes 786440 | tf_op jit(solution)/shard_map/ppermute | solution.py:245
  147.9 11.7 %collective-permute-start.16 = (bf16[64,2048]{1,0:T(8,128)(2,1)}, bf16[64,2048]{1,0:T(8,128)(2,1)S(1)}, u32[]{:S(2)}, u32[]{:S(2)}) collective-permute-start(bf16[64,2048]{1,0:T(8,128)(2,1)} %get-tuple-element.24), channel_id=1, source_target_pairs={{0,4},{4,0},{8,12},{12,8},{16,20},{20,16},{24,28},{28,24},{1,5},{5... | collective-permute-start | bytes 786440 | tf_op jit(solution)/shard_map/ppermute | solution.py:245
  154.8 10.4 %collective-permute-start.26 = (bf16[64,2048]{1,0:T(8,128)(2,1)S(1)}, bf16[64,2048]{1,0:T(8,128)(2,1)S(1)}, u32[]{:S(2)}, u32[]{:S(2)}) collective-permute-start(bf16[64,2048]{1,0:T(8,128)(2,1)S(1)} %add_convert_fusion.1), channel_id=1, source_target_pairs={{8,0},{12,4},{0,8},{4,12},{24,16},{28,20},{16,24},{20,28},{9,1},{1... | collective-permute-start | bytes 786440 | tf_op jit(solution)/shard_map/ppermute | solution.py:256
  156.6 16.6 %collective-permute-start.25 = (bf16[64,2048]{1,0:T(8,128)(2,1)S(1)}, bf16[64,2048]{1,0:T(8,128)(2,1)S(1)}, u32[]{:S(2)}, u32[]{:S(2)}) collective-permute-start(bf16[64,2048]{1,0:T(8,128)(2,1)S(1)} %add_convert_fusion.2), channel_id=1, source_target_pairs={{16,0},{20,4},{24,8},{28,12},{0,16},{4,20},{8,24},{12,28},{17,1},{... | collective-permute-start | bytes 786440 | tf_op jit(solution)/shard_map/ppermute | solution.py:256
  158.7 14.5 %collective-permute-start.24 = (bf16[64,2048]{1,0:T(8,128)(2,1)S(1)}, bf16[64,2048]{1,0:T(8,128)(2,1)S(1)}, u32[]{:S(2)}, u32[]{:S(2)}) collective-permute-start(bf16[64,2048]{1,0:T(8,128)(2,1)S(1)} %add_convert_fusion.3), channel_id=1, source_target_pairs={{24,0},{28,4},{16,8},{20,12},{8,16},{12,20},{0,24},{4,28},{25,1},{... | collective-permute-start | bytes 786440 | tf_op jit(solution)/shard_map/ppermute | solution.py:256

commit v4 on v3

v4 whole, which is shorter than its diff:
```python
import functools

import jax
import jax.numpy as jnp
from jax import lax
from jax.experimental import pallas as pl
from jax.experimental.pallas import tpu as pltpu
from jax.sharding import PartitionSpec as P


epsilon = 1e-06
chunk_rows = 128
chunks_per_step = 2


def product(left, right, contract=((1,), (0,))):
    left, right = left.astype(jnp.bfloat16), right.astype(jnp.bfloat16)
    return lax.dot_general(left, right, (contract, ((), ())), preferred_element_type=jnp.float32)


def split_exact(value):
    parts = []
    for _ in range(3):
        part = value.astype(jnp.bfloat16)
        parts.append(part)
        value = value - part.astype(jnp.float32)
    return jnp.concatenate(parts, axis=0)


def mix_kernel(
    heads,
    requests,
    owned,
    rows,
    query_ref,
    key_ref,
    value_ref,
    gate_ref,
    beta_ref,
    decay_ref,
    lengths_ref,
    cache_ref,
    gain_ref,
    proj_ref,
    states_ref,
    *share_refs,
):
    step = pl.program_id(0)
    parts = query_ref.shape[0] // rows
    dim = gain_ref.shape[1]
    f32, bf16 = jnp.float32, jnp.bfloat16

    @pl.when(step == 0)
    def _():
        states_ref[...] = cache_ref[...]

    row_of = lax.broadcasted_iota(jnp.int32, (rows, rows), 0)
    col_of = lax.broadcasted_iota(jnp.int32, (rows, rows), 1)
    eye = (row_of == col_of).astype(f32)
    levels = []
    span = 2
    while span < rows:
        levels.append(
            (row_of // (2 * span) == col_of // (2 * span))
            & ((row_of // span) % 2 == 1)
            & ((col_of // span) % 2 == 0)
        )
        span *= 2
    first = (row_of // 2 == col_of // 2) & (row_of != col_of)

    chunks, terms = [], []
    for part in range(parts):
        here = slice(part * rows, (part + 1) * rows)
        request_col = jnp.zeros((rows, 1), jnp.int32)
        request_row = jnp.zeros((1, rows), jnp.int32)
        base = (step * parts + part) * rows
        place_col = lax.broadcasted_iota(jnp.int32, (rows, 1), 0) + base
        place_row = lax.broadcasted_iota(jnp.int32, (1, rows), 1) + base
        end = jnp.int32(0)
        for r in range(requests):
            end = end + lengths_ref[0, r]
            request_col = request_col + (place_col >= end).astype(jnp.int32)
            request_row = request_row + (place_row >= end).astype(jnp.int32)
        shared = request_col == request_row
        inside = shared & (row_of >= col_of)
        after = shared & (row_of < col_of)
        strict = shared & (row_of > col_of)
        decay = decay_ref[:, here]
        pieces = jnp.concatenate([split_exact(decay), split_exact(beta_ref[:, here])], axis=0)
        inside_b = inside.astype(f32)
        masks = jnp.concatenate([inside_b, after.astype(f32), eye], axis=0)
        sums = product(masks, pieces, ((1,), (1,)))
        triple = lambda value, at: (
            value[:, at : at + heads]
            + value[:, at + heads : at + 2 * heads]
            + value[:, at + 2 * heads : at + 3 * heads]
        )
        running = triple(sums[:rows], 0)
        left = triple(sums[rows : 2 * rows], 0)
        strength = triple(sums[2 * rows :], 3 * heads)
        across = product(pieces[: 3 * heads], inside_b, ((1,), (1,)))
        running_t = across[:heads] + across[heads : 2 * heads] + across[2 * heads :]
        totals = [
            jnp.exp(jnp.sum(jnp.where(request_row == r, decay, 0.0), axis=1, keepdims=True))
            for r in range(requests)
        ]
        in_col = [request_col == r for r in range(requests)]
        in_row = [request_row == r for r in range(requests)]
        items = []
        for h in range(heads):
            lanes = slice(h * dim, (h + 1) * dim)
            key = key_ref[here, lanes].astype(f32)
            key = key * lax.rsqrt(jnp.sum(key * key, axis=-1, keepdims=True) + epsilon)
            query = query_ref[here, lanes].astype(f32)
            query = query * (
                lax.rsqrt(jnp.sum(query * query, axis=-1, keepdims=True) + epsilon)
                * dim ** (-0.5)
            )
            beta = strength[:, h : h + 1]
            gaps = running[:, h : h + 1] - running_t[h : h + 1, :]
            decays = jnp.where(inside, jnp.exp(jnp.minimum(gaps, 0.0)), 0.0)
            key_b = key.astype(bf16)
            both = product(
                jnp.concatenate([key_b, query.astype(bf16)], axis=0), key_b, ((1,), (1,))
            )
            growth = jnp.exp(running[:, h : h + 1])
            terms.append(jnp.where(strict, decays * both[:rows] * beta, 0.0).astype(bf16))
            targets = jnp.concatenate(
                [
                    (key * (beta * growth)).astype(bf16),
                    (value_ref[here, lanes].astype(f32) * beta).astype(bf16),
                ],
                axis=1,
            )
            items.append(
                (
                    targets,
                    (query * growth).astype(bf16),
                    (both[rows:] * decays).astype(bf16),
                    (key * jnp.exp(left[:, h : h + 1])).T.astype(bf16),
                )
            )
        chunks.append((here, items, totals, in_col, in_row))

    inverses = [eye - jnp.where(first, term.astype(f32), 0.0) for term in terms]
    count = len(terms)
    for mask in levels:
        narrow = [inverse.astype(bf16) for inverse in inverses]
        inner = [
            product(jnp.where(mask, terms[n], 0), narrow[n]).astype(bf16) for n in range(count)
        ]
        inverses = [inverses[n] - product(narrow[n], inner[n]) for n in range(count)]
    solutions = [
        product(inverses[n], chunks[n // heads][1][n % heads][0]) for n in range(count)
    ]

    for part, (here, items, totals, in_col, in_row) in enumerate(chunks):
        normed = []
        for h in range(heads):
            lanes = slice(h * dim, (h + 1) * dim)
            targets, query_g, dots, key_t = items[h]
            solved = solutions[part * heads + h]
            probe = jnp.concatenate([solved[:, :dim].astype(bf16), query_g], axis=0)
            wide = jnp.concatenate(
                [
                    jnp.where(jnp.concatenate([in_col[r], in_col[r]], axis=0), probe, 0)
                    for r in range(requests)
                ],
                axis=1,
            )
            seen = product(wide, states_ref[:, h].reshape(requests * dim, dim))
            update = (solved[:, dim:] - seen[:rows]).astype(bf16)
            mixed = seen[rows:] + product(dots, update)
            for r in range(requests):
                fresh = product(jnp.where(in_row[r], key_t, 0), update)
                states_ref[r, h] = totals[r][h : h + 1, :] * states_ref[r, h] + fresh
            scale = lax.rsqrt(jnp.mean(mixed * mixed, axis=-1, keepdims=True) + epsilon)
            gate = gate_ref[here, lanes].astype(f32)
            normed.append(
                (mixed * scale * gain_ref[...] * (gate * jax.nn.sigmoid(gate))).astype(bf16)
            )
        share = product(jnp.concatenate(normed, axis=1), proj_ref[...]).astype(bf16)
        for block in range(rows // owned):
            slot = part_slot("expert", (step * parts + part) * (rows // owned) + block)
            for place, share_ref in enumerate(share_refs):

                @pl.when(slot == place)
                def _(block=block, share=share, share_ref=share_ref):
                    share_ref[...] = share[block * owned : (block + 1) * owned]


def mix(queries, keys_in, values_in, gate_in, beta, decay, lengths, cache, norm_gain, out_proj, owned):
    tok_count, heads = beta.shape
    requests = lengths.shape[1]
    dim = norm_gain.shape[0]
    rows = min(chunk_rows, tok_count)
    taken = rows * (chunks_per_step if tok_count % (rows * chunks_per_step) == 0 else 1)
    width = out_proj.shape[1]
    block = lambda cols: pl.BlockSpec((taken, cols), lambda c: (c, 0))
    whole = lambda shape: pl.BlockSpec(shape, lambda c: (0,) * len(shape))
    return pl.pallas_call(
        functools.partial(mix_kernel, heads, requests, owned, rows),
        grid=(tok_count // taken,),
        in_specs=[
            block(heads * dim),
            block(heads * dim),
            block(heads * dim),
            block(heads * dim),
            pl.BlockSpec((heads, taken), lambda c: (0, c)),
            pl.BlockSpec((heads, taken), lambda c: (0, c)),
            pl.BlockSpec(memory_space=pltpu.SMEM),
            whole(cache.shape),
            whole((1, dim)),
            whole(out_proj.shape),
        ],
        out_specs=[whole(cache.shape)] + [whole((owned, width))] * (tok_count // owned),
        out_shape=[
            jax.ShapeDtypeStruct(cache.shape, jnp.float32),
        ]
        + [jax.ShapeDtypeStruct((owned, width), jnp.bfloat16)] * (tok_count // owned),
        compiler_params=pltpu.CompilerParams(
            dimension_semantics=("arbitrary",), vmem_limit_bytes=56 << 20
        ),
        cost_estimate=pl.CostEstimate(
            flops=40 * tok_count * heads * dim * dim * requests,
            bytes_accessed=12 * cache.size,
            transcendentals=0,
        ),
        name="mix",
    )(
        queries,
        keys_in,
        values_in,
        gate_in,
        beta.T,
        decay.T,
        lengths,
        cache,
        norm_gain[None],
        out_proj,
    )


def factors(size):
    low = 2 if size % 2 == 0 else 1
    return size // low, low


def partner(size, step, place):
    return place ^ step if size & (size - 1) == 0 else (place + step) % size


def source(size, step, place):
    return place ^ step if size & (size - 1) == 0 else (place - step) % size


def high_pairs(high, low, step):
    return [
        (h * low + m, partner(high, step, h) * low + m) for h in range(high) for m in range(low)
    ]


def low_pairs(high, low):
    return [(h * low + m, h * low + (m ^ 1)) for h in range(high) for m in range(low)]


def reverse(pairs):
    return [(target, origin) for origin, target in pairs]


def gather_parts(block, axis):
    high, low = factors(lax.axis_size(axis))
    parts = [[block]]
    for step in range(1, high):
        if high & (high - 1) == 0 and step & (step - 1):
            sent, hop = parts[step & (step - 1)][0], step & -step
        else:
            sent, hop = block, step
        parts.append([lax.ppermute(sent, axis, high_pairs(high, low, hop))])
    if low == 2:
        for row in parts:
            row.append(lax.ppermute(row[0], axis, low_pairs(high, low)))
    return parts


def scatter_parts(parts, axis, order):
    high, low = factors(lax.axis_size(axis))
    near = {}
    if low == 2:
        for step in order:
            near[step] = lax.ppermute(parts[step][1], axis, low_pairs(high, low))
    addends, before = [], None
    for step in order:
        pair = [parts[step][0]]
        if low == 2:
            other = near[step]
            if before is not None:
                other, before = lax.optimization_barrier((other, before))
            pair.append(other)
        if step == 0:
            addends += pair
            continue
        before = sum_parts(pair).astype(jnp.bfloat16)
        addends.append(lax.ppermute(before, axis, reverse(high_pairs(high, low, step))))
    return addends


def sum_parts(parts):
    total = parts[0].astype(jnp.float32)
    for part in parts[1:]:
        total = total + part.astype(jnp.float32)
    return total


def part_slot(axis, owner):
    high, low = factors(lax.axis_size(axis))
    place = lax.axis_index(axis)
    h, m = place // low, place % low
    other, n = owner // low, owner % low
    step = other ^ h if high & (high - 1) == 0 else (h - other + high) % high
    return step * low + (m ^ n)


def part_sources(axis):
    high, low = factors(lax.axis_size(axis))
    place = lax.axis_index(axis)
    h, m = place // low, place % low
    return [[source(high, step, h) * low + (m ^ j) for j in range(low)] for step in range(high)]


def on_device(
    queries,
    keys_in,
    values_in,
    gate_in,
    beta,
    decay,
    lengths,
    cache,
    norm_gain,
    out_proj,
    residual,
    post_gain,
    expert_ids,
    route_weights,
    gate_up,
    down_proj,
):
    tok_local = residual.shape[0]
    experts_all = lax.axis_size("expert") * lax.axis_size("dp")
    gate_up_parts = sum(gather_parts(gate_up[0], "dp"), [])
    down_parts = sum(gather_parts(down_proj[0], "dp"), [])
    expert_of = sum(part_sources("dp"), [])
    expert_of = [lax.axis_index("expert") * lax.axis_size("dp") + place for place in expert_of]
    new_states, *share = mix(
        queries,
        keys_in,
        values_in,
        gate_in,
        beta,
        decay,
        lengths,
        cache,
        norm_gain,
        out_proj,
        tok_local,
    )
    high, low = factors(lax.axis_size("expert"))
    shares = scatter_parts(
        [share[step * low : (step + 1) * low] for step in range(high)],
        "expert",
        range(high - 1, -1, -1),
    )
    expert_range = jnp.arange(experts_all, dtype=jnp.int32)
    mixing = jnp.sum(
        jnp.where(expert_ids[:, :, None] == expert_range, route_weights[:, :, None], 0.0), axis=1
    )
    coarse = mixing.astype(jnp.bfloat16)
    fine = (mixing - coarse.astype(jnp.float32)).astype(jnp.bfloat16)
    pad = jnp.zeros((tok_local, -2 * experts_all % 128), jnp.bfloat16)
    attn_out, block = close(
        shares, residual, post_gain, jnp.concatenate([coarse, fine, pad], axis=1)
    )
    gathered = gather_parts(block, "expert")
    places = jnp.stack(expert_of).astype(jnp.int32)
    half = high // 2
    middle = half + (high - half) // 2
    groups = [range(half, middle), range(middle, high), range(half)]
    results = {}
    for group in groups:
        blocks = [(step, j) for step in group for j in range(low)]
        if blocks:
            outs = experts(
                places,
                [gathered[step][j] for step, j in blocks],
                gate_up_parts,
                down_parts,
                experts_all,
            )
            results.update(zip(blocks, outs))
    moe_out = sum_parts(scatter_parts(
        [[results[step, j] for j in range(low)] for step in range(high)],
        "expert",
        [*groups[0], *groups[1], *reversed(groups[2])],
    )).astype(jnp.bfloat16)
    return (moe_out, attn_out, new_states)


def close_kernel(count, *refs):
    gain_ref, mixing_ref, attn_ref, block_ref, buffer, sems = refs[count:]
    width = attn_ref.shape[1]
    loads = [pltpu.make_async_copy(refs[n], buffer.at[n], sems.at[n]) for n in range(count)]
    for load in loads:
        load.start()
    for load in loads:
        load.wait()
    attn_ref[...] = sum_parts([buffer[n] for n in range(count)]).astype(jnp.bfloat16)
    stream = attn_ref[...].astype(jnp.float32)
    scale = lax.rsqrt(jnp.mean(stream * stream, axis=-1, keepdims=True) + epsilon)
    block_ref[:, :width] = (stream * scale * gain_ref[...]).astype(jnp.bfloat16)
    block_ref[:, width:] = mixing_ref[...]


def close(shares, residual, post_gain, mixing):
    rows, width = residual.shape
    parts = [residual, *shares]
    wide = width + mixing.shape[1]
    vmem = pl.BlockSpec(memory_space=pltpu.VMEM)
    return pl.pallas_call(
        functools.partial(close_kernel, len(parts)),
        in_specs=[pl.BlockSpec(memory_space=pl.ANY)] * len(parts) + [vmem] * 2,
        out_specs=[vmem] * 2,
        out_shape=[
            jax.ShapeDtypeStruct((rows, width), jnp.bfloat16),
            jax.ShapeDtypeStruct((rows, wide), jnp.bfloat16),
        ],
        scratch_shapes=[
            pltpu.VMEM((len(parts), rows, width), jnp.bfloat16),
            pltpu.SemaphoreType.DMA((len(parts),)),
        ],
        compiler_params=pltpu.CompilerParams(vmem_limit_bytes=16 << 20),
        name="close",
    )(*parts, post_gain[None], mixing)


def experts_kernel(blocks, slots, experts_all, places_ref, *refs):
    row_refs = refs[:blocks]
    gate_up_refs = refs[blocks : blocks + slots]
    down_refs = refs[blocks + slots : blocks + 2 * slots]
    out_refs = refs[blocks + 2 * slots : 2 * blocks + 2 * slots]
    hidden_buf = refs[2 * blocks + 2 * slots]
    width, hidden_width = gate_up_refs[0].shape[0], down_refs[0].shape[0]
    rows = jnp.concatenate([ref[:, :width] for ref in row_refs], axis=0)
    mixing = jnp.concatenate([ref[:, width:] for ref in row_refs], axis=0).astype(jnp.float32)
    lane = lax.broadcasted_iota(jnp.int32, mixing.shape, 1)
    for i in range(slots):
        place = places_ref[i]
        named = (lane == place) | (lane == place + experts_all)
        weight = jnp.sum(jnp.where(named, mixing, 0.0), axis=1, keepdims=True)
        both = product(rows, gate_up_refs[i][...])
        gate = both[:, :hidden_width]
        hidden = gate * jax.nn.sigmoid(gate) * both[:, hidden_width:] * weight
        hidden_buf[:, i * hidden_width : (i + 1) * hidden_width] = hidden.astype(jnp.bfloat16)
    size = row_refs[0].shape[0]
    tile = min(512, width)
    for start in range(0, width, tile):
        down = jnp.concatenate([ref[:, start : start + tile] for ref in down_refs], axis=0)
        result = product(hidden_buf[...], down).astype(jnp.bfloat16)
        for n in range(blocks):
            out_refs[n][:, start : start + tile] = result[n * size : (n + 1) * size]


def experts(places, row_blocks, gate_up_parts, down_parts, experts_all):
    blocks, slots = len(row_blocks), len(gate_up_parts)
    size = row_blocks[0].shape[0]
    width, hidden_twice = gate_up_parts[0].shape
    hidden_width = down_parts[0].shape[0]
    vmem = pl.BlockSpec(memory_space=pltpu.VMEM)
    return pl.pallas_call(
        functools.partial(experts_kernel, blocks, slots, experts_all),
        in_specs=[pl.BlockSpec(memory_space=pltpu.SMEM)]
        + [vmem] * (blocks + 2 * slots),
        out_specs=[vmem] * blocks,
        out_shape=[jax.ShapeDtypeStruct((size, width), jnp.bfloat16)] * blocks,
        scratch_shapes=[
            pltpu.VMEM((blocks * size, slots * hidden_width), jnp.bfloat16),
        ],
        cost_estimate=pl.CostEstimate(
            flops=2 * blocks * size * slots * width * (hidden_twice + hidden_width),
            bytes_accessed=4 * blocks * size * width,
            transcendentals=0,
        ),
        compiler_params=pltpu.CompilerParams(
            vmem_limit_bytes=(12 << 20)
            + 2 * slots * width * (hidden_twice + hidden_width)
        ),
        name="experts",
    )(places, *row_blocks, *gate_up_parts, *down_parts)


def solution(mesh):
    return jax.shard_map(
        on_device,
        mesh=mesh,
        in_specs=(
            P(("groups", "dp"), "expert"),
            P(("groups", "dp"), "expert"),
            P(("groups", "dp"), "expert"),
            P(("groups", "dp"), "expert"),
            P(("groups", "dp"), "expert"),
            P(("groups", "dp"), "expert"),
            P(("groups", "dp"), None),
            P(("groups", "dp"), "expert", None, None),
            P(),
            P("expert", None),
            P(("groups", "dp", "expert"), None),
            P(),
            P(("groups", "dp", "expert"), None),
            P(("groups", "dp", "expert"), None),
            P(("expert", "dp"), None, None),
            P(("expert", "dp"), None, None),
        ),
        out_specs=(
            P(("groups", "dp", "expert"), None),
            P(("groups", "dp", "expert"), None),
            P(("groups", "dp"), "expert", None, None),
        ),
        check_vma=False,
    )
```

time: 176 us -> 177 us (level)
  waiting for transfers between devices: 84.6 us -> 90.6 us
  other arithmetic: 9.64 us -> 4.41 us
  Pallas kernels: 38.2 us -> 36.3 us
  local copies, waits for them, and re-layouts: 4.86 us -> 6.73 us
    ppermute x19, waiting for transfers between devices: 73.2 us -> 89.4 us  [the longest x6 34.4 us: scatter_parts(): lax.ppermute(before, axis, reverse(high_pairs(high, low, step)))]
    ppermute x8, waiting for transfers between devices: 11.4 us -> 1.22 us  [gather_parts(): row.append(lax.ppermute(row[0], axis, low_pairs(high, low)))]
    unnamed x28, local copies, waits for them, and re-layouts: 1.48 us -> 6.48 us
    convert_element_type x8 -> x7, other arithmetic: 7.3 us -> 4.21 us  [the longest x6 3.33 us: scatter_parts(): before = sum_parts(pair).astype(jnp.bfloat16)]
    pallas_call x1 -> x2, Pallas kernels: 21 us -> 18.6 us  [the longest x1 17.3 us: mix(): pl.pallas_call(functools.partial(mix_kernel, heads, requests, owned, rows...]
    squeeze x1 -> x0, local copies, waits for them, and re-layouts: 2.15 us -> none  [on_device(): share[step, j]]
    pallas_call x2 -> x3, Pallas kernels: 17.1 us -> 17.7 us  [experts(): pl.pallas_call(functools.partial(experts_kernel, blocks, slots, experts_a...]
  transfers between devices with their start and end apart: 27 -> 27, of which waited for: 14 -> 16; matrix products, arithmetic and copies ran while one was open for 7% -> 2% of each run, Pallas kernels for 22% -> 21%
where the time goes in v4:
time: 177 us; the launch traced here: 176 us
  waiting for transfers between devices  90.6 us (51%)
  starting transfers between devices  37.6 us (21%)
  Pallas kernels  36.3 us (21%)
  local copies, waits for them, and re-layouts  6.73 us (4%)
  other arithmetic  4.41 us (2%)
    ppermute x6, waiting for transfers between devices, scatter_parts(): lax.ppermute(before, axis, reverse(high_pairs(high, low, step)))  34.4 us
    ppermute x5, waiting for transfers between devices, gather_parts(): parts.append([lax.ppermute(sent, axis, high_pairs(high, low, hop))])  31 us
    ppermute x8, waiting for transfers between devices, scatter_parts(): near[step] = lax.ppermute(parts[step][1], axis, low_pairs(high, low))  24 us
    pallas_call x3, Pallas kernels, experts(): pl.pallas_call(functools.partial(experts_kernel, blocks, slots, experts_a...  17.7 us
    pallas_call x1, Pallas kernels, mix(): pl.pallas_call(functools.partial(mix_kernel, heads, requests, owned, rows...  17.3 us
    ppermute x6, starting transfers between devices, scatter_parts(): lax.ppermute(before, axis, reverse(high_pairs(high, low, step)))  12.6 us
    ppermute x8, starting transfers between devices, scatter_parts(): near[step] = lax.ppermute(parts[step][1], axis, low_pairs(high, low))  10 us
    ppermute x5, starting transfers between devices, gather_parts(): parts.append([lax.ppermute(sent, axis, high_pairs(high, low, hop))])  9.3 us
  transfers between devices with their start and end apart: 27, of which 16 were waited for; matrix products, arithmetic and copies ran while one was open for 2% of the time, Pallas kernels for 21%

profile of v4, /device:TPU:0, one launch (start us, length us, event | category | flops | bytes accessed | tf_op | source)
XLA Modules:
  0.0 176.4 jit_solution(1906080489764835646)
XLA Ops:
  0.6 3.0 %collective-permute-start.10 = (bf16[2048,512]{1,0:T(8,128)(2,1)}, bf16[2048,512]{1,0:T(8,128)(2,1)}, u32[]{:S(2)}, u32[]{:S(2)}) collective-permute-start(bf16[2048,512]{1,0:T(8,128)(2,1)} %bitcast.10), channel_id=1, source_target_pairs={{0,2},{1,3},{2,0},{3,1},{4,6},{5,7},{6,4},{7,5},{8,10},{9,11},{10,... | collective-permute-start | bytes 6291464 | tf_op jit(solution)/shard_map/ppermute | solution.py:279
  3.7 17.3 %mix.1 = (f32[4,4,128,128]{3,2,1,0:T(8,128)}, bf16[64,2048]{1,0:T(8,128)(2,1)}, bf16[64,2048]{1,0:T(8,128)(2,1)}, bf16[64,2048]{1,0:T(8,128)(2,1)}, bf16[64,2048...) custom-call(bf16[512,512]{1,0:T(8,128)(2,1)} %query_ref.1, ...), custom_call_target="tpu_custom_call" | custom-call | flops 5368709120 | bytes 3145728 | tf_op jit(solution)/shard_map/mix/pallas_call | solution.py:201
  21.0 1.6 collective-permute-start
  23.5 7.0 %collective-permute-done = bf16[64,2048]{1,0:T(8,128)(2,1)} collective-permute-done((bf16[64,2048]{1,0:T(8,128)(2,1)}, bf16[64,2048]{1,0:T(8,128)(2,1)}, u32[]{:S(2)}, u32[]{:S(2)}) %collective-permute-start) | collective-permute-done | bytes 262176 | tf_op jit(solution)/shard_map/ppermute | solution.py:291
  30.5 1.5 collective-permute-start.4
  32.0 1.1 add_convert_fusion.6
  33.1 2.9 %collective-permute-done.2 = bf16[64,2048]{1,0:T(8,128)(2,1)S(1)} collective-permute-done((bf16[64,2048]{1,0:T(8,128)(2,1)}, bf16[64,2048]{1,0:T(8,128)(2,1)S(1)}, u32[]{:S(2)}, u32[]{:S(2)}) %collective-permute-start.2) | collective-permute-done | bytes 262176 | tf_op jit(solution)/shard_map/ppermute | solution.py:291
  36.0 1.5 collective-permute-start.6
  37.5 4.1 %collective-permute-done.4 = bf16[64,2048]{1,0:T(8,128)(2,1)S(1)} collective-permute-done((bf16[64,2048]{1,0:T(8,128)(2,1)}, bf16[64,2048]{1,0:T(8,128)(2,1)S(1)}, u32[]{:S(2)}, u32[]{:S(2)}) %collective-permute-start.4) | collective-permute-done | bytes 262176 | tf_op jit(solution)/shard_map/ppermute | solution.py:291
  41.6 3.6 %collective-permute-start.1 = (bf16[64,2048]{1,0:T(8,128)(2,1)S(1)}, bf16[64,2048]{1,0:T(8,128)(2,1)S(1)}, u32[]{:S(2)}, u32[]{:S(2)}) collective-permute-start(bf16[64,2048]{1,0:T(8,128)(2,1)S(1)} %add_convert_fusion.6), channel_id=1, source_target_pairs={{24,0},{28,4},{16,8},{20,12},{8,16},{12,20},{0,24},{4,28},{25,1},{... | collective-permute-start | bytes 786440 | tf_op jit(solution)/shard_map/ppermute | solution.py:304
  45.2 5.2 %collective-permute-done.10.refs_4_.refs_6_ = bf16[2048,512]{1,0:T(8,128)(2,1)} collective-permute-done((bf16[2048,512]{1,0:T(8,128)(2,1)}, bf16[2048,512]{1,0:T(8,128)(2,1)}, u32[]{:S(2)}, u32[]{:S(2)}) %collective-permute-start.10) | collective-permute-done | bytes 2097184 | tf_op jit(solution)/shard_map/ppermute | solution.py:279
  50.5 1.0 add_convert_fusion.5
  52.1 3.4 %collective-permute-start.3 = (bf16[64,2048]{1,0:T(8,128)(2,1)S(1)}, bf16[64,2048]{1,0:T(8,128)(2,1)S(1)}, u32[]{:S(2)}, u32[]{:S(2)}) collective-permute-start(bf16[64,2048]{1,0:T(8,128)(2,1)S(1)} %add_convert_fusion.5), channel_id=1, source_target_pairs={{16,0},{20,4},{24,8},{28,12},{0,16},{4,20},{8,24},{12,28},{17,1},{... | collective-permute-start | bytes 786440 | tf_op jit(solution)/shard_map/ppermute | solution.py:304
  55.4 1.0 add_convert_fusion.4
  56.5 10.9 %collective-permute-done.3.refs_2_ = bf16[64,2048]{1,0:T(8,128)(2,1)S(1)} collective-permute-done((bf16[64,2048]{1,0:T(8,128)(2,1)S(1)}, bf16[64,2048]{1,0:T(8,128)(2,1)S(1)}, u32[]{:S(2)}, u32[]{:S(2)}) %collective-permute-start.3) | collective-permute-done | bytes 262176 | tf_op jit(solution)/shard_map/ppermute | solution.py:304
  67.4 0.7 collective-permute-start.5
  68.2 3.9 %collective-permute-done.13.refs_8_.refs_10_ = bf16[256,2048]{1,0:T(8,128)(2,1)} collective-permute-done((bf16[256,2048]{1,0:T(8,128)(2,1)S(1)}, bf16[256,2048]{1,0:T(8,128)(2,1)}, u32[]{:S(2)}, u32[]{:S(2)}) %collective-permute-start.13) | collective-permute-done | bytes 1048608 | tf_op jit(solution)/shard_map/ppermute | solution.py:279
  72.2 2.6 %collective-permute-done.5.refs_3_ = bf16[64,2048]{1,0:T(8,128)(2,1)S(1)} collective-permute-done((bf16[64,2048]{1,0:T(8,128)(2,1)S(1)}, bf16[64,2048]{1,0:T(8,128)(2,1)S(1)}, u32[]{:S(2)}, u32[]{:S(2)}) %collective-permute-start.5) | collective-permute-done | bytes 262176 | tf_op jit(solution)/shard_map/ppermute | solution.py:304
  74.8 0.9 copy-done.9
  75.8 1.3 close.1
  77.1 1.6 collective-permute-start.22
  78.6 6.1 %collective-permute-done.22.refs_2_ = bf16[64,2176]{1,0:T(8,128)(2,1)} collective-permute-done((bf16[64,2176]{1,0:T(8,128)(2,1)S(1)}, bf16[64,2176]{1,0:T(8,128)(2,1)}, u32[]{:S(2)}, u32[]{:S(2)}) %collective-permute-start.22) | collective-permute-done | bytes 278560 | tf_op jit(solution)/shard_map/ppermute | solution.py:279
  84.7 3.7 %collective-permute-start.7 = (bf16[64,2176]{1,0:T(8,128)(2,1)S(1)}, bf16[64,2176]{1,0:T(8,128)(2,1)S(1)}, u32[]{:S(2)}, u32[]{:S(2)}) collective-permute-start(bf16[64,2176]{1,0:T(8,128)(2,1)S(1)} %get-tuple-element.39.refs_0_), channel_id=1, source_target_pairs={{0,16},{4,20},{8,24},{12,28},{16,0},{20,4},{24,8},{28,12},{1,17},{... | collective-permute-start | bytes 835592 | tf_op jit(solution)/shard_map/ppermute | solution.py:279
  88.4 11.4 %collective-permute-done.7.refs_0_ = bf16[64,2176]{1,0:T(8,128)(2,1)S(1)} collective-permute-done((bf16[64,2176]{1,0:T(8,128)(2,1)S(1)}, bf16[64,2176]{1,0:T(8,128)(2,1)S(1)}, u32[]{:S(2)}, u32[]{:S(2)}) %collective-permute-start.7) | collective-permute-done | bytes 278560 | tf_op jit(solution)/shard_map/ppermute | solution.py:279
  100.2 1.0 copy-done.2
  101.2 1.5 collective-permute-start.8
  102.7 0.7 copy-done.5
  103.4 4.4 %collective-permute-done.17.refs_0_ = bf16[64,2176]{1,0:T(8,128)(2,1)} collective-permute-done((bf16[64,2176]{1,0:T(8,128)(2,1)S(1)}, bf16[64,2176]{1,0:T(8,128)(2,1)}, u32[]{:S(2)}, u32[]{:S(2)}) %collective-permute-start.17) | collective-permute-done | bytes 278560 | tf_op jit(solution)/shard_map/ppermute | solution.py:279
  107.8 1.5 collective-permute-start.21
  109.4 0.7 copy-done.7
  110.1 1.5 collective-permute-start.23
  112.3 1.2 copy-done.3
  113.5 1.0 copy-done.6
  114.5 1.0 copy-done.8
  115.4 5.3 %experts.3 = (bf16[64,2048]{1,0:T(8,128)(2,1)S(1)}, bf16[64,2048]{1,0:T(8,128)(2,1)S(1)}) custom-call(s32[4]{0:T(128)S(1)} %pad_add_fusion.places_ref, bf16[64,2176]{1,0:T(8,128)(2,1)S(1)} %copy-done.6, bf16[64,2176]{1,0:T(8,128)(2,1)S(1)} %copy-done.8, bf16[2048,512]{1,0:T(8,128)(2,1)S(1)} %bitcast.12, ...), custom_call_target="tpu_custom_call" | custom-call | flops 1610612736 | bytes 1048576 | tf_op jit(solution)/shard_map/experts/pallas_call | solution.py:479
  120.7 1.6 collective-permute-start.15
  122.3 1.1 collective-permute-done.23.refs_3_
  123.5 7.1 %experts.5 = (bf16[64,2048]{1,0:T(8,128)(2,1)S(1)}, bf16[64,2048]{1,0:T(8,128)(2,1)S(1)}, bf16[64,2048]{1,0:T(8,128)(2,1)S(1)}, bf16[64,2048]{1,0:T(8,128)(2,1)S(1)}) custom-call(s32[4]{0:T(128)S(1)} %pad_add_fusion.places_ref, bf16[64,2176]{1,0:T(8,128)(2,1)S(1)} %get-tuple-element.39.refs_0_, bf16[64,2176]{1,0:T(8,128)(2,1)} %collective-permute-done.21.refs_1_, ...), custom_call_target="tpu_custom_call" | custom-call | flops 3221225472 | bytes 2097152 | tf_op jit(solution)/shard_map/experts/pallas_call | solution.py:479
  130.5 1.6 collective-permute-start.24
  132.6 5.3 %experts.4 = (bf16[64,2048]{1,0:T(8,128)(2,1)S(1)}, bf16[64,2048]{1,0:T(8,128)(2,1)S(1)}) custom-call(s32[4]{0:T(128)S(1)} %pad_add_fusion.places_ref, bf16[64,2176]{1,0:T(8,128)(2,1)} %collective-permute-done.17.refs_0_, bf16[64,2176]{1,0:T(8,128)(2,1)S(1)} %collective-permute-done.18.refs_1_, bf16[2048,512]{1,0:T(8,128)(2,1)S(1)} %bitcast.14, ...), custom_call_target="tpu_custom_call" | custom-call | flops 1610612736 | bytes 1048576 | tf_op jit(solution)/shard_map/experts/pallas_call | solution.py:479
  137.9 1.6 collective-permute-start.19
  139.6 10.0 %collective-permute-done.19 = bf16[64,2048]{1,0:T(8,128)(2,1)S(1)} collective-permute-done((bf16[64,2048]{1,0:T(8,128)(2,1)S(1)}, bf16[64,2048]{1,0:T(8,128)(2,1)S(1)}, u32[]{:S(2)}, u32[]{:S(2)}) %collective-permute-start.19) | collective-permute-done | bytes 262176 | tf_op jit(solution)/shard_map/ppermute | solution.py:291
  149.7 1.3 collective-permute-start.25
  151.1 3.6 %collective-permute-start.20 = (bf16[64,2048]{1,0:T(8,128)(2,1)S(1)}, bf16[64,2048]{1,0:T(8,128)(2,1)S(1)}, u32[]{:S(2)}, u32[]{:S(2)}) collective-permute-start(bf16[64,2048]{1,0:T(8,128)(2,1)S(1)} %add_convert_fusion.2), channel_id=1, source_target_pairs={{24,0},{28,4},{16,8},{20,12},{8,16},{12,20},{0,24},{4,28},{25,1},{... | collective-permute-start | bytes 786440 | tf_op jit(solution)/shard_map/ppermute | solution.py:304
  154.7 2.3 %collective-permute-done.25 = bf16[64,2048]{1,0:T(8,128)(2,1)S(1)} collective-permute-done((bf16[64,2048]{1,0:T(8,128)(2,1)S(1)}, bf16[64,2048]{1,0:T(8,128)(2,1)S(1)}, u32[]{:S(2)}, u32[]{:S(2)}) %collective-permute-start.25) | collective-permute-done | bytes 262176 | tf_op jit(solution)/shard_map/ppermute | solution.py:304
  157.0 10.6 %collective-permute-done.20 = bf16[64,2048]{1,0:T(8,128)(2,1)S(1)} collective-permute-done((bf16[64,2048]{1,0:T(8,128)(2,1)S(1)}, bf16[64,2048]{1,0:T(8,128)(2,1)S(1)}, u32[]{:S(2)}, u32[]{:S(2)}) %collective-permute-start.20) | collective-permute-done | bytes 262176 | tf_op jit(solution)/shard_map/ppermute | solution.py:304
  167.5 7.9 %collective-permute-done.16 = bf16[64,2048]{1,0:T(8,128)(2,1)S(1)} collective-permute-done((bf16[64,2048]{1,0:T(8,128)(2,1)S(1)}, bf16[64,2048]{1,0:T(8,128)(2,1)S(1)}, u32[]{:S(2)}, u32[]{:S(2)}) %collective-permute-start.16) | collective-permute-done | bytes 262176 | tf_op jit(solution)/shard_map/ppermute | solution.py:304
  175.5 0.9 add_convert_fusion
  (55 shorter events, 3.6 us)
Async XLA Ops:
  0.6 49.8 %collective-permute-start.10 = (bf16[2048,512]{1,0:T(8,128)(2,1)}, bf16[2048,512]{1,0:T(8,128)(2,1)}, u32[]{:S(2)}, u32[]{:S(2)}) collective-permute-start(bf16[2048,512]{1,0:T(8,128)(2,1)} %bitcast.10), channel_id=1, source_target_pairs={{0,2},{1,3},{2,0},{3,1},{4,6},{5,7},{6,4},{7,5},{8,10},{9,11},{10,... | collective-permute-start | bytes 6291464 | tf_op jit(solution)/shard_map/ppermute | solution.py:279
  3.7 18.9 %copy-start = (bf16[1,2048,512]{2,1,0:T(8,128)(2,1)S(1)}, bf16[1,2048,512]{2,1,0:T(8,128)(2,1)}, u32[]{:S(2)}) copy-start(bf16[1,2048,512]{2,1,0:T(8,128)(2,1)} %param.30) | copy-start | bytes 6291460
  3.7 18.9 %copy-start.1 = (bf16[1,256,2048]{2,1,0:T(8,128)(2,1)S(1)}, bf16[1,256,2048]{2,1,0:T(8,128)(2,1)}, u32[]{:S(2)}) copy-start(bf16[1,256,2048]{2,1,0:T(8,128)(2,1)} %param.31) | copy-start | bytes 3145732
  3.7 19.6 %copy-start.12 = (f32[64,10]{0,1:T(8,128)S(1)}, f32[64,10]{0,1:T(8,128)}, u32[]{:S(2)}) copy-start(f32[64,10]{0,1:T(8,128)} %param.29) | copy-start | bytes 7684
  3.7 19.6 %copy-start.13 = (s32[64,10]{0,1:T(8,128)S(1)}, s32[64,10]{0,1:T(8,128)}, u32[]{:S(2)}) copy-start(s32[64,10]{0,1:T(8,128)} %param.28) | copy-start | bytes 7684
  20.9 53.9 %copy-start.11 = (f32[2048]{0:T(1024)S(1)}, f32[2048]{0:T(1024)}, u32[]{:S(2)}) copy-start(f32[2048]{0:T(1024)} %param.27) | copy-start | bytes 24580
  21.0 9.6 %collective-permute-start = (bf16[64,2048]{1,0:T(8,128)(2,1)}, bf16[64,2048]{1,0:T(8,128)(2,1)}, u32[]{:S(2)}, u32[]{:S(2)}) collective-permute-start(bf16[64,2048]{1,0:T(8,128)(2,1)} %get-tuple-element.29), channel_id=1, source_target_pairs={{0,4},{4,0},{8,12},{12,8},{16,20},{20,16},{24,28},{28,24},{1,5},{5... | collective-permute-start | bytes 786440 | tf_op jit(solution)/shard_map/ppermute | solution.py:291
  22.5 89.7 %collective-permute-start.9 = (bf16[2048,512]{1,0:T(8,128)(2,1)S(1)}, bf16[2048,512]{1,0:T(8,128)(2,1)}, u32[]{:S(2)}, u32[]{:S(2)}) collective-permute-start(bf16[2048,512]{1,0:T(8,128)(2,1)S(1)} %bitcast.11), channel_id=1, source_target_pairs={{0,1},{1,0},{2,3},{3,2},{4,5},{5,4},{6,7},{7,6},{8,9},{9,8},{10,11... | collective-permute-start | bytes 6291464 | tf_op jit(solution)/shard_map/ppermute | solution.py:282
  22.5 49.5 %collective-permute-start.13 = (bf16[256,2048]{1,0:T(8,128)(2,1)S(1)}, bf16[256,2048]{1,0:T(8,128)(2,1)}, u32[]{:S(2)}, u32[]{:S(2)}) collective-permute-start(bf16[256,2048]{1,0:T(8,128)(2,1)S(1)} %bitcast.15), channel_id=1, source_target_pairs={{0,2},{1,3},{2,0},{3,1},{4,6},{5,7},{6,4},{7,5},{8,10},{9,11},{10,... | collective-permute-start | bytes 3145736 | tf_op jit(solution)/shard_map/ppermute | solution.py:279
  23.2 12.9 %collective-permute-start.2 = (bf16[64,2048]{1,0:T(8,128)(2,1)}, bf16[64,2048]{1,0:T(8,128)(2,1)S(1)}, u32[]{:S(2)}, u32[]{:S(2)}) collective-permute-start(bf16[64,2048]{1,0:T(8,128)(2,1)} %get-tuple-element.31), channel_id=1, source_target_pairs={{0,4},{4,0},{8,12},{12,8},{16,20},{20,16},{24,28},{28,24},{1,5},{5... | collective-permute-start | bytes 786440 | tf_op jit(solution)/shard_map/ppermute | solution.py:291
  23.5 51.3 %copy-start.10 = (bf16[64,2048]{1,0:T(8,128)(2,1)S(1)}, bf16[64,2048]{1,0:T(8,128)(2,1)}, u32[]{:S(2)}) copy-start(bf16[64,2048]{1,0:T(8,128)(2,1)} %get-tuple-element.36.refs_4_) | copy-start | bytes 786436
  30.5 11.1 %collective-permute-start.4 = (bf16[64,2048]{1,0:T(8,128)(2,1)}, bf16[64,2048]{1,0:T(8,128)(2,1)S(1)}, u32[]{:S(2)}, u32[]{:S(2)}) collective-permute-start(bf16[64,2048]{1,0:T(8,128)(2,1)} %get-tuple-element.34), channel_id=1, source_target_pairs={{0,4},{4,0},{8,12},{12,8},{16,20},{20,16},{24,28},{28,24},{1,5},{5... | collective-permute-start | bytes 786440 | tf_op jit(solution)/shard_map/ppermute | solution.py:291
  36.0 15.5 %collective-permute-start.6 = (bf16[64,2048]{1,0:T(8,128)(2,1)}, bf16[64,2048]{1,0:T(8,128)(2,1)S(1)}, u32[]{:S(2)}, u32[]{:S(2)}) collective-permute-start(bf16[64,2048]{1,0:T(8,128)(2,1)} %get-tuple-element.37), channel_id=1, source_target_pairs={{0,4},{4,0},{8,12},{12,8},{16,20},{20,16},{24,28},{28,24},{1,5},{5... | collective-permute-start | bytes 786440 | tf_op jit(solution)/shard_map/ppermute | solution.py:291
  41.6 10.4 %collective-permute-start.1 = (bf16[64,2048]{1,0:T(8,128)(2,1)S(1)}, bf16[64,2048]{1,0:T(8,128)(2,1)S(1)}, u32[]{:S(2)}, u32[]{:S(2)}) collective-permute-start(bf16[64,2048]{1,0:T(8,128)(2,1)S(1)} %add_convert_fusion.6), channel_id=1, source_target_pairs={{24,0},{28,4},{16,8},{20,12},{8,16},{12,20},{0,24},{4,28},{25,1},{... | collective-permute-start | bytes 786440 | tf_op jit(solution)/shard_map/ppermute | solution.py:304
  50.5 61.8 %collective-permute-start.11 = (bf16[2048,512]{1,0:T(8,128)(2,1)}, bf16[2048,512]{1,0:T(8,128)(2,1)}, u32[]{:S(2)}, u32[]{:S(2)}) collective-permute-start(bf16[2048,512]{1,0:T(8,128)(2,1)} %collective-permute-done.10.refs_4_.refs_6_), channel_id=1, source_target_pairs={{0,1},{1,0},{2,3},{3,2},{4,5},{5,4},{6,7},{7,6},{8,9},{9,8},{10,11... | collective-permute-start | bytes 6291464 | tf_op jit(solution)/shard_map/ppermute | solution.py:282
  51.5 48.7 %collective-permute-start.12 = (bf16[256,2048]{1,0:T(8,128)(2,1)S(1)}, bf16[256,2048]{1,0:T(8,128)(2,1)S(1)}, u32[]{:S(2)}, u32[]{:S(2)}) collective-permute-start(bf16[256,2048]{1,0:T(8,128)(2,1)S(1)} %bitcast.16), channel_id=1, source_target_pairs={{0,1},{1,0},{2,3},{3,2},{4,5},{5,4},{6,7},{7,6},{8,9},{9,8},{10,11... | collective-permute-start | bytes 3145736 | tf_op jit(solution)/shard_map/ppermute | solution.py:282
  52.1 15.3 %collective-permute-start.3 = (bf16[64,2048]{1,0:T(8,128)(2,1)S(1)}, bf16[64,2048]{1,0:T(8,128)(2,1)S(1)}, u32[]{:S(2)}, u32[]{:S(2)}) collective-permute-start(bf16[64,2048]{1,0:T(8,128)(2,1)S(1)} %add_convert_fusion.5), channel_id=1, source_target_pairs={{16,0},{20,4},{24,8},{28,12},{0,16},{4,20},{8,24},{12,28},{17,1},{... | collective-permute-start | bytes 786440 | tf_op jit(solution)/shard_map/ppermute | solution.py:304
  67.4 7.5 %collective-permute-start.5 = (bf16[64,2048]{1,0:T(8,128)(2,1)S(1)}, bf16[64,2048]{1,0:T(8,128)(2,1)S(1)}, u32[]{:S(2)}, u32[]{:S(2)}) collective-permute-start(bf16[64,2048]{1,0:T(8,128)(2,1)S(1)} %add_convert_fusion.4), channel_id=1, source_target_pairs={{8,0},{12,4},{0,8},{4,12},{24,16},{28,20},{16,24},{20,28},{9,1},{1... | collective-permute-start | bytes 786440 | tf_op jit(solution)/shard_map/ppermute | solution.py:304
  72.1 39.7 %collective-permute-start.14 = (bf16[256,2048]{1,0:T(8,128)(2,1)}, bf16[256,2048]{1,0:T(8,128)(2,1)}, u32[]{:S(2)}, u32[]{:S(2)}) collective-permute-start(bf16[256,2048]{1,0:T(8,128)(2,1)} %collective-permute-done.13.refs_8_.refs_10_), channel_id=1, source_target_pairs={{0,1},{1,0},{2,3},{3,2},{4,5},{5,4},{6,7},{7,6},{8,9},{9,8},{10,11... | collective-permute-start | bytes 3145736 | tf_op jit(solution)/shard_map/ppermute | solution.py:282
  74.8 1.0 copy-start.9
  77.1 7.7 %collective-permute-start.22 = (bf16[64,2176]{1,0:T(8,128)(2,1)S(1)}, bf16[64,2176]{1,0:T(8,128)(2,1)}, u32[]{:S(2)}, u32[]{:S(2)}) collective-permute-start(bf16[64,2176]{1,0:T(8,128)(2,1)S(1)} %get-tuple-element.39.refs_0_), channel_id=1, source_target_pairs={{0,8},{4,12},{8,0},{12,4},{16,24},{20,28},{24,16},{28,20},{1,9},{5... | collective-permute-start | bytes 835592 | tf_op jit(solution)/shard_map/ppermute | solution.py:279
  84.7 15.0 %collective-permute-start.7 = (bf16[64,2176]{1,0:T(8,128)(2,1)S(1)}, bf16[64,2176]{1,0:T(8,128)(2,1)S(1)}, u32[]{:S(2)}, u32[]{:S(2)}) collective-permute-start(bf16[64,2176]{1,0:T(8,128)(2,1)S(1)} %get-tuple-element.39.refs_0_), channel_id=1, source_target_pairs={{0,16},{4,20},{8,24},{12,28},{16,0},{20,4},{24,8},{28,12},{1,17},{... | collective-permute-start | bytes 835592 | tf_op jit(solution)/shard_map/ppermute | solution.py:279
  99.8 8.1 %collective-permute-start.17 = (bf16[64,2176]{1,0:T(8,128)(2,1)S(1)}, bf16[64,2176]{1,0:T(8,128)(2,1)}, u32[]{:S(2)}, u32[]{:S(2)}) collective-permute-start(bf16[64,2176]{1,0:T(8,128)(2,1)S(1)} %collective-permute-done.7.refs_0_), channel_id=1, source_target_pairs={{0,8},{4,12},{8,0},{12,4},{16,24},{20,28},{24,16},{28,20},{1,9},{5... | collective-permute-start | bytes 835592 | tf_op jit(solution)/shard_map/ppermute | solution.py:279
  100.2 1.0 copy-start.2
  101.2 8.2 %collective-permute-start.8 = (bf16[64,2176]{1,0:T(8,128)(2,1)S(1)}, bf16[64,2176]{1,0:T(8,128)(2,1)S(1)}, u32[]{:S(2)}, u32[]{:S(2)}) collective-permute-start(bf16[64,2176]{1,0:T(8,128)(2,1)S(1)} %collective-permute-done.7.refs_0_), channel_id=1, source_target_pairs={{0,4},{4,0},{8,12},{12,8},{16,20},{20,16},{24,28},{28,24},{1,5},{5... | collective-permute-start | bytes 835592 | tf_op jit(solution)/shard_map/ppermute | solution.py:282
  102.7 0.7 copy-start.5
  107.8 14.5 %collective-permute-start.21 = (bf16[64,2176]{1,0:T(8,128)(2,1)S(1)}, bf16[64,2176]{1,0:T(8,128)(2,1)}, u32[]{:S(2)}, u32[]{:S(2)}) collective-permute-start(bf16[64,2176]{1,0:T(8,128)(2,1)S(1)} %get-tuple-element.39.refs_0_), channel_id=1, source_target_pairs={{0,4},{4,0},{8,12},{12,8},{16,20},{20,16},{24,28},{28,24},{1,5},{5... | collective-permute-start | bytes 835592 | tf_op jit(solution)/shard_map/ppermute | solution.py:282
  109.4 0.7 copy-start.7
  110.1 13.3 %collective-permute-start.23 = (bf16[64,2176]{1,0:T(8,128)(2,1)}, bf16[64,2176]{1,0:T(8,128)(2,1)}, u32[]{:S(2)}, u32[]{:S(2)}) collective-permute-start(bf16[64,2176]{1,0:T(8,128)(2,1)} %collective-permute-done.22.refs_2_), channel_id=1, source_target_pairs={{0,4},{4,0},{8,12},{12,8},{16,20},{20,16},{24,28},{28,24},{1,5},{5... | collective-permute-start | bytes 835592 | tf_op jit(solution)/shard_map/ppermute | solution.py:282
  111.7 20.9 %collective-permute-start.18 = (bf16[64,2176]{1,0:T(8,128)(2,1)}, bf16[64,2176]{1,0:T(8,128)(2,1)S(1)}, u32[]{:S(2)}, u32[]{:S(2)}) collective-permute-start(bf16[64,2176]{1,0:T(8,128)(2,1)} %collective-permute-done.17.refs_0_), channel_id=1, source_target_pairs={{0,4},{4,0},{8,12},{12,8},{16,20},{20,16},{24,28},{28,24},{1,5},{5... | collective-permute-start | bytes 835592 | tf_op jit(solution)/shard_map/ppermute | solution.py:282
  112.3 1.2 copy-start.3
  113.5 1.0 copy-start.6
  114.5 1.0 copy-start.8
  115.4 8.0 %copy-start.4 = (bf16[256,2048]{1,0:T(8,128)(2,1)S(1)}, bf16[256,2048]{1,0:T(8,128)(2,1)}, u32[]{:S(2)}) copy-start(bf16[256,2048]{1,0:T(8,128)(2,1)} %copy-done.2) | copy-start | bytes 3145732
  120.7 18.8 %collective-permute-start.15 = (bf16[64,2048]{1,0:T(8,128)(2,1)S(1)}, bf16[64,2048]{1,0:T(8,128)(2,1)S(1)}, u32[]{:S(2)}, u32[]{:S(2)}) collective-permute-start(bf16[64,2048]{1,0:T(8,128)(2,1)S(1)} %get-tuple-element.41), channel_id=1, source_target_pairs={{0,4},{4,0},{8,12},{12,8},{16,20},{20,16},{24,28},{28,24},{1,5},{5... | collective-permute-start | bytes 786440 | tf_op jit(solution)/shard_map/ppermute | solution.py:291
  130.5 19.1 %collective-permute-start.24 = (bf16[64,2048]{1,0:T(8,128)(2,1)S(1)}, bf16[64,2048]{1,0:T(8,128)(2,1)S(1)}, u32[]{:S(2)}, u32[]{:S(2)}) collective-permute-start(bf16[64,2048]{1,0:T(8,128)(2,1)S(1)} %get-tuple-element.46), channel_id=1, source_target_pairs={{0,4},{4,0},{8,12},{12,8},{16,20},{20,16},{24,28},{28,24},{1,5},{5... | collective-permute-start | bytes 786440 | tf_op jit(solution)/shard_map/ppermute | solution.py:291
  132.1 22.5 %collective-permute-start.26 = (bf16[64,2048]{1,0:T(8,128)(2,1)S(1)}, bf16[64,2048]{1,0:T(8,128)(2,1)S(1)}, u32[]{:S(2)}, u32[]{:S(2)}) collective-permute-start(bf16[64,2048]{1,0:T(8,128)(2,1)S(1)} %get-tuple-element.49), channel_id=1, source_target_pairs={{0,4},{4,0},{8,12},{12,8},{16,20},{20,16},{24,28},{28,24},{1,5},{5... | collective-permute-start | bytes 786440 | tf_op jit(solution)/shard_map/ppermute | solution.py:291
  137.9 11.6 %collective-permute-start.19 = (bf16[64,2048]{1,0:T(8,128)(2,1)S(1)}, bf16[64,2048]{1,0:T(8,128)(2,1)S(1)}, u32[]{:S(2)}, u32[]{:S(2)}) collective-permute-start(bf16[64,2048]{1,0:T(8,128)(2,1)S(1)} %get-tuple-element.43), channel_id=1, source_target_pairs={{0,4},{4,0},{8,12},{12,8},{16,20},{20,16},{24,28},{28,24},{1,5},{5... | collective-permute-start | bytes 786440 | tf_op jit(solution)/shard_map/ppermute | solution.py:291
  149.7 7.2 %collective-permute-start.25 = (bf16[64,2048]{1,0:T(8,128)(2,1)S(1)}, bf16[64,2048]{1,0:T(8,128)(2,1)S(1)}, u32[]{:S(2)}, u32[]{:S(2)}) collective-permute-start(bf16[64,2048]{1,0:T(8,128)(2,1)S(1)} %add_convert_fusion.1), channel_id=1, source_target_pairs={{8,0},{12,4},{0,8},{4,12},{24,16},{28,20},{16,24},{20,28},{9,1},{1... | collective-permute-start | bytes 786440 | tf_op jit(solution)/shard_map/ppermute | solution.py:304
  151.1 16.5 %collective-permute-start.20 = (bf16[64,2048]{1,0:T(8,128)(2,1)S(1)}, bf16[64,2048]{1,0:T(8,128)(2,1)S(1)}, u32[]{:S(2)}, u32[]{:S(2)}) collective-permute-start(bf16[64,2048]{1,0:T(8,128)(2,1)S(1)} %add_convert_fusion.2), channel_id=1, source_target_pairs={{24,0},{28,4},{16,8},{20,12},{8,16},{12,20},{0,24},{4,28},{25,1},{... | collective-permute-start | bytes 786440 | tf_op jit(solution)/shard_map/ppermute | solution.py:304
  154.7 20.8 %collective-permute-start.16 = (bf16[64,2048]{1,0:T(8,128)(2,1)S(1)}, bf16[64,2048]{1,0:T(8,128)(2,1)S(1)}, u32[]{:S(2)}, u32[]{:S(2)}) collective-permute-start(bf16[64,2048]{1,0:T(8,128)(2,1)S(1)} %add_convert_fusion.3), channel_id=1, source_target_pairs={{16,0},{20,4},{24,8},{28,12},{0,16},{4,20},{8,24},{12,28},{17,1},{... | collective-permute-start | bytes 786440 | tf_op jit(solution)/shard_map/ppermute | solution.py:304

commit v5 on v4

--- a/solution.py
+++ b/solution.py
@@ -289,7 +289,7 @@
     if low == 2:
         for step in order:
             near[step] = lax.ppermute(parts[step][1], axis, low_pairs(high, low))
-    addends, before = [], None
+    own, rest, before = [], [], None
     for step in order:
         pair = [parts[step][0]]
         if low == 2:
@@ -298,11 +298,11 @@
                 other, before = lax.optimization_barrier((other, before))
             pair.append(other)
         if step == 0:
-            addends += pair
+            own = pair
             continue
         before = sum_parts(pair).astype(jnp.bfloat16)
-        addends.append(lax.ppermute(before, axis, reverse(high_pairs(high, low, step))))
-    return addends
+        rest.append(lax.ppermute(before, axis, reverse(high_pairs(high, low, step))))
+    return own, rest
 
 
 def sum_parts(parts):
@@ -366,7 +366,7 @@
         tok_local,
     )
     high, low = factors(lax.axis_size("expert"))
-    shares = scatter_parts(
+    own, rest = scatter_parts(
         [share[step * low : (step + 1) * low] for step in range(high)],
         "expert",
         range(high - 1, -1, -1),
@@ -379,7 +379,10 @@
     fine = (mixing - coarse.astype(jnp.float32)).astype(jnp.bfloat16)
     pad = jnp.zeros((tok_local, -2 * experts_all % 128), jnp.bfloat16)
     attn_out, block = close(
-        shares, residual, post_gain, jnp.concatenate([coarse, fine, pad], axis=1)
+        sum_parts([residual, *own]),
+        rest,
+        post_gain,
+        jnp.concatenate([coarse, fine, pad], axis=1),
     )
     gathered = gather_parts(block, "expert")
     places = jnp.stack(expert_of).astype(jnp.int32)
@@ -398,49 +401,40 @@
                 experts_all,
             )
             results.update(zip(blocks, outs))
-    moe_out = sum_parts(scatter_parts(
+    own, rest = scatter_parts(
         [[results[step, j] for j in range(low)] for step in range(high)],
         "expert",
         [*groups[0], *groups[1], *reversed(groups[2])],
-    )).astype(jnp.bfloat16)
+    )
+    moe_out = sum_parts([*own, *rest]).astype(jnp.bfloat16)
     return (moe_out, attn_out, new_states)
 
 
-def close_kernel(count, *refs):
-    gain_ref, mixing_ref, attn_ref, block_ref, buffer, sems = refs[count:]
+def close_kernel(count, base_ref, *refs):
+    gain_ref, mixing_ref, attn_ref, block_ref = refs[count:]
     width = attn_ref.shape[1]
-    loads = [pltpu.make_async_copy(refs[n], buffer.at[n], sems.at[n]) for n in range(count)]
-    for load in loads:
-        load.start()
-    for load in loads:
-        load.wait()
-    attn_ref[...] = sum_parts([buffer[n] for n in range(count)]).astype(jnp.bfloat16)
+    total = sum_parts([base_ref[...]] + [ref[...] for ref in refs[:count]])
+    attn_ref[...] = total.astype(jnp.bfloat16)
     stream = attn_ref[...].astype(jnp.float32)
     scale = lax.rsqrt(jnp.mean(stream * stream, axis=-1, keepdims=True) + epsilon)
     block_ref[:, :width] = (stream * scale * gain_ref[...]).astype(jnp.bfloat16)
     block_ref[:, width:] = mixing_ref[...]
 
 
-def close(shares, residual, post_gain, mixing):
-    rows, width = residual.shape
-    parts = [residual, *shares]
-    wide = width + mixing.shape[1]
+def close(base, rest, post_gain, mixing):
+    rows, width = base.shape
     vmem = pl.BlockSpec(memory_space=pltpu.VMEM)
     return pl.pallas_call(
-        functools.partial(close_kernel, len(parts)),
-        in_specs=[pl.BlockSpec(memory_space=pl.ANY)] * len(parts) + [vmem] * 2,
+        functools.partial(close_kernel, len(rest)),
+        in_specs=[vmem] * (len(rest) + 3),
         out_specs=[vmem] * 2,
         out_shape=[
             jax.ShapeDtypeStruct((rows, width), jnp.bfloat16),
-            jax.ShapeDtypeStruct((rows, wide), jnp.bfloat16),
+            jax.ShapeDtypeStruct((rows, width + mixing.shape[1]), jnp.bfloat16),
         ],
-        scratch_shapes=[
-            pltpu.VMEM((len(parts), rows, width), jnp.bfloat16),
-            pltpu.SemaphoreType.DMA((len(parts),)),
-        ],
-        compiler_params=pltpu.CompilerParams(vmem_limit_bytes=16 << 20),
+        compiler_params=pltpu.CompilerParams(vmem_limit_bytes=8 << 20),
         name="close",
-    )(*parts, post_gain[None], mixing)
+    )(base, *rest, post_gain[None], mixing)
 
 
 def experts_kernel(blocks, slots, experts_all, places_ref, *refs):

time: 177 us -> 167 us (0.944)
  waiting for transfers between devices: 90.6 us -> 84.3 us
  starting transfers between devices: 37.6 us -> 34.9 us
    ppermute x5, waiting for transfers between devices: 31 us -> 24.5 us  [gather_parts(): parts.append([lax.ppermute(sent, axis, high_pairs(high, low, hop))])]
    ppermute x5, starting transfers between devices: 9.3 us -> 6.32 us  [gather_parts(): parts.append([lax.ppermute(sent, axis, high_pairs(high, low, hop))])]
    unnamed x28 -> x32, local copies, waits for them, and re-layouts: 6.48 us -> 5.55 us
  transfers between devices with their start and end apart: 27 -> 27, of which waited for: 16 -> 15; matrix products, arithmetic and copies ran while one was open for 2% -> 2% of each run, Pallas kernels for 21% -> 22%
where the time goes in v5:
time: 167 us; the launch traced here: 166 us
  waiting for transfers between devices  84.3 us (50%)
  Pallas kernels  35.8 us (21%)
  starting transfers between devices  34.9 us (21%)
  local copies, waits for them, and re-layouts  5.81 us (3%)
  other arithmetic  4.73 us (3%)
    ppermute x6, waiting for transfers between devices, scatter_parts(): lax.ppermute(before, axis, reverse(high_pairs(high, low, step)))  34.7 us
    ppermute x5, waiting for transfers between devices, gather_parts(): parts.append([lax.ppermute(sent, axis, high_pairs(high, low, hop))])  24.5 us
    ppermute x8, waiting for transfers between devices, scatter_parts(): near[step] = lax.ppermute(parts[step][1], axis, low_pairs(high, low))  23.6 us
    pallas_call x3, Pallas kernels, experts(): pl.pallas_call(functools.partial(experts_kernel, blocks, slots, experts_a...  17.7 us
    pallas_call x1, Pallas kernels, mix(): pl.pallas_call(functools.partial(mix_kernel, heads, requests, owned, rows...  17.3 us
    ppermute x6, starting transfers between devices, scatter_parts(): lax.ppermute(before, axis, reverse(high_pairs(high, low, step)))  14 us
    ppermute x8, starting transfers between devices, scatter_parts(): near[step] = lax.ppermute(parts[step][1], axis, low_pairs(high, low))  10.1 us
    ppermute x5, starting transfers between devices, gather_parts(): parts.append([lax.ppermute(sent, axis, high_pairs(high, low, hop))])  6.32 us
  transfers between devices with their start and end apart: 27, of which 15 were waited for; matrix products, arithmetic and copies ran while one was open for 2% of the time, Pallas kernels for 22%

profile of v5, /device:TPU:0, one launch (start us, length us, event | category | flops | bytes accessed | tf_op | source)
XLA Modules:
  0.0 166.4 jit_solution(13234111190590877613)
XLA Ops:
  0.6 3.0 %collective-permute-start.11 = (bf16[2048,512]{1,0:T(8,128)(2,1)}, bf16[2048,512]{1,0:T(8,128)(2,1)}, u32[]{:S(2)}, u32[]{:S(2)}) collective-permute-start(bf16[2048,512]{1,0:T(8,128)(2,1)} %bitcast.10), channel_id=1, source_target_pairs={{0,2},{1,3},{2,0},{3,1},{4,6},{5,7},{6,4},{7,5},{8,10},{9,11},{10,... | collective-permute-start | bytes 6291464 | tf_op jit(solution)/shard_map/ppermute | solution.py:279
  3.7 17.3 %mix.1 = (f32[4,4,128,128]{3,2,1,0:T(8,128)}, bf16[64,2048]{1,0:T(8,128)(2,1)}, bf16[64,2048]{1,0:T(8,128)(2,1)}, bf16[64,2048]{1,0:T(8,128)(2,1)}, bf16[64,2048...) custom-call(bf16[512,512]{1,0:T(8,128)(2,1)} %query_ref.1, ...), custom_call_target="tpu_custom_call" | custom-call | flops 5368709120 | bytes 3145728 | tf_op jit(solution)/shard_map/mix/pallas_call | solution.py:201
  21.0 1.6 collective-permute-start.1
  22.5 0.5 collective-permute-start.2
  23.1 1.5 collective-permute-start.3
  25.0 16.2 %collective-permute-done.3 = bf16[64,2048]{1,0:T(8,128)(2,1)S(1)} collective-permute-done((bf16[64,2048]{1,0:T(8,128)(2,1)}, bf16[64,2048]{1,0:T(8,128)(2,1)S(1)}, u32[]{:S(2)}, u32[]{:S(2)}) %collective-permute-start.3) | collective-permute-done | bytes 262176 | tf_op jit(solution)/shard_map/ppermute | solution.py:291
  41.2 0.3 collective-permute-start.14
  41.5 1.0 add_convert_fusion.6
  42.5 1.8 %collective-permute-start = (bf16[64,2048]{1,0:T(8,128)(2,1)}, bf16[64,2048]{1,0:T(8,128)(2,1)S(1)}, u32[]{:S(2)}, u32[]{:S(2)}) collective-permute-start(bf16[64,2048]{1,0:T(8,128)(2,1)} %get-tuple-element.29), channel_id=1, source_target_pairs={{0,4},{4,0},{8,12},{12,8},{16,20},{20,16},{24,28},{28,24},{1,5},{5... | collective-permute-start | bytes 786440 | tf_op jit(solution)/shard_map/ppermute | solution.py:291
  44.3 3.6 %collective-permute-start.4 = (bf16[64,2048]{1,0:T(8,128)(2,1)S(1)}, bf16[64,2048]{1,0:T(8,128)(2,1)S(1)}, u32[]{:S(2)}, u32[]{:S(2)}) collective-permute-start(bf16[64,2048]{1,0:T(8,128)(2,1)S(1)} %add_convert_fusion.6), channel_id=1, source_target_pairs={{24,0},{28,4},{16,8},{20,12},{8,16},{12,20},{0,24},{4,28},{25,1},{... | collective-permute-start | bytes 786440 | tf_op jit(solution)/shard_map/ppermute | solution.py:304
  47.9 2.5 %collective-permute-done.11.refs_6_.refs_4_ = bf16[2048,512]{1,0:T(8,128)(2,1)} collective-permute-done((bf16[2048,512]{1,0:T(8,128)(2,1)}, bf16[2048,512]{1,0:T(8,128)(2,1)}, u32[]{:S(2)}, u32[]{:S(2)}) %collective-permute-start.11) | collective-permute-done | bytes 2097184 | tf_op jit(solution)/shard_map/ppermute | solution.py:279
  50.5 1.2 add_convert_fusion.5
  51.7 0.6 collective-permute-start.13
  52.3 1.4 collective-permute-done.4.refs_0_
  53.7 6.2 %collective-permute-start.5 = (bf16[64,2048]{1,0:T(8,128)(2,1)S(1)}, bf16[64,2048]{1,0:T(8,128)(2,1)S(1)}, u32[]{:S(2)}, u32[]{:S(2)}) collective-permute-start(bf16[64,2048]{1,0:T(8,128)(2,1)S(1)} %add_convert_fusion.5), channel_id=1, source_target_pairs={{16,0},{20,4},{24,8},{28,12},{0,16},{4,20},{8,24},{12,28},{17,1},{... | collective-permute-start | bytes 786440 | tf_op jit(solution)/shard_map/ppermute | solution.py:304
  59.9 1.1 add_convert_fusion.4
  61.0 9.4 %collective-permute-done.5.refs_1_ = bf16[64,2048]{1,0:T(8,128)(2,1)S(1)} collective-permute-done((bf16[64,2048]{1,0:T(8,128)(2,1)S(1)}, bf16[64,2048]{1,0:T(8,128)(2,1)S(1)}, u32[]{:S(2)}, u32[]{:S(2)}) %collective-permute-start.5) | collective-permute-done | bytes 262176 | tf_op jit(solution)/shard_map/ppermute | solution.py:304
  70.4 1.7 %collective-permute-done.14.refs_10_.refs_8_ = bf16[256,2048]{1,0:T(8,128)(2,1)} collective-permute-done((bf16[256,2048]{1,0:T(8,128)(2,1)S(1)}, bf16[256,2048]{1,0:T(8,128)(2,1)}, u32[]{:S(2)}, u32[]{:S(2)}) %collective-permute-start.14) | collective-permute-done | bytes 1048608 | tf_op jit(solution)/shard_map/ppermute | solution.py:279
  72.2 4.6 %collective-permute-done.6.refs_2_ = bf16[64,2048]{1,0:T(8,128)(2,1)S(1)} collective-permute-done((bf16[64,2048]{1,0:T(8,128)(2,1)S(1)}, bf16[64,2048]{1,0:T(8,128)(2,1)S(1)}, u32[]{:S(2)}, u32[]{:S(2)}) %collective-permute-start.6) | collective-permute-done | bytes 262176 | tf_op jit(solution)/shard_map/ppermute | solution.py:304
  76.8 0.9 close.1
  77.9 6.5 %collective-permute-done.8.refs_2_ = bf16[64,2176]{1,0:T(8,128)(2,1)} collective-permute-done((bf16[64,2176]{1,0:T(8,128)(2,1)S(1)}, bf16[64,2176]{1,0:T(8,128)(2,1)}, u32[]{:S(2)}, u32[]{:S(2)}) %collective-permute-start.8) | collective-permute-done | bytes 278560 | tf_op jit(solution)/shard_map/ppermute | solution.py:279
  84.3 2.5 %collective-permute-start.18 = (bf16[64,2176]{1,0:T(8,128)(2,1)S(1)}, bf16[64,2176]{1,0:T(8,128)(2,1)S(1)}, u32[]{:S(2)}, u32[]{:S(2)}) collective-permute-start(bf16[64,2176]{1,0:T(8,128)(2,1)S(1)} %get-tuple-element.39.refs_0_), channel_id=1, source_target_pairs={{0,16},{4,20},{8,24},{12,28},{16,0},{20,4},{24,8},{28,12},{1,17},{... | collective-permute-start | bytes 835592 | tf_op jit(solution)/shard_map/ppermute | solution.py:279
  86.9 9.3 %collective-permute-done.18.refs_0_ = bf16[64,2176]{1,0:T(8,128)(2,1)S(1)} collective-permute-done((bf16[64,2176]{1,0:T(8,128)(2,1)S(1)}, bf16[64,2176]{1,0:T(8,128)(2,1)S(1)}, u32[]{:S(2)}, u32[]{:S(2)}) %collective-permute-start.18) | collective-permute-done | bytes 278560 | tf_op jit(solution)/shard_map/ppermute | solution.py:279
  96.5 1.0 copy-done.2
  97.5 0.9 collective-permute-start.22
  98.4 0.7 copy-done.5
  99.1 4.5 %collective-permute-done.19.refs_0_ = bf16[64,2176]{1,0:T(8,128)(2,1)} collective-permute-done((bf16[64,2176]{1,0:T(8,128)(2,1)S(1)}, bf16[64,2176]{1,0:T(8,128)(2,1)}, u32[]{:S(2)}, u32[]{:S(2)}) %collective-permute-start.19) | collective-permute-done | bytes 278560 | tf_op jit(solution)/shard_map/ppermute | solution.py:279
  103.6 0.4 collective-permute-start.7
  104.0 1.2 collective-permute-done.22.refs_1_
  105.2 0.7 copy-done.7
  105.9 2.5 %collective-permute-start.9 = (bf16[64,2176]{1,0:T(8,128)(2,1)}, bf16[64,2176]{1,0:T(8,128)(2,1)}, u32[]{:S(2)}, u32[]{:S(2)}) collective-permute-start(bf16[64,2176]{1,0:T(8,128)(2,1)} %collective-permute-done.8.refs_2_), channel_id=1, source_target_pairs={{0,4},{4,0},{8,12},{12,8},{16,20},{20,16},{24,28},{28,24},{1,5},{5... | collective-permute-start | bytes 835592 | tf_op jit(solution)/shard_map/ppermute | solution.py:282
  108.5 1.2 copy-done.3
  109.7 1.0 copy-done.6
  110.7 1.0 copy-done.8
  111.6 5.3 %experts.5 = (bf16[64,2048]{1,0:T(8,128)(2,1)S(1)}, bf16[64,2048]{1,0:T(8,128)(2,1)S(1)}) custom-call(s32[4]{0:T(128)S(1)} %pad_add_fusion.places_ref, bf16[64,2176]{1,0:T(8,128)(2,1)S(1)} %copy-done.6, bf16[64,2176]{1,0:T(8,128)(2,1)S(1)} %copy-done.8, bf16[2048,512]{1,0:T(8,128)(2,1)S(1)} %bitcast.12, ...), custom_call_target="tpu_custom_call" | custom-call | flops 1610612736 | bytes 1048576 | tf_op jit(solution)/shard_map/experts/pallas_call | solution.py:473
  116.9 2.1 %collective-permute-start.23 = (bf16[64,2048]{1,0:T(8,128)(2,1)S(1)}, bf16[64,2048]{1,0:T(8,128)(2,1)S(1)}, u32[]{:S(2)}, u32[]{:S(2)}) collective-permute-start(bf16[64,2048]{1,0:T(8,128)(2,1)S(1)} %get-tuple-element.47), channel_id=1, source_target_pairs={{0,4},{4,0},{8,12},{12,8},{16,20},{20,16},{24,28},{28,24},{1,5},{5... | collective-permute-start | bytes 786440 | tf_op jit(solution)/shard_map/ppermute | solution.py:291
  119.2 7.1 %experts.3 = (bf16[64,2048]{1,0:T(8,128)(2,1)S(1)}, bf16[64,2048]{1,0:T(8,128)(2,1)S(1)}, bf16[64,2048]{1,0:T(8,128)(2,1)S(1)}, bf16[64,2048]{1,0:T(8,128)(2,1)S(1)}) custom-call(s32[4]{0:T(128)S(1)} %pad_add_fusion.places_ref, bf16[64,2176]{1,0:T(8,128)(2,1)S(1)} %get-tuple-element.39.refs_0_, bf16[64,2176]{1,0:T(8,128)(2,1)} %collective-permute-done.7.refs_1_, ...), custom_call_target="tpu_custom_call" | custom-call | flops 3221225472 | bytes 2097152 | tf_op jit(solution)/shard_map/experts/pallas_call | solution.py:473
  126.3 0.6 collective-permute-start.17
  126.9 5.3 %experts.4 = (bf16[64,2048]{1,0:T(8,128)(2,1)S(1)}, bf16[64,2048]{1,0:T(8,128)(2,1)S(1)}) custom-call(s32[4]{0:T(128)S(1)} %pad_add_fusion.places_ref, bf16[64,2176]{1,0:T(8,128)(2,1)} %collective-permute-done.19.refs_0_, bf16[64,2176]{1,0:T(8,128)(2,1)S(1)} %collective-permute-done.20.refs_1_, bf16[2048,512]{1,0:T(8,128)(2,1)S(1)} %bitcast.14, ...), custom_call_target="tpu_custom_call" | custom-call | flops 1610612736 | bytes 1048576 | tf_op jit(solution)/shard_map/experts/pallas_call | solution.py:473
  132.2 1.6 collective-permute-start.21
  133.8 0.5 collective-permute-start.16
  134.3 7.4 %collective-permute-done.21 = bf16[64,2048]{1,0:T(8,128)(2,1)S(1)} collective-permute-done((bf16[64,2048]{1,0:T(8,128)(2,1)S(1)}, bf16[64,2048]{1,0:T(8,128)(2,1)S(1)}, u32[]{:S(2)}, u32[]{:S(2)}) %collective-permute-start.21) | collective-permute-done | bytes 262176 | tf_op jit(solution)/shard_map/ppermute | solution.py:291
  141.9 1.1 collective-permute-start.26
  143.0 3.1 %collective-permute-start.25 = (bf16[64,2048]{1,0:T(8,128)(2,1)S(1)}, bf16[64,2048]{1,0:T(8,128)(2,1)S(1)}, u32[]{:S(2)}, u32[]{:S(2)}) collective-permute-start(bf16[64,2048]{1,0:T(8,128)(2,1)S(1)} %add_convert_fusion.2), channel_id=1, source_target_pairs={{24,0},{28,4},{16,8},{20,12},{8,16},{12,20},{0,24},{4,28},{25,1},{... | collective-permute-start | bytes 786440 | tf_op jit(solution)/shard_map/ppermute | solution.py:304
  146.1 6.9 %collective-permute-done.26 = bf16[64,2048]{1,0:T(8,128)(2,1)S(1)} collective-permute-done((bf16[64,2048]{1,0:T(8,128)(2,1)S(1)}, bf16[64,2048]{1,0:T(8,128)(2,1)S(1)}, u32[]{:S(2)}, u32[]{:S(2)}) %collective-permute-start.26) | collective-permute-done | bytes 262176 | tf_op jit(solution)/shard_map/ppermute | solution.py:304
  153.0 4.5 %collective-permute-done.25 = bf16[64,2048]{1,0:T(8,128)(2,1)S(1)} collective-permute-done((bf16[64,2048]{1,0:T(8,128)(2,1)S(1)}, bf16[64,2048]{1,0:T(8,128)(2,1)S(1)}, u32[]{:S(2)}, u32[]{:S(2)}) %collective-permute-start.25) | collective-permute-done | bytes 262176 | tf_op jit(solution)/shard_map/ppermute | solution.py:304
  157.5 7.9 %collective-permute-done.24 = bf16[64,2048]{1,0:T(8,128)(2,1)S(1)} collective-permute-done((bf16[64,2048]{1,0:T(8,128)(2,1)S(1)}, bf16[64,2048]{1,0:T(8,128)(2,1)S(1)}, u32[]{:S(2)}, u32[]{:S(2)}) %collective-permute-start.24) | collective-permute-done | bytes 262176 | tf_op jit(solution)/shard_map/ppermute | solution.py:304
  165.5 0.9 add_convert_fusion
  (60 shorter events, 1.5 us)
Async XLA Ops:
  0.6 49.8 %collective-permute-start.11 = (bf16[2048,512]{1,0:T(8,128)(2,1)}, bf16[2048,512]{1,0:T(8,128)(2,1)}, u32[]{:S(2)}, u32[]{:S(2)}) collective-permute-start(bf16[2048,512]{1,0:T(8,128)(2,1)} %bitcast.10), channel_id=1, source_target_pairs={{0,2},{1,3},{2,0},{3,1},{4,6},{5,7},{6,4},{7,5},{8,10},{9,11},{10,... | collective-permute-start | bytes 6291464 | tf_op jit(solution)/shard_map/ppermute | solution.py:279
  3.7 104.8 %collective-permute-start.10 = (bf16[2048,512]{1,0:T(8,128)(2,1)}, bf16[2048,512]{1,0:T(8,128)(2,1)}, u32[]{:S(2)}, u32[]{:S(2)}) collective-permute-start(bf16[2048,512]{1,0:T(8,128)(2,1)} %bitcast.11), channel_id=1, source_target_pairs={{0,1},{1,0},{2,3},{3,2},{4,5},{5,4},{6,7},{7,6},{8,9},{9,8},{10,11... | collective-permute-start | bytes 6291464 | tf_op jit(solution)/shard_map/ppermute | solution.py:282
  3.7 20.9 %copy-start.14 = (f32[64,10]{0,1:T(8,128)S(1)}, f32[64,10]{0,1:T(8,128)}, u32[]{:S(2)}) copy-start(f32[64,10]{0,1:T(8,128)} %param.29) | copy-start | bytes 7684
  3.7 20.9 %copy-start.15 = (s32[64,10]{0,1:T(8,128)S(1)}, s32[64,10]{0,1:T(8,128)}, u32[]{:S(2)}) copy-start(s32[64,10]{0,1:T(8,128)} %param.28) | copy-start | bytes 7684
  3.7 37.5 %copy-start.1 = (bf16[1,256,2048]{2,1,0:T(8,128)(2,1)S(1)}, bf16[1,256,2048]{2,1,0:T(8,128)(2,1)}, u32[]{:S(2)}) copy-start(bf16[1,256,2048]{2,1,0:T(8,128)(2,1)} %param.31) | copy-start | bytes 3145732
  20.9 51.2 %copy-start.10 = (bf16[64,2048]{1,0:T(8,128)(2,1)S(1)}, bf16[64,2048]{1,0:T(8,128)(2,1)}, u32[]{:S(2)}) copy-start(bf16[64,2048]{1,0:T(8,128)(2,1)} %param.26) | copy-start | bytes 786436
  20.9 55.8 %copy-start.9 = (f32[2048]{0:T(1024)S(1)}, f32[2048]{0:T(1024)}, u32[]{:S(2)}) copy-start(f32[2048]{0:T(1024)} %param.27) | copy-start | bytes 24580
  21.0 23.4 %collective-permute-start.1 = (bf16[64,2048]{1,0:T(8,128)(2,1)}, bf16[64,2048]{1,0:T(8,128)(2,1)S(1)}, u32[]{:S(2)}, u32[]{:S(2)}) collective-permute-start(bf16[64,2048]{1,0:T(8,128)(2,1)} %get-tuple-element.31), channel_id=1, source_target_pairs={{0,4},{4,0},{8,12},{12,8},{16,20},{20,16},{24,28},{28,24},{1,5},{5... | collective-permute-start | bytes 786440 | tf_op jit(solution)/shard_map/ppermute | solution.py:291
  22.5 20.0 %collective-permute-start.2 = (bf16[64,2048]{1,0:T(8,128)(2,1)}, bf16[64,2048]{1,0:T(8,128)(2,1)S(1)}, u32[]{:S(2)}, u32[]{:S(2)}) collective-permute-start(bf16[64,2048]{1,0:T(8,128)(2,1)} %get-tuple-element.33), channel_id=1, source_target_pairs={{0,4},{4,0},{8,12},{12,8},{16,20},{20,16},{24,28},{28,24},{1,5},{5... | collective-permute-start | bytes 786440 | tf_op jit(solution)/shard_map/ppermute | solution.py:291
  23.1 18.1 %collective-permute-start.3 = (bf16[64,2048]{1,0:T(8,128)(2,1)}, bf16[64,2048]{1,0:T(8,128)(2,1)S(1)}, u32[]{:S(2)}, u32[]{:S(2)}) collective-permute-start(bf16[64,2048]{1,0:T(8,128)(2,1)} %get-tuple-element.35), channel_id=1, source_target_pairs={{0,4},{4,0},{8,12},{12,8},{16,20},{20,16},{24,28},{28,24},{1,5},{5... | collective-permute-start | bytes 786440 | tf_op jit(solution)/shard_map/ppermute | solution.py:291
  24.8 47.3 %copy-start.11 = (bf16[64,2048]{1,0:T(8,128)(2,1)S(1)}, bf16[64,2048]{1,0:T(8,128)(2,1)}, u32[]{:S(2)}) copy-start(bf16[64,2048]{1,0:T(8,128)(2,1)} %get-tuple-element.28) | copy-start | bytes 786436
  41.2 30.9 %collective-permute-start.14 = (bf16[256,2048]{1,0:T(8,128)(2,1)S(1)}, bf16[256,2048]{1,0:T(8,128)(2,1)}, u32[]{:S(2)}, u32[]{:S(2)}) collective-permute-start(bf16[256,2048]{1,0:T(8,128)(2,1)S(1)} %bitcast.15), channel_id=1, source_target_pairs={{0,2},{1,3},{2,0},{3,1},{4,6},{5,7},{6,4},{7,5},{8,10},{9,11},{10,... | collective-permute-start | bytes 3145736 | tf_op jit(solution)/shard_map/ppermute | solution.py:279
  42.5 8.0 %copy-start.13 = (bf16[64,2048]{1,0:T(8,128)(2,1)}, bf16[64,2048]{1,0:T(8,128)(2,1)S(1)}, u32[]{:S(2)}) copy-start(bf16[64,2048]{1,0:T(8,128)(2,1)S(1)} %collective-permute-done.2) | copy-start | bytes 786436
  42.5 9.2 %collective-permute-start = (bf16[64,2048]{1,0:T(8,128)(2,1)}, bf16[64,2048]{1,0:T(8,128)(2,1)S(1)}, u32[]{:S(2)}, u32[]{:S(2)}) collective-permute-start(bf16[64,2048]{1,0:T(8,128)(2,1)} %get-tuple-element.29), channel_id=1, source_target_pairs={{0,4},{4,0},{8,12},{12,8},{16,20},{20,16},{24,28},{28,24},{1,5},{5... | collective-permute-start | bytes 786440 | tf_op jit(solution)/shard_map/ppermute | solution.py:291
  44.3 6.1 %copy-start.12 = (bf16[64,2048]{1,0:T(8,128)(2,1)}, bf16[64,2048]{1,0:T(8,128)(2,1)S(1)}, u32[]{:S(2)}) copy-start(bf16[64,2048]{1,0:T(8,128)(2,1)S(1)} %collective-permute-done.1) | copy-start | bytes 786436
  44.3 9.3 %collective-permute-start.4 = (bf16[64,2048]{1,0:T(8,128)(2,1)S(1)}, bf16[64,2048]{1,0:T(8,128)(2,1)S(1)}, u32[]{:S(2)}, u32[]{:S(2)}) collective-permute-start(bf16[64,2048]{1,0:T(8,128)(2,1)S(1)} %add_convert_fusion.6), channel_id=1, source_target_pairs={{24,0},{28,4},{16,8},{20,12},{8,16},{12,20},{0,24},{4,28},{25,1},{... | collective-permute-start | bytes 786440 | tf_op jit(solution)/shard_map/ppermute | solution.py:304
  50.5 58.0 %collective-permute-start.12 = (bf16[2048,512]{1,0:T(8,128)(2,1)}, bf16[2048,512]{1,0:T(8,128)(2,1)}, u32[]{:S(2)}, u32[]{:S(2)}) collective-permute-start(bf16[2048,512]{1,0:T(8,128)(2,1)} %collective-permute-done.11.refs_6_.refs_4_), channel_id=1, source_target_pairs={{0,1},{1,0},{2,3},{3,2},{4,5},{5,4},{6,7},{7,6},{8,9},{9,8},{10,11... | collective-permute-start | bytes 6291464 | tf_op jit(solution)/shard_map/ppermute | solution.py:282
  50.5 58.0 %copy-start = (bf16[1,2048,512]{2,1,0:T(8,128)(2,1)S(1)}, bf16[1,2048,512]{2,1,0:T(8,128)(2,1)}, u32[]{:S(2)}) copy-start(bf16[1,2048,512]{2,1,0:T(8,128)(2,1)} %param.30) | copy-start | bytes 6291460
  51.7 44.8 %collective-permute-start.13 = (bf16[256,2048]{1,0:T(8,128)(2,1)S(1)}, bf16[256,2048]{1,0:T(8,128)(2,1)S(1)}, u32[]{:S(2)}, u32[]{:S(2)}) collective-permute-start(bf16[256,2048]{1,0:T(8,128)(2,1)S(1)} %bitcast.16), channel_id=1, source_target_pairs={{0,1},{1,0},{2,3},{3,2},{4,5},{5,4},{6,7},{7,6},{8,9},{9,8},{10,11... | collective-permute-start | bytes 3145736 | tf_op jit(solution)/shard_map/ppermute | solution.py:282
  53.7 16.7 %collective-permute-start.5 = (bf16[64,2048]{1,0:T(8,128)(2,1)S(1)}, bf16[64,2048]{1,0:T(8,128)(2,1)S(1)}, u32[]{:S(2)}, u32[]{:S(2)}) collective-permute-start(bf16[64,2048]{1,0:T(8,128)(2,1)S(1)} %add_convert_fusion.5), channel_id=1, source_target_pairs={{16,0},{20,4},{24,8},{28,12},{0,16},{4,20},{8,24},{12,28},{17,1},{... | collective-permute-start | bytes 786440 | tf_op jit(solution)/shard_map/ppermute | solution.py:304
  70.4 6.4 %collective-permute-start.6 = (bf16[64,2048]{1,0:T(8,128)(2,1)S(1)}, bf16[64,2048]{1,0:T(8,128)(2,1)S(1)}, u32[]{:S(2)}, u32[]{:S(2)}) collective-permute-start(bf16[64,2048]{1,0:T(8,128)(2,1)S(1)} %add_convert_fusion.4), channel_id=1, source_target_pairs={{8,0},{12,4},{0,8},{4,12},{24,16},{28,20},{16,24},{20,28},{9,1},{1... | collective-permute-start | bytes 786440 | tf_op jit(solution)/shard_map/ppermute | solution.py:304
  72.1 36.4 %collective-permute-start.15 = (bf16[256,2048]{1,0:T(8,128)(2,1)}, bf16[256,2048]{1,0:T(8,128)(2,1)}, u32[]{:S(2)}, u32[]{:S(2)}) collective-permute-start(bf16[256,2048]{1,0:T(8,128)(2,1)} %collective-permute-done.14.refs_10_.refs_8_), channel_id=1, source_target_pairs={{0,1},{1,0},{2,3},{3,2},{4,5},{5,4},{6,7},{7,6},{8,9},{9,8},{10,11... | collective-permute-start | bytes 3145736 | tf_op jit(solution)/shard_map/ppermute | solution.py:282
  77.7 6.7 %collective-permute-start.8 = (bf16[64,2176]{1,0:T(8,128)(2,1)S(1)}, bf16[64,2176]{1,0:T(8,128)(2,1)}, u32[]{:S(2)}, u32[]{:S(2)}) collective-permute-start(bf16[64,2176]{1,0:T(8,128)(2,1)S(1)} %get-tuple-element.39.refs_0_), channel_id=1, source_target_pairs={{0,8},{4,12},{8,0},{12,4},{16,24},{20,28},{24,16},{28,20},{1,9},{5... | collective-permute-start | bytes 835592 | tf_op jit(solution)/shard_map/ppermute | solution.py:279
  84.3 11.9 %collective-permute-start.18 = (bf16[64,2176]{1,0:T(8,128)(2,1)S(1)}, bf16[64,2176]{1,0:T(8,128)(2,1)S(1)}, u32[]{:S(2)}, u32[]{:S(2)}) collective-permute-start(bf16[64,2176]{1,0:T(8,128)(2,1)S(1)} %get-tuple-element.39.refs_0_), channel_id=1, source_target_pairs={{0,16},{4,20},{8,24},{12,28},{16,0},{20,4},{24,8},{28,12},{1,17},{... | collective-permute-start | bytes 835592 | tf_op jit(solution)/shard_map/ppermute | solution.py:279
  96.2 7.4 %collective-permute-start.19 = (bf16[64,2176]{1,0:T(8,128)(2,1)S(1)}, bf16[64,2176]{1,0:T(8,128)(2,1)}, u32[]{:S(2)}, u32[]{:S(2)}) collective-permute-start(bf16[64,2176]{1,0:T(8,128)(2,1)S(1)} %collective-permute-done.18.refs_0_), channel_id=1, source_target_pairs={{0,8},{4,12},{8,0},{12,4},{16,24},{20,28},{24,16},{28,20},{1,9},{5... | collective-permute-start | bytes 835592 | tf_op jit(solution)/shard_map/ppermute | solution.py:279
  96.5 1.0 copy-start.2
  97.5 7.7 %collective-permute-start.22 = (bf16[64,2176]{1,0:T(8,128)(2,1)S(1)}, bf16[64,2176]{1,0:T(8,128)(2,1)S(1)}, u32[]{:S(2)}, u32[]{:S(2)}) collective-permute-start(bf16[64,2176]{1,0:T(8,128)(2,1)S(1)} %collective-permute-done.18.refs_0_), channel_id=1, source_target_pairs={{0,4},{4,0},{8,12},{12,8},{16,20},{20,16},{24,28},{28,24},{1,5},{5... | collective-permute-start | bytes 835592 | tf_op jit(solution)/shard_map/ppermute | solution.py:282
  98.4 0.7 copy-start.5
  103.6 15.4 %collective-permute-start.7 = (bf16[64,2176]{1,0:T(8,128)(2,1)S(1)}, bf16[64,2176]{1,0:T(8,128)(2,1)}, u32[]{:S(2)}, u32[]{:S(2)}) collective-permute-start(bf16[64,2176]{1,0:T(8,128)(2,1)S(1)} %get-tuple-element.39.refs_0_), channel_id=1, source_target_pairs={{0,4},{4,0},{8,12},{12,8},{16,20},{20,16},{24,28},{28,24},{1,5},{5... | collective-permute-start | bytes 835592 | tf_op jit(solution)/shard_map/ppermute | solution.py:282
  105.2 0.7 copy-start.7
  105.9 13.3 %collective-permute-start.9 = (bf16[64,2176]{1,0:T(8,128)(2,1)}, bf16[64,2176]{1,0:T(8,128)(2,1)}, u32[]{:S(2)}, u32[]{:S(2)}) collective-permute-start(bf16[64,2176]{1,0:T(8,128)(2,1)} %collective-permute-done.8.refs_2_), channel_id=1, source_target_pairs={{0,4},{4,0},{8,12},{12,8},{16,20},{20,16},{24,28},{28,24},{1,5},{5... | collective-permute-start | bytes 835592 | tf_op jit(solution)/shard_map/ppermute | solution.py:282
  108.4 18.4 %collective-permute-start.20 = (bf16[64,2176]{1,0:T(8,128)(2,1)}, bf16[64,2176]{1,0:T(8,128)(2,1)S(1)}, u32[]{:S(2)}, u32[]{:S(2)}) collective-permute-start(bf16[64,2176]{1,0:T(8,128)(2,1)} %collective-permute-done.19.refs_0_), channel_id=1, source_target_pairs={{0,4},{4,0},{8,12},{12,8},{16,20},{20,16},{24,28},{28,24},{1,5},{5... | collective-permute-start | bytes 835592 | tf_op jit(solution)/shard_map/ppermute | solution.py:282
  108.5 1.2 copy-start.3
  109.7 1.0 copy-start.6
  110.7 1.0 copy-start.8
  111.6 7.6 %copy-start.4 = (bf16[256,2048]{1,0:T(8,128)(2,1)S(1)}, bf16[256,2048]{1,0:T(8,128)(2,1)}, u32[]{:S(2)}) copy-start(bf16[256,2048]{1,0:T(8,128)(2,1)} %copy-done.2) | copy-start | bytes 3145732
  116.9 17.3 %collective-permute-start.23 = (bf16[64,2048]{1,0:T(8,128)(2,1)S(1)}, bf16[64,2048]{1,0:T(8,128)(2,1)S(1)}, u32[]{:S(2)}, u32[]{:S(2)}) collective-permute-start(bf16[64,2048]{1,0:T(8,128)(2,1)S(1)} %get-tuple-element.47), channel_id=1, source_target_pairs={{0,4},{4,0},{8,12},{12,8},{16,20},{20,16},{24,28},{28,24},{1,5},{5... | collective-permute-start | bytes 786440 | tf_op jit(solution)/shard_map/ppermute | solution.py:291
  126.3 15.6 %collective-permute-start.17 = (bf16[64,2048]{1,0:T(8,128)(2,1)S(1)}, bf16[64,2048]{1,0:T(8,128)(2,1)S(1)}, u32[]{:S(2)}, u32[]{:S(2)}) collective-permute-start(bf16[64,2048]{1,0:T(8,128)(2,1)S(1)} %get-tuple-element.43), channel_id=1, source_target_pairs={{0,4},{4,0},{8,12},{12,8},{16,20},{20,16},{24,28},{28,24},{1,5},{5... | collective-permute-start | bytes 786440 | tf_op jit(solution)/shard_map/ppermute | solution.py:291
  132.2 9.6 %collective-permute-start.21 = (bf16[64,2048]{1,0:T(8,128)(2,1)S(1)}, bf16[64,2048]{1,0:T(8,128)(2,1)S(1)}, u32[]{:S(2)}, u32[]{:S(2)}) collective-permute-start(bf16[64,2048]{1,0:T(8,128)(2,1)S(1)} %get-tuple-element.45), channel_id=1, source_target_pairs={{0,4},{4,0},{8,12},{12,8},{16,20},{20,16},{24,28},{28,24},{1,5},{5... | collective-permute-start | bytes 786440 | tf_op jit(solution)/shard_map/ppermute | solution.py:291
  133.8 12.4 %collective-permute-start.16 = (bf16[64,2048]{1,0:T(8,128)(2,1)S(1)}, bf16[64,2048]{1,0:T(8,128)(2,1)S(1)}, u32[]{:S(2)}, u32[]{:S(2)}) collective-permute-start(bf16[64,2048]{1,0:T(8,128)(2,1)S(1)} %get-tuple-element.41), channel_id=1, source_target_pairs={{0,4},{4,0},{8,12},{12,8},{16,20},{20,16},{24,28},{28,24},{1,5},{5... | collective-permute-start | bytes 786440 | tf_op jit(solution)/shard_map/ppermute | solution.py:291
  141.9 11.1 %collective-permute-start.26 = (bf16[64,2048]{1,0:T(8,128)(2,1)S(1)}, bf16[64,2048]{1,0:T(8,128)(2,1)S(1)}, u32[]{:S(2)}, u32[]{:S(2)}) collective-permute-start(bf16[64,2048]{1,0:T(8,128)(2,1)S(1)} %add_convert_fusion.1), channel_id=1, source_target_pairs={{8,0},{12,4},{0,8},{4,12},{24,16},{28,20},{16,24},{20,28},{9,1},{1... | collective-permute-start | bytes 786440 | tf_op jit(solution)/shard_map/ppermute | solution.py:304
  143.0 14.5 %collective-permute-start.25 = (bf16[64,2048]{1,0:T(8,128)(2,1)S(1)}, bf16[64,2048]{1,0:T(8,128)(2,1)S(1)}, u32[]{:S(2)}, u32[]{:S(2)}) collective-permute-start(bf16[64,2048]{1,0:T(8,128)(2,1)S(1)} %add_convert_fusion.2), channel_id=1, source_target_pairs={{24,0},{28,4},{16,8},{20,12},{8,16},{12,20},{0,24},{4,28},{25,1},{... | collective-permute-start | bytes 786440 | tf_op jit(solution)/shard_map/ppermute | solution.py:304
  146.1 19.3 %collective-permute-start.24 = (bf16[64,2048]{1,0:T(8,128)(2,1)S(1)}, bf16[64,2048]{1,0:T(8,128)(2,1)S(1)}, u32[]{:S(2)}, u32[]{:S(2)}) collective-permute-start(bf16[64,2048]{1,0:T(8,128)(2,1)S(1)} %add_convert_fusion.3), channel_id=1, source_target_pairs={{16,0},{20,4},{24,8},{28,12},{0,16},{4,20},{8,24},{12,28},{17,1},{... | collective-permute-start | bytes 786440 | tf_op jit(solution)/shard_map/ppermute | solution.py:304

commit v6 on v5

--- a/solution.py
+++ b/solution.py
@@ -10,7 +10,7 @@
 
 epsilon = 1e-06
 chunk_rows = 128
-chunks_per_step = 2
+chunks_per_step = 4
 
 
 def product(left, right, contract=((1,), (0,))):
@@ -268,7 +268,7 @@
     return [(target, origin) for origin, target in pairs]
 
 
-def gather_parts(block, axis):
+def gather_parts(block, axis, around=False):
     high, low = factors(lax.axis_size(axis))
     parts = [[block]]
     for step in range(1, high):
@@ -278,8 +278,11 @@
             sent, hop = block, step
         parts.append([lax.ppermute(sent, axis, high_pairs(high, low, hop))])
     if low == 2:
-        for row in parts:
-            row.append(lax.ppermute(row[0], axis, low_pairs(high, low)))
+        for step, row in enumerate(parts):
+            if around and step == 1:
+                row.append(lax.ppermute(parts[0][1], axis, high_pairs(high, low, step)))
+            else:
+                row.append(lax.ppermute(row[0], axis, low_pairs(high, low)))
     return parts
 
 
@@ -366,10 +369,13 @@
         tok_local,
     )
     high, low = factors(lax.axis_size("expert"))
+    half = high // 2
+    middle = half + (high - half) // 2
+    groups = [range(half, middle), range(middle, high), range(half)]
     own, rest = scatter_parts(
         [share[step * low : (step + 1) * low] for step in range(high)],
         "expert",
-        range(high - 1, -1, -1),
+        [*groups[0], *groups[1], *reversed(groups[2])],
     )
     expert_range = jnp.arange(experts_all, dtype=jnp.int32)
     mixing = jnp.sum(
@@ -384,11 +390,16 @@
         post_gain,
         jnp.concatenate([coarse, fine, pad], axis=1),
     )
-    gathered = gather_parts(block, "expert")
+    gathered = gather_parts(block, "expert", around=True)
+    slots = len(gate_up_parts)
+    late = max(1, slots - factors(lax.axis_size("dp"))[1] + 1)
+    held = [[gate_up_parts[0], down_parts[0]]]
+    for part in (slice(1, late), slice(late, slots)):
+        arrays = gate_up_parts[part] + down_parts[part]
+        held.append(hold(arrays) if arrays else arrays)
+    gate_up_parts = sum([list(part[: len(part) // 2]) for part in held], [])
+    down_parts = sum([list(part[len(part) // 2 :]) for part in held], [])
     places = jnp.stack(expert_of).astype(jnp.int32)
-    half = high // 2
-    middle = half + (high - half) // 2
-    groups = [range(half, middle), range(middle, high), range(half)]
     results = {}
     for group in groups:
         blocks = [(step, j) for step in group for j in range(low)]
@@ -435,6 +446,30 @@
         compiler_params=pltpu.CompilerParams(vmem_limit_bytes=8 << 20),
         name="close",
     )(base, *rest, post_gain[None], mixing)
+
+
+def hold_kernel(*refs):
+    count = (len(refs) - 1) // 2
+    loads = [
+        pltpu.make_async_copy(refs[n], refs[count + n], refs[-1].at[n]) for n in range(count)
+    ]
+    for load in loads:
+        load.start()
+    for load in loads:
+        load.wait()
+
+
+def hold(arrays):
+    count = len(arrays)
+    return pl.pallas_call(
+        hold_kernel,
+        in_specs=[pl.BlockSpec(memory_space=pltpu.HBM)] * count,
+        out_specs=[pl.BlockSpec(memory_space=pltpu.VMEM)] * count,
+        out_shape=[pltpu.VMEM(array.shape, array.dtype) for array in arrays],
+        scratch_shapes=[pltpu.SemaphoreType.DMA((count,))],
+        compiler_params=pltpu.CompilerParams(vmem_limit_bytes=16 << 20),
+        name="hold",
+    )(*arrays)
 
 
 def experts_kernel(blocks, slots, experts_all, places_ref, *refs):

time: 167 us -> 166 us (level)
  waiting for transfers between devices: 84.3 us -> 93.3 us
  starting transfers between devices: 34.9 us -> 29.4 us
  Pallas kernels: 35.8 us -> 31.4 us
  other arithmetic: 4.73 us -> 7.7 us
  local copies, waits for them, and re-layouts: 5.81 us -> 3.45 us
    ppermute x5, waiting for transfers between devices: 24.5 us -> 32.4 us  [gather_parts(): parts.append([lax.ppermute(sent, axis, high_pairs(high, low, hop))])]
    pallas_call x3, Pallas kernels: 17.7 us -> 10.3 us  [experts(): pl.pallas_call(functools.partial(experts_kernel, blocks, slots, experts_a...]
    ppermute x6, waiting for transfers between devices: 34.7 us -> 41.6 us  [scatter_parts(): lax.ppermute(before, axis, reverse(high_pairs(high, low, step)))]
    ppermute x8, waiting for transfers between devices: 23.6 us -> 19.1 us  [scatter_parts(): near[step] = lax.ppermute(parts[step][1], axis, low_pairs(high, low))]
    pallas_call x0 -> x2, Pallas kernels: none -> 4.4 us  [hold(): pl.pallas_call(hold_kernel, in_specs=[pl.BlockSpec(memory_space=pltpu.HBM...]
    ppermute x6, starting transfers between devices: 14 us -> 10.3 us  [scatter_parts(): lax.ppermute(before, axis, reverse(high_pairs(high, low, step)))]
    ppermute x5, starting transfers between devices: 6.32 us -> 3.42 us  [gather_parts(): parts.append([lax.ppermute(sent, axis, high_pairs(high, low, hop))])]
    unnamed x32 -> x18, local copies, waits for them, and re-layouts: 5.55 us -> 3.19 us
  transfers between devices with their start and end apart: 27 -> 27, of which waited for: 15 -> 16; matrix products, arithmetic and copies ran while one was open for 2% -> 4% of each run, Pallas kernels for 22% -> 19%
where the time goes in v6:
time: 166 us
  waiting for transfers between devices  93.3 us (56%)
  Pallas kernels  31.4 us (19%)
  starting transfers between devices  29.4 us (18%)
  other arithmetic  7.7 us (5%)
  local copies, waits for them, and re-layouts  3.45 us (2%)
    ppermute x6, waiting for transfers between devices, scatter_parts(): lax.ppermute(before, axis, reverse(high_pairs(high, low, step)))  41.6 us
    ppermute x5, waiting for transfers between devices, gather_parts(): parts.append([lax.ppermute(sent, axis, high_pairs(high, low, hop))])  32.4 us
    ppermute x8, waiting for transfers between devices, scatter_parts(): near[step] = lax.ppermute(parts[step][1], axis, low_pairs(high, low))  19.1 us
    pallas_call x1, Pallas kernels, mix(): pl.pallas_call(functools.partial(mix_kernel, heads, requests, owned, rows...  15.9 us
    ppermute x8, starting transfers between devices, scatter_parts(): near[step] = lax.ppermute(parts[step][1], axis, low_pairs(high, low))  10.4 us
    pallas_call x3, Pallas kernels, experts(): pl.pallas_call(functools.partial(experts_kernel, blocks, slots, experts_a...  10.3 us
    ppermute x6, starting transfers between devices, scatter_parts(): lax.ppermute(before, axis, reverse(high_pairs(high, low, step)))  10.3 us
    convert_element_type x6, other arithmetic, scatter_parts(): before = sum_parts(pair).astype(jnp.bfloat16)  5.42 us
  transfers between devices with their start and end apart: 27, of which 16 were waited for; matrix products, arithmetic and copies ran while one was open for 4% of the time, Pallas kernels for 19%

profile of v6, /device:TPU:0, one launch (start us, length us, event | category | flops | bytes accessed | tf_op | source)
XLA Modules:
  0.0 166.0 jit_solution(2074362769897179333)
XLA Ops:
  0.6 3.0 %collective-permute-start.11 = (bf16[2048,512]{1,0:T(8,128)(2,1)}, bf16[2048,512]{1,0:T(8,128)(2,1)}, u32[]{:S(2)}, u32[]{:S(2)}) collective-permute-start(bf16[2048,512]{1,0:T(8,128)(2,1)} %bitcast.10), channel_id=1, source_target_pairs={{0,2},{1,3},{2,0},{3,1},{4,6},{5,7},{6,4},{7,5},{8,10},{9,11},{10,... | collective-permute-start | bytes 6291464 | tf_op jit(solution)/shard_map/ppermute | solution.py:279
  3.7 15.9 %mix.1 = (f32[4,4,128,128]{3,2,1,0:T(8,128)}, bf16[64,2048]{1,0:T(8,128)(2,1)}, bf16[64,2048]{1,0:T(8,128)(2,1)}, bf16[64,2048]{1,0:T(8,128)(2,1)}, bf16[64,2048...) custom-call(bf16[512,512]{1,0:T(8,128)(2,1)} %query_ref.1, ...), custom_call_target="tpu_custom_call" | custom-call | flops 5368709120 | bytes 3145728 | tf_op jit(solution)/shard_map/mix/pallas_call | solution.py:201
  19.6 1.6 collective-permute-start.3
  21.7 1.5 collective-permute-start.1
  23.2 5.8 %collective-permute-done.3 = bf16[64,2048]{1,0:T(8,128)(2,1)S(1)} collective-permute-done((bf16[64,2048]{1,0:T(8,128)(2,1)}, bf16[64,2048]{1,0:T(8,128)(2,1)S(1)}, u32[]{:S(2)}, u32[]{:S(2)}) %collective-permute-start.3) | collective-permute-done | bytes 262176 | tf_op jit(solution)/shard_map/ppermute | solution.py:294
  29.0 1.5 collective-permute-start
  30.5 1.7 %add_convert_fusion.6 = bf16[64,2048]{1,0:T(8,128)(2,1)} fusion(bf16[64,2048]{1,0:T(8,128)(2,1)S(1)} %collective-permute-done.3, bf16[64,2048]{1,0:T(8,128)(2,1)} %get-tuple-element.40), kind=kLoop, calls=%fused_computation.7 | loop fusion | flops 524288 | bytes 786432 | tf_op jit(solution)/shard_map/convert_element_type | solution.py:306
  32.3 2.4 %collective-permute-done.2 = bf16[64,2048]{1,0:T(8,128)(2,1)S(1)} collective-permute-done((bf16[64,2048]{1,0:T(8,128)(2,1)}, bf16[64,2048]{1,0:T(8,128)(2,1)S(1)}, u32[]{:S(2)}, u32[]{:S(2)}) %collective-permute-start.2) | collective-permute-done | bytes 262176 | tf_op jit(solution)/shard_map/ppermute | solution.py:294
  34.7 1.7 %add_convert_fusion.5 = bf16[64,2048]{1,0:T(8,128)(2,1)} fusion(bf16[64,2048]{1,0:T(8,128)(2,1)S(1)} %collective-permute-done.2, bf16[64,2048]{1,0:T(8,128)(2,1)} %get-tuple-element.38), kind=kLoop, calls=%fused_computation.6 | loop fusion | flops 524288 | bytes 786432 | tf_op jit(solution)/shard_map/convert_element_type | solution.py:306
  36.4 3.8 %collective-permute-done.1 = bf16[64,2048]{1,0:T(8,128)(2,1)S(1)} collective-permute-done((bf16[64,2048]{1,0:T(8,128)(2,1)}, bf16[64,2048]{1,0:T(8,128)(2,1)S(1)}, u32[]{:S(2)}, u32[]{:S(2)}) %collective-permute-start.1) | collective-permute-done | bytes 262176 | tf_op jit(solution)/shard_map/ppermute | solution.py:294
  40.3 10.2 %collective-permute-done.11.refs_1_ = bf16[2048,512]{1,0:T(8,128)(2,1)} collective-permute-done((bf16[2048,512]{1,0:T(8,128)(2,1)}, bf16[2048,512]{1,0:T(8,128)(2,1)}, u32[]{:S(2)}, u32[]{:S(2)}) %collective-permute-start.11) | collective-permute-done | bytes 2097184 | tf_op jit(solution)/shard_map/ppermute | solution.py:279
  50.5 1.8 %add_convert_fusion.4 = bf16[64,2048]{1,0:T(8,128)(2,1)} fusion(bf16[64,2048]{1,0:T(8,128)(2,1)S(1)} %collective-permute-done.1, bf16[64,2048]{1,0:T(8,128)(2,1)} %get-tuple-element.36), kind=kLoop, calls=%fused_computation.5 | loop fusion | flops 524288 | bytes 786432 | tf_op jit(solution)/shard_map/convert_element_type | solution.py:306
  52.2 2.1 %collective-permute-start.6 = (bf16[64,2048]{1,0:T(8,128)(2,1)}, bf16[64,2048]{1,0:T(8,128)(2,1)S(1)}, u32[]{:S(2)}, u32[]{:S(2)}) collective-permute-start(bf16[64,2048]{1,0:T(8,128)(2,1)} %add_convert_fusion.4), channel_id=1, source_target_pairs={{8,0},{12,4},{0,8},{4,12},{24,16},{28,20},{16,24},{20,28},{9,1},{1... | collective-permute-start | bytes 786440 | tf_op jit(solution)/shard_map/ppermute | solution.py:307
  54.6 2.5 %collective-permute-start.5 = (bf16[64,2048]{1,0:T(8,128)(2,1)}, bf16[64,2048]{1,0:T(8,128)(2,1)S(1)}, u32[]{:S(2)}, u32[]{:S(2)}) collective-permute-start(bf16[64,2048]{1,0:T(8,128)(2,1)} %add_convert_fusion.5), channel_id=1, source_target_pairs={{24,0},{28,4},{16,8},{20,12},{8,16},{12,20},{0,24},{4,28},{25,1},{... | collective-permute-start | bytes 786440 | tf_op jit(solution)/shard_map/ppermute | solution.py:307
  57.2 4.3 %collective-permute-done.6.refs_2_ = bf16[64,2048]{1,0:T(8,128)(2,1)S(1)} collective-permute-done((bf16[64,2048]{1,0:T(8,128)(2,1)}, bf16[64,2048]{1,0:T(8,128)(2,1)S(1)}, u32[]{:S(2)}, u32[]{:S(2)}) %collective-permute-start.6) | collective-permute-done | bytes 262176 | tf_op jit(solution)/shard_map/ppermute | solution.py:307
  61.7 7.8 %collective-permute-done.5.refs_1_ = bf16[64,2048]{1,0:T(8,128)(2,1)S(1)} collective-permute-done((bf16[64,2048]{1,0:T(8,128)(2,1)}, bf16[64,2048]{1,0:T(8,128)(2,1)S(1)}, u32[]{:S(2)}, u32[]{:S(2)}) %collective-permute-start.5) | collective-permute-done | bytes 262176 | tf_op jit(solution)/shard_map/ppermute | solution.py:307
  69.5 2.1 %collective-permute-start.4 = (bf16[64,2048]{1,0:T(8,128)(2,1)}, bf16[64,2048]{1,0:T(8,128)(2,1)S(1)}, u32[]{:S(2)}, u32[]{:S(2)}) collective-permute-start(bf16[64,2048]{1,0:T(8,128)(2,1)} %add_convert_fusion.6), channel_id=1, source_target_pairs={{16,0},{20,4},{24,8},{28,12},{0,16},{4,20},{8,24},{12,28},{17,1},{... | collective-permute-start | bytes 786440 | tf_op jit(solution)/shard_map/ppermute | solution.py:307
  71.5 0.6 collective-permute-done.13.refs_3_
  72.1 1.2 convert_add_fusion.base_ref
  73.3 10.6 %collective-permute-done.4.refs_0_ = bf16[64,2048]{1,0:T(8,128)(2,1)S(1)} collective-permute-done((bf16[64,2048]{1,0:T(8,128)(2,1)}, bf16[64,2048]{1,0:T(8,128)(2,1)S(1)}, u32[]{:S(2)}, u32[]{:S(2)}) %collective-permute-start.4) | collective-permute-done | bytes 262176 | tf_op jit(solution)/shard_map/ppermute | solution.py:307
  83.9 0.9 copy-done.5
  84.8 0.9 close.1
  85.8 15.2 %collective-permute-done.18.refs_0_ = bf16[64,2176]{1,0:T(8,128)(2,1)} collective-permute-done((bf16[64,2176]{1,0:T(8,128)(2,1)S(1)}, bf16[64,2176]{1,0:T(8,128)(2,1)}, u32[]{:S(2)}, u32[]{:S(2)}) %collective-permute-start.18) | collective-permute-done | bytes 278560 | tf_op jit(solution)/shard_map/ppermute | solution.py:279
  101.0 1.0 copy-done.2
  102.0 1.5 collective-permute-start.7
  103.5 6.4 %collective-permute-done.19.refs_0_ = bf16[64,2176]{1,0:T(8,128)(2,1)} collective-permute-done((bf16[64,2176]{1,0:T(8,128)(2,1)}, bf16[64,2176]{1,0:T(8,128)(2,1)}, u32[]{:S(2)}, u32[]{:S(2)}) %collective-permute-start.19) | collective-permute-done | bytes 278560 | tf_op jit(solution)/shard_map/ppermute | solution.py:279
  109.9 1.5 collective-permute-start.22
  111.4 0.5 collective-permute-start.20
  112.0 1.2 copy-done.3
  113.2 2.5 %hold.2 = (bf16[2048,512]{1,0:T(8,128)(2,1)S(1)}, bf16[2048,512]{1,0:T(8,128)(2,1)S(1)}, bf16[256,2048]{1,0:T(8,128)(2,1)S(1)}, bf16[256,2048]{1,0:T(8,128)(2,1)S(1)}) custom-call(bf16[2048,512]{1,0:T(8,128)(2,1)} %collective-permute-done.10.refs_0_, bf16[2048,512]{1,0:T(8,128)(2,1)} %collective-permute-done.11.refs_1_, bf16[256,2048]{1,0:T(8,128)(2,1)S(1)} %copy-done.3, ...), custom_call_target="tpu_custom_call" | custom-call | tf_op jit(solution)/shard_map/hold/pallas_call | solution.py:464
  116.1 1.7 %collective-permute-start.9 = (bf16[64,2176]{1,0:T(8,128)(2,1)}, bf16[64,2176]{1,0:T(8,128)(2,1)S(1)}, u32[]{:S(2)}, u32[]{:S(2)}) collective-permute-start(bf16[64,2176]{1,0:T(8,128)(2,1)} %collective-permute-done.7.refs_1_), channel_id=1, source_target_pairs={{0,8},{4,12},{8,0},{12,4},{16,24},{20,28},{24,16},{28,20},{1,9},{5... | collective-permute-start | bytes 835592 | tf_op jit(solution)/shard_map/ppermute | solution.py:283
  117.9 1.9 %hold.3 = (bf16[2048,512]{1,0:T(8,128)(2,1)S(1)}, bf16[256,2048]{1,0:T(8,128)(2,1)S(1)}) custom-call(bf16[2048,512]{1,0:T(8,128)(2,1)} %collective-permute-done.14.refs_0_, bf16[256,2048]{1,0:T(8,128)(2,1)} %collective-permute-done.15.refs_1_), custom_call_target="tpu_custom_call" | custom-call | tf_op jit(solution)/shard_map/hold/pallas_call | solution.py:464
  119.8 2.9 %experts.5 = (bf16[64,2048]{1,0:T(8,128)(2,1)S(1)}, bf16[64,2048]{1,0:T(8,128)(2,1)S(1)}) custom-call(s32[4]{0:T(128)S(1)} %pad_add_fusion.places_ref, bf16[64,2176]{1,0:T(8,128)(2,1)} %collective-permute-done.18.refs_0_, bf16[64,2176]{1,0:T(8,128)(2,1)} %collective-permute-done.22.refs_1_, bf16[2048,512]{1,0:T(8,128)(2,1)S(1)} %bitcast.12, ...), custom_call_target="tpu_custom_call" | custom-call | flops 1610612736 | bytes 1048576 | tf_op jit(solution)/shard_map/experts/pallas_call | solution.py:508
  122.7 1.6 collective-permute-start.23
  124.3 2.9 %experts.4 = (bf16[64,2048]{1,0:T(8,128)(2,1)S(1)}, bf16[64,2048]{1,0:T(8,128)(2,1)S(1)}) custom-call(s32[4]{0:T(128)S(1)} %pad_add_fusion.places_ref, bf16[64,2176]{1,0:T(8,128)(2,1)} %collective-permute-done.19.refs_0_, bf16[64,2176]{1,0:T(8,128)(2,1)} %collective-permute-done.20.refs_1_, bf16[2048,512]{1,0:T(8,128)(2,1)S(1)} %bitcast.13, ...), custom_call_target="tpu_custom_call" | custom-call | flops 1610612736 | bytes 1048576 | tf_op jit(solution)/shard_map/experts/pallas_call | solution.py:508
  127.2 1.6 collective-permute-start.21
  129.0 4.4 %experts.3 = (bf16[64,2048]{1,0:T(8,128)(2,1)S(1)}, bf16[64,2048]{1,0:T(8,128)(2,1)S(1)}, bf16[64,2048]{1,0:T(8,128)(2,1)S(1)}, bf16[64,2048]{1,0:T(8,128)(2,1)S(1)}) custom-call(s32[4]{0:T(128)S(1)} %pad_add_fusion.places_ref, bf16[64,2176]{1,0:T(8,128)(2,1)S(1)} %get-tuple-element.45.refs_0_, bf16[64,2176]{1,0:T(8,128)(2,1)} %collective-permute-done.7.refs_1_, ...), custom_call_target="tpu_custom_call" | custom-call | flops 3221225472 | bytes 2097152 | tf_op jit(solution)/shard_map/experts/pallas_call | solution.py:508
  133.4 1.6 collective-permute-start.17
  135.0 0.5 collective-permute-start.16
  135.6 0.7 collective-permute-done.21
  136.3 6.3 %collective-permute-done.17 = bf16[64,2048]{1,0:T(8,128)(2,1)S(1)} collective-permute-done((bf16[64,2048]{1,0:T(8,128)(2,1)S(1)}, bf16[64,2048]{1,0:T(8,128)(2,1)S(1)}, u32[]{:S(2)}, u32[]{:S(2)}) %collective-permute-start.17) | collective-permute-done | bytes 262176 | tf_op jit(solution)/shard_map/ppermute | solution.py:294
  142.7 0.6 collective-permute-start.26
  143.3 1.5 collective-permute-start.25
  144.8 1.5 collective-permute-start.24
  146.3 4.0 %collective-permute-done.26 = bf16[64,2048]{1,0:T(8,128)(2,1)S(1)} collective-permute-done((bf16[64,2048]{1,0:T(8,128)(2,1)S(1)}, bf16[64,2048]{1,0:T(8,128)(2,1)S(1)}, u32[]{:S(2)}, u32[]{:S(2)}) %collective-permute-start.26) | collective-permute-done | bytes 262176 | tf_op jit(solution)/shard_map/ppermute | solution.py:307
  150.2 5.4 %collective-permute-done.25 = bf16[64,2048]{1,0:T(8,128)(2,1)S(1)} collective-permute-done((bf16[64,2048]{1,0:T(8,128)(2,1)S(1)}, bf16[64,2048]{1,0:T(8,128)(2,1)S(1)}, u32[]{:S(2)}, u32[]{:S(2)}) %collective-permute-start.25) | collective-permute-done | bytes 262176 | tf_op jit(solution)/shard_map/ppermute | solution.py:307
  155.6 9.6 %collective-permute-done.24 = bf16[64,2048]{1,0:T(8,128)(2,1)S(1)} collective-permute-done((bf16[64,2048]{1,0:T(8,128)(2,1)S(1)}, bf16[64,2048]{1,0:T(8,128)(2,1)S(1)}, u32[]{:S(2)}, u32[]{:S(2)}) %collective-permute-start.24) | collective-permute-done | bytes 262176 | tf_op jit(solution)/shard_map/ppermute | solution.py:307
  165.2 0.9 add_convert_fusion
  (48 shorter events, 1.8 us)
Async XLA Ops:
  0.6 49.8 %collective-permute-start.11 = (bf16[2048,512]{1,0:T(8,128)(2,1)}, bf16[2048,512]{1,0:T(8,128)(2,1)}, u32[]{:S(2)}, u32[]{:S(2)}) collective-permute-start(bf16[2048,512]{1,0:T(8,128)(2,1)} %bitcast.10), channel_id=1, source_target_pairs={{0,2},{1,3},{2,0},{3,1},{4,6},{5,7},{6,4},{7,5},{8,10},{9,11},{10,... | collective-permute-start | bytes 6291464 | tf_op jit(solution)/shard_map/ppermute | solution.py:279
  3.7 17.5 %copy-start = (bf16[1,2048,512]{2,1,0:T(8,128)(2,1)S(1)}, bf16[1,2048,512]{2,1,0:T(8,128)(2,1)}, u32[]{:S(2)}) copy-start(bf16[1,2048,512]{2,1,0:T(8,128)(2,1)} %param.30) | copy-start | bytes 6291460
  3.7 31.0 %copy-start.1 = (bf16[1,256,2048]{2,1,0:T(8,128)(2,1)S(1)}, bf16[1,256,2048]{2,1,0:T(8,128)(2,1)}, u32[]{:S(2)}) copy-start(bf16[1,256,2048]{2,1,0:T(8,128)(2,1)} %param.31) | copy-start | bytes 3145732
  19.5 34.8 %copy-start.7 = (f32[64,10]{0,1:T(8,128)S(1)}, f32[64,10]{0,1:T(8,128)}, u32[]{:S(2)}) copy-start(f32[64,10]{0,1:T(8,128)} %param.29) | copy-start | bytes 7684
  19.5 34.8 %copy-start.8 = (s32[64,10]{0,1:T(8,128)S(1)}, s32[64,10]{0,1:T(8,128)}, u32[]{:S(2)}) copy-start(s32[64,10]{0,1:T(8,128)} %param.28) | copy-start | bytes 7684
  19.5 64.3 %copy-start.6 = (f32[2048]{0:T(1024)S(1)}, f32[2048]{0:T(1024)}, u32[]{:S(2)}) copy-start(f32[2048]{0:T(1024)} %param.27) | copy-start | bytes 24580
  19.6 9.5 %collective-permute-start.3 = (bf16[64,2048]{1,0:T(8,128)(2,1)}, bf16[64,2048]{1,0:T(8,128)(2,1)S(1)}, u32[]{:S(2)}, u32[]{:S(2)}) collective-permute-start(bf16[64,2048]{1,0:T(8,128)(2,1)} %get-tuple-element.41), channel_id=1, source_target_pairs={{0,4},{4,0},{8,12},{12,8},{16,20},{20,16},{24,28},{28,24},{1,5},{5... | collective-permute-start | bytes 786440 | tf_op jit(solution)/shard_map/ppermute | solution.py:294
  21.2 90.3 %collective-permute-start.10 = (bf16[2048,512]{1,0:T(8,128)(2,1)S(1)}, bf16[2048,512]{1,0:T(8,128)(2,1)}, u32[]{:S(2)}, u32[]{:S(2)}) collective-permute-start(bf16[2048,512]{1,0:T(8,128)(2,1)S(1)} %bitcast.11), channel_id=1, source_target_pairs={{0,1},{1,0},{2,3},{3,2},{4,5},{5,4},{6,7},{7,6},{8,9},{9,8},{10,11... | collective-permute-start | bytes 6291464 | tf_op jit(solution)/shard_map/ppermute | solution.py:285
  21.2 13.5 %collective-permute-start.2 = (bf16[64,2048]{1,0:T(8,128)(2,1)}, bf16[64,2048]{1,0:T(8,128)(2,1)S(1)}, u32[]{:S(2)}, u32[]{:S(2)}) collective-permute-start(bf16[64,2048]{1,0:T(8,128)(2,1)} %get-tuple-element.39), channel_id=1, source_target_pairs={{0,4},{4,0},{8,12},{12,8},{16,20},{20,16},{24,28},{28,24},{1,5},{5... | collective-permute-start | bytes 786440 | tf_op jit(solution)/shard_map/ppermute | solution.py:294
  21.7 18.6 %collective-permute-start.1 = (bf16[64,2048]{1,0:T(8,128)(2,1)}, bf16[64,2048]{1,0:T(8,128)(2,1)S(1)}, u32[]{:S(2)}, u32[]{:S(2)}) collective-permute-start(bf16[64,2048]{1,0:T(8,128)(2,1)} %get-tuple-element.37), channel_id=1, source_target_pairs={{0,4},{4,0},{8,12},{12,8},{16,20},{20,16},{24,28},{28,24},{1,5},{5... | collective-permute-start | bytes 786440 | tf_op jit(solution)/shard_map/ppermute | solution.py:294
  29.0 25.6 %collective-permute-start = (bf16[64,2048]{1,0:T(8,128)(2,1)}, bf16[64,2048]{1,0:T(8,128)(2,1)}, u32[]{:S(2)}, u32[]{:S(2)}) collective-permute-start(bf16[64,2048]{1,0:T(8,128)(2,1)} %get-tuple-element.35), channel_id=1, source_target_pairs={{0,4},{4,0},{8,12},{12,8},{16,20},{20,16},{24,28},{28,24},{1,5},{5... | collective-permute-start | bytes 786440 | tf_op jit(solution)/shard_map/ppermute | solution.py:294
  34.6 37.4 %collective-permute-start.13 = (bf16[256,2048]{1,0:T(8,128)(2,1)S(1)}, bf16[256,2048]{1,0:T(8,128)(2,1)}, u32[]{:S(2)}, u32[]{:S(2)}) collective-permute-start(bf16[256,2048]{1,0:T(8,128)(2,1)S(1)} %bitcast.15), channel_id=1, source_target_pairs={{0,2},{1,3},{2,0},{3,1},{4,6},{5,7},{6,4},{7,5},{8,10},{9,11},{10,... | collective-permute-start | bytes 3145736 | tf_op jit(solution)/shard_map/ppermute | solution.py:279
  50.5 67.4 %collective-permute-start.14 = (bf16[2048,512]{1,0:T(8,128)(2,1)}, bf16[2048,512]{1,0:T(8,128)(2,1)}, u32[]{:S(2)}, u32[]{:S(2)}) collective-permute-start(bf16[2048,512]{1,0:T(8,128)(2,1)} %collective-permute-done.11.refs_1_), channel_id=1, source_target_pairs={{0,1},{1,0},{2,3},{3,2},{4,5},{5,4},{6,7},{7,6},{8,9},{9,8},{10,11... | collective-permute-start | bytes 6291464 | tf_op jit(solution)/shard_map/ppermute | solution.py:285
  52.2 9.3 %collective-permute-start.6 = (bf16[64,2048]{1,0:T(8,128)(2,1)}, bf16[64,2048]{1,0:T(8,128)(2,1)S(1)}, u32[]{:S(2)}, u32[]{:S(2)}) collective-permute-start(bf16[64,2048]{1,0:T(8,128)(2,1)} %add_convert_fusion.4), channel_id=1, source_target_pairs={{8,0},{12,4},{0,8},{4,12},{24,16},{28,20},{16,24},{20,28},{9,1},{1... | collective-permute-start | bytes 786440 | tf_op jit(solution)/shard_map/ppermute | solution.py:307
  54.6 14.9 %collective-permute-start.5 = (bf16[64,2048]{1,0:T(8,128)(2,1)}, bf16[64,2048]{1,0:T(8,128)(2,1)S(1)}, u32[]{:S(2)}, u32[]{:S(2)}) collective-permute-start(bf16[64,2048]{1,0:T(8,128)(2,1)} %add_convert_fusion.5), channel_id=1, source_target_pairs={{24,0},{28,4},{16,8},{20,12},{8,16},{12,20},{0,24},{4,28},{25,1},{... | collective-permute-start | bytes 786440 | tf_op jit(solution)/shard_map/ppermute | solution.py:307
  61.5 22.4 %copy-start.4 = (bf16[64,2048]{1,0:T(8,128)(2,1)}, bf16[64,2048]{1,0:T(8,128)(2,1)S(1)}, u32[]{:S(2)}) copy-start(bf16[64,2048]{1,0:T(8,128)(2,1)S(1)} %collective-permute-done.6.refs_2_) | copy-start | bytes 786436
  61.5 39.5 %collective-permute-start.12 = (bf16[256,2048]{1,0:T(8,128)(2,1)S(1)}, bf16[256,2048]{1,0:T(8,128)(2,1)S(1)}, u32[]{:S(2)}, u32[]{:S(2)}) collective-permute-start(bf16[256,2048]{1,0:T(8,128)(2,1)S(1)} %bitcast.16), channel_id=1, source_target_pairs={{0,1},{1,0},{2,3},{3,2},{4,5},{5,4},{6,7},{7,6},{8,9},{9,8},{10,11... | collective-permute-start | bytes 3145736 | tf_op jit(solution)/shard_map/ppermute | solution.py:285
  69.5 14.4 %collective-permute-start.4 = (bf16[64,2048]{1,0:T(8,128)(2,1)}, bf16[64,2048]{1,0:T(8,128)(2,1)S(1)}, u32[]{:S(2)}, u32[]{:S(2)}) collective-permute-start(bf16[64,2048]{1,0:T(8,128)(2,1)} %add_convert_fusion.6), channel_id=1, source_target_pairs={{16,0},{20,4},{24,8},{28,12},{0,16},{4,20},{8,24},{12,28},{17,1},{... | collective-permute-start | bytes 786440 | tf_op jit(solution)/shard_map/ppermute | solution.py:307
  72.1 44.0 %collective-permute-start.15 = (bf16[256,2048]{1,0:T(8,128)(2,1)}, bf16[256,2048]{1,0:T(8,128)(2,1)}, u32[]{:S(2)}, u32[]{:S(2)}) collective-permute-start(bf16[256,2048]{1,0:T(8,128)(2,1)} %collective-permute-done.13.refs_3_), channel_id=1, source_target_pairs={{0,1},{1,0},{2,3},{3,2},{4,5},{5,4},{6,7},{7,6},{8,9},{9,8},{10,11... | collective-permute-start | bytes 3145736 | tf_op jit(solution)/shard_map/ppermute | solution.py:285
  83.9 1.0 copy-start.5
  85.7 15.3 %collective-permute-start.18 = (bf16[64,2176]{1,0:T(8,128)(2,1)S(1)}, bf16[64,2176]{1,0:T(8,128)(2,1)}, u32[]{:S(2)}, u32[]{:S(2)}) collective-permute-start(bf16[64,2176]{1,0:T(8,128)(2,1)S(1)} %get-tuple-element.45.refs_0_), channel_id=1, source_target_pairs={{0,16},{4,20},{8,24},{12,28},{16,0},{20,4},{24,8},{28,12},{1,17},{... | collective-permute-start | bytes 835592 | tf_op jit(solution)/shard_map/ppermute | solution.py:279
  101.0 8.9 %collective-permute-start.19 = (bf16[64,2176]{1,0:T(8,128)(2,1)}, bf16[64,2176]{1,0:T(8,128)(2,1)}, u32[]{:S(2)}, u32[]{:S(2)}) collective-permute-start(bf16[64,2176]{1,0:T(8,128)(2,1)} %collective-permute-done.18.refs_0_), channel_id=1, source_target_pairs={{0,8},{4,12},{8,0},{12,4},{16,24},{20,28},{24,16},{28,20},{1,9},{5... | collective-permute-start | bytes 835592 | tf_op jit(solution)/shard_map/ppermute | solution.py:279
  101.0 1.0 copy-start.2
  102.0 13.8 %collective-permute-start.7 = (bf16[64,2176]{1,0:T(8,128)(2,1)S(1)}, bf16[64,2176]{1,0:T(8,128)(2,1)}, u32[]{:S(2)}, u32[]{:S(2)}) collective-permute-start(bf16[64,2176]{1,0:T(8,128)(2,1)S(1)} %get-tuple-element.45.refs_0_), channel_id=1, source_target_pairs={{0,4},{4,0},{8,12},{12,8},{16,20},{20,16},{24,28},{28,24},{1,5},{5... | collective-permute-start | bytes 835592 | tf_op jit(solution)/shard_map/ppermute | solution.py:285
  109.9 9.9 %collective-permute-start.22 = (bf16[64,2176]{1,0:T(8,128)(2,1)}, bf16[64,2176]{1,0:T(8,128)(2,1)}, u32[]{:S(2)}, u32[]{:S(2)}) collective-permute-start(bf16[64,2176]{1,0:T(8,128)(2,1)} %collective-permute-done.18.refs_0_), channel_id=1, source_target_pairs={{0,4},{4,0},{8,12},{12,8},{16,20},{20,16},{24,28},{28,24},{1,5},{5... | collective-permute-start | bytes 835592 | tf_op jit(solution)/shard_map/ppermute | solution.py:285
  111.4 12.9 %collective-permute-start.20 = (bf16[64,2176]{1,0:T(8,128)(2,1)}, bf16[64,2176]{1,0:T(8,128)(2,1)}, u32[]{:S(2)}, u32[]{:S(2)}) collective-permute-start(bf16[64,2176]{1,0:T(8,128)(2,1)} %collective-permute-done.19.refs_0_), channel_id=1, source_target_pairs={{0,4},{4,0},{8,12},{12,8},{16,20},{20,16},{24,28},{28,24},{1,5},{5... | collective-permute-start | bytes 835592 | tf_op jit(solution)/shard_map/ppermute | solution.py:285
  112.0 1.2 copy-start.3
  115.8 13.0 %collective-permute-start.8 = (bf16[64,2176]{1,0:T(8,128)(2,1)S(1)}, bf16[64,2176]{1,0:T(8,128)(2,1)S(1)}, u32[]{:S(2)}, u32[]{:S(2)}) collective-permute-start(bf16[64,2176]{1,0:T(8,128)(2,1)S(1)} %get-tuple-element.45.refs_0_), channel_id=1, source_target_pairs={{0,8},{4,12},{8,0},{12,4},{16,24},{20,28},{24,16},{28,20},{1,9},{5... | collective-permute-start | bytes 835592 | tf_op jit(solution)/shard_map/ppermute | solution.py:279
  116.1 12.9 %collective-permute-start.9 = (bf16[64,2176]{1,0:T(8,128)(2,1)}, bf16[64,2176]{1,0:T(8,128)(2,1)S(1)}, u32[]{:S(2)}, u32[]{:S(2)}) collective-permute-start(bf16[64,2176]{1,0:T(8,128)(2,1)} %collective-permute-done.7.refs_1_), channel_id=1, source_target_pairs={{0,8},{4,12},{8,0},{12,4},{16,24},{20,28},{24,16},{28,20},{1,9},{5... | collective-permute-start | bytes 835592 | tf_op jit(solution)/shard_map/ppermute | solution.py:283
  122.7 12.8 %collective-permute-start.23 = (bf16[64,2048]{1,0:T(8,128)(2,1)S(1)}, bf16[64,2048]{1,0:T(8,128)(2,1)S(1)}, u32[]{:S(2)}, u32[]{:S(2)}) collective-permute-start(bf16[64,2048]{1,0:T(8,128)(2,1)S(1)} %get-tuple-element.59), channel_id=1, source_target_pairs={{0,4},{4,0},{8,12},{12,8},{16,20},{20,16},{24,28},{28,24},{1,5},{5... | collective-permute-start | bytes 786440 | tf_op jit(solution)/shard_map/ppermute | solution.py:294
  127.2 9.0 %collective-permute-start.21 = (bf16[64,2048]{1,0:T(8,128)(2,1)S(1)}, bf16[64,2048]{1,0:T(8,128)(2,1)S(1)}, u32[]{:S(2)}, u32[]{:S(2)}) collective-permute-start(bf16[64,2048]{1,0:T(8,128)(2,1)S(1)} %get-tuple-element.57), channel_id=1, source_target_pairs={{0,4},{4,0},{8,12},{12,8},{16,20},{20,16},{24,28},{28,24},{1,5},{5... | collective-permute-start | bytes 786440 | tf_op jit(solution)/shard_map/ppermute | solution.py:294
  133.4 9.2 %collective-permute-start.17 = (bf16[64,2048]{1,0:T(8,128)(2,1)S(1)}, bf16[64,2048]{1,0:T(8,128)(2,1)S(1)}, u32[]{:S(2)}, u32[]{:S(2)}) collective-permute-start(bf16[64,2048]{1,0:T(8,128)(2,1)S(1)} %get-tuple-element.55), channel_id=1, source_target_pairs={{0,4},{4,0},{8,12},{12,8},{16,20},{20,16},{24,28},{28,24},{1,5},{5... | collective-permute-start | bytes 786440 | tf_op jit(solution)/shard_map/ppermute | solution.py:294
  135.0 11.3 %collective-permute-start.16 = (bf16[64,2048]{1,0:T(8,128)(2,1)S(1)}, bf16[64,2048]{1,0:T(8,128)(2,1)S(1)}, u32[]{:S(2)}, u32[]{:S(2)}) collective-permute-start(bf16[64,2048]{1,0:T(8,128)(2,1)S(1)} %get-tuple-element.53), channel_id=1, source_target_pairs={{0,4},{4,0},{8,12},{12,8},{16,20},{20,16},{24,28},{28,24},{1,5},{5... | collective-permute-start | bytes 786440 | tf_op jit(solution)/shard_map/ppermute | solution.py:294
  142.7 7.5 %collective-permute-start.26 = (bf16[64,2048]{1,0:T(8,128)(2,1)S(1)}, bf16[64,2048]{1,0:T(8,128)(2,1)S(1)}, u32[]{:S(2)}, u32[]{:S(2)}) collective-permute-start(bf16[64,2048]{1,0:T(8,128)(2,1)S(1)} %add_convert_fusion.1), channel_id=1, source_target_pairs={{8,0},{12,4},{0,8},{4,12},{24,16},{28,20},{16,24},{20,28},{9,1},{1... | collective-permute-start | bytes 786440 | tf_op jit(solution)/shard_map/ppermute | solution.py:307
  143.3 12.3 %collective-permute-start.25 = (bf16[64,2048]{1,0:T(8,128)(2,1)S(1)}, bf16[64,2048]{1,0:T(8,128)(2,1)S(1)}, u32[]{:S(2)}, u32[]{:S(2)}) collective-permute-start(bf16[64,2048]{1,0:T(8,128)(2,1)S(1)} %add_convert_fusion.2), channel_id=1, source_target_pairs={{24,0},{28,4},{16,8},{20,12},{8,16},{12,20},{0,24},{4,28},{25,1},{... | collective-permute-start | bytes 786440 | tf_op jit(solution)/shard_map/ppermute | solution.py:307
  144.8 20.3 %collective-permute-start.24 = (bf16[64,2048]{1,0:T(8,128)(2,1)S(1)}, bf16[64,2048]{1,0:T(8,128)(2,1)S(1)}, u32[]{:S(2)}, u32[]{:S(2)}) collective-permute-start(bf16[64,2048]{1,0:T(8,128)(2,1)S(1)} %add_convert_fusion.3), channel_id=1, source_target_pairs={{16,0},{20,4},{24,8},{28,12},{0,16},{4,20},{8,24},{12,28},{17,1},{... | collective-permute-start | bytes 786440 | tf_op jit(solution)/shard_map/ppermute | solution.py:307
